TPU v7x, 32 devices: a whole 2x2x4 slice. The times are simulated.
32 devices in a mesh: group: 1, path: 32 (over z, y, x, core).
Axes of the slice: x: 2, y: 2, z: 4, core: 2. Of those that a mesh axis runs over, the one named last changes fastest.
Arguments:
- normals: float32 [8, 32, 8192], P(None, None, ('group', 'path')), may hold values from -6 to 6
- start_state: float32 [32, 8192], P(None, ('group', 'path')), may hold values from -0.12 to 0.12
- later_adjoint: float32 [32, 8192], P(None, ('group', 'path')), may hold values from -1.8 to 1.8
- vol: float32 [8], replicated, may hold values from 0.004 to 0.016
- factor_load: float32 [32, 960], replicated, may hold values from -2.1 to 2.1
- knots: float32 [960], replicated, may hold values from 0.01 to 0.05
- spline_jac: float32 [960, 960], replicated
- cashflows: bfloat16 [256, 960], P(('group', 'path')), may hold values from -0.1875 to 0.1875
- trade_set: int32 [256, 1], P(('group', 'path')), may hold values from 0 to 127
- trade_end: int32 [256], P(('group', 'path')), may hold values from 240 to 960
- set_cpty: int32 [128, 1], P('group'), may hold values from 0 to 63
- default_prob: float32 [8, 64], replicated, may hold values from 0.01 to 0.1
- base_value: float32 [8, 128], P(None, 'group'), may hold values from -3 to 3
Outputs:
- knot_grad: float32 [960], P('group')
- alloc: float32 [256], P(('group', 'path'))
- start_adjoint: float32 [32, 8192], P(None, ('group', 'path'))
All inputs are finite; a program needn't handle non-finite values.
Results may differ from a plain program's by a relative error of at most 0.0011.
Values may be sent and summed in bfloat16 or wider, within the bound.
No kernel may reach another device: no remote copies, remote signals or barrier semaphores. Data moves between devices by JAX's collectives and lax.ppermute only.
A program may use at most 64 MiB of HBM per device.

v0:
```python
import math

import jax
import jax.numpy as jnp
from jax import lax
from jax.sharding import PartitionSpec as P

MEAN_REV = 0.05
STEP_YEARS = 0.25
HORIZON_YEARS = 30.0
SHARPNESS = 4.0
LOSS_RATE = 0.6


def curve_terms(knots, spline_jac, date_count, knot_count):
    zero_rate = jnp.dot(spline_jac, knots, precision=lax.Precision.HIGHEST)
    knot_index = jnp.arange(knot_count, dtype=jnp.int32)
    date_index = jnp.arange(date_count, dtype=jnp.int32)
    is_alive = 120 * (knot_index[None, :] + 1) > knot_count * (date_index[:, None] + 1)
    maturity = HORIZON_YEARS * (knot_index + 1).astype(jnp.float32) / knot_count
    fixing = STEP_YEARS * (date_index + 1).astype(jnp.float32)
    horizon = jnp.where(is_alive, maturity[None, :] - fixing[:, None], jnp.float32(0.0))
    loading = (1.0 - jnp.exp(-MEAN_REV * horizon)) / MEAN_REV
    discount = jnp.where(is_alive, jnp.exp(-zero_rate[None, :] * horizon), jnp.float32(0.0))
    return (horizon, loading, discount)


def state_path(start_state, vol, normals):
    decay_factor = math.exp(-MEAN_REV * STEP_YEARS)
    state = start_state
    collected = []
    for index in range(normals.shape[0]):
        state = decay_factor * state + vol[index] * normals[index]
        collected.append(state)
    return jnp.stack(collected)


def per_device(
    normals,
    start_state,
    later_adjoint,
    vol,
    factor_load,
    knots,
    spline_jac,
    cashflows,
    trade_set,
    trade_end,
    set_cpty,
    default_prob,
    base_value,
):
    highest = lax.Precision.HIGHEST
    date_count = normals.shape[0]
    knot_count = knots.shape[0]
    set_count = base_value.shape[1]
    paths_all = normals.shape[2] * lax.axis_size("path")
    horizon, loading, discount = curve_terms(knots, spline_jac, date_count, knot_count)
    knot_index = jnp.arange(knot_count, dtype=jnp.int32)
    live_flows = jnp.where(
        knot_index[None, :] < trade_end[:, None], cashflows, jnp.zeros_like(cashflows)
    )
    set_ids = trade_set[:, 0]
    labels = jnp.arange(set_count, dtype=jnp.int32)
    all_flows, all_sets = (
        lax.all_gather(live_flows, "path", axis=0, tiled=True),
        lax.all_gather(set_ids, "path", axis=0, tiled=True),
    )
    member = (labels[:, None] == all_sets[None, :]).astype(jnp.bfloat16)
    net_flows = jnp.dot(member, all_flows, preferred_element_type=jnp.float32).astype(jnp.bfloat16)
    counter = (
        jnp.arange(default_prob.shape[1], dtype=jnp.int32)[:, None] == set_cpty[:, 0][None, :]
    ).astype(jnp.float32)
    weight = LOSS_RATE * jnp.dot(default_prob, counter, precision=highest)
    states = state_path(start_state, vol, normals)
    shift = jnp.einsum("fm,ifp->imp", factor_load, states, precision=highest)
    bond_term = jnp.exp(-loading[:, :, None] * shift)
    feat_exact = discount[:, :, None] * bond_term
    features = feat_exact.astype(jnp.bfloat16)
    values = jnp.einsum("nm,imp->inp", net_flows, features, preferred_element_type=jnp.float32)
    mean_value = lax.psum(jnp.sum(values, axis=2), "path") / paths_all
    shifted = values - mean_value[:, :, None] + base_value[:, :, None]
    slope = weight[:, :, None] * jax.nn.sigmoid(SHARPNESS * shifted)
    mean_slope = lax.psum(jnp.sum(slope, axis=2), "path") / paths_all
    set_adjoint = (slope - mean_slope[:, :, None]).astype(jnp.bfloat16)
    feat_adjoint = jnp.einsum(
        "nm,inp->imp", net_flows, set_adjoint, preferred_element_type=jnp.float32
    )
    state_local = -jnp.einsum(
        "fm,imp->ifp",
        factor_load,
        feat_adjoint * feat_exact * loading[:, :, None],
        precision=highest,
    )
    discount_grad = jnp.sum(feat_adjoint * bond_term, axis=2)
    rate_adjoint = -jnp.sum(discount_grad * discount * horizon, axis=0) / paths_all
    rate_total = lax.psum(rate_adjoint, "path")
    knot_grad = jnp.dot(spline_jac.T, rate_total, precision=highest)
    load_sums = (
        jnp.einsum("inp,imp->nm", set_adjoint, features, preferred_element_type=jnp.float32)
        / paths_all
    )
    set_rows = load_sums[all_sets]
    trade_part = jnp.sum(all_flows.astype(jnp.float32) * set_rows, axis=1)
    alloc = lax.psum_scatter(trade_part, "path", scatter_dimension=0, tiled=True)
    decay_factor = math.exp(-MEAN_REV * STEP_YEARS)
    carried = later_adjoint + state_local[date_count - 1]
    for index in reversed(range(date_count - 1)):
        carried = state_local[index] + decay_factor * carried
    start_adjoint = decay_factor * carried
    return (knot_grad, alloc, start_adjoint)


def solution(mesh):
    in_specs = (
        P(None, None, ("group", "path")),
        P(None, ("group", "path")),
        P(None, ("group", "path")),
        P(),
        P(),
        P(),
        P(),
        P(("group", "path"), None),
        P(("group", "path"), None),
        P(("group", "path")),
        P("group", None),
        P(),
        P(None, "group"),
    )
    out_specs = (P("group"), P(("group", "path")), P(None, ("group", "path")))
    return jax.shard_map(
        per_device, mesh=mesh, in_specs=in_specs, out_specs=out_specs, check_vma=False
    )
```

profile of v0, /device:TPU:0, one launch (start us, length us, event | category | flops | bytes accessed | tf_op | source)
XLA Modules:
  0.0 270.6 jit_solution(15762425865365894682)
XLA Ops:
  1.5 41.9 %all-reduce = s32[256]{0:T(256)S(1)} all-reduce(s32[256]{0:T(256)S(1)} %bitcast_dynamic-update-slice_fusion.8), channel_id=2, replica_groups=mesh['group'=1,'path'=32] {'path'}, use_global_device_ids=true, to_apply=%add | all-reduce | flops 256 | bytes 2048 | tf_op jit(solution)/shard_map/all_gather | solution.py:67
  44.0 0.8 fusion.18
  44.9 5.4 %fusion.50 = f32[1,960]{1,0:T(1,128)S(1)} fusion(f32[960,960]{1,0:T(8,128)} %param.19, f32[960,1]{0,1:T(1,128)} %bitcast.192), kind=kOutput, calls=%fused_computation.96 | convolution fusion | flops 11059200 | bytes 3694080 | tf_op jit(solution)/shard_map/dot_general | solution.py:16
  50.3 1.6 fusion.48
  53.5 1.5 bitcast_dynamic-update-slice_fusion.7
  54.9 2.0 bitcast_dynamic-update-slice_fusion.6
  57.0 1.5 bitcast_dynamic-update-slice_fusion.5
  58.4 2.0 bitcast_dynamic-update-slice_fusion.4
  60.5 1.5 bitcast_dynamic-update-slice_fusion.3
  61.9 2.1 bitcast_dynamic-update-slice_fusion.2
  64.1 1.4 bitcast_dynamic-update-slice_fusion.1
  65.4 2.1 bitcast_dynamic-update-slice_fusion
  67.5 41.7 %all_gather.7 = bf16[256,960]{1,0:T(8,128)(2,1)S(1)} all-gather(bf16[8,960]{1,0:T(8,128)(2,1)S(1)} %fusion.42), channel_id=1, replica_groups=mesh['group'=1,'path'=32] {'path'}, dimensions={0}, use_global_device_ids=true | all-gather | bytes 506880 | tf_op jit(solution)/shard_map/all_gather | solution.py:66
  109.6 6.5 %fusion.23 = f32[8,256,960]{1,2,0:T(8,128)S(1)} fusion(f32[8,32,256]{2,1,0:T(8,128)S(1)} %bitcast_dynamic-update-slice_fusion, f32[32,960]{1,0:T(8,128)S(1)} %copy-done), kind=kOutput, calls=%fused_computation.28 | convolution fusion | flops 754974720 | bytes 8249344 | tf_op jit(solution)/shard_map/fm,ifp->imp/dot_general | solution.py:76
  116.1 3.1 %copy-done.1 = f32[8,256,960]{1,2,0:T(8,128)} copy-done((f32[8,256,960]{1,2,0:T(8,128)}, f32[8,256,960]{1,2,0:T(8,128)S(1)}, u32[]{:S(2)}) %copy-start.1) | copy-done | bytes 7864344
  119.1 5.4 %fusion.49 = (f32[8,128]{1,0:T(8,128)S(1)}, f32[8,128,256]{1,2,0:T(8,128)S(1)}) fusion(bf16[128,960,1]{0,1,2:T(8,128)(2,1)S(1)} %fusion.17, f32[8,256,960]{1,2,0:T(8,128)S(1)} %fusion.23, f32[8,960]{1,0:T(8,128)S(1)} %get-tuple-element.12, f32[8,960]{1,0:T(8,128)S(1)} %get-tuple-element.13), kind=kOutput, calls=%fused_computation.95 | convolution fusion | flops 509475840 | bytes 9224192 | tf_op jit(solution)/shard_map/nm,imp->inp/dot_general | solution.py:80
  124.6 37.0 %psum.21 = f32[8,128]{1,0:T(8,128)S(1)} all-reduce(f32[8,128]{1,0:T(8,128)S(1)} %get-tuple-element.22), channel_id=1, replica_groups=mesh['group'=1,'path'=32] {'path'}, use_global_device_ids=true, to_apply=%region_1.2 | all-reduce | flops 1024 | bytes 8192 | tf_op jit(solution)/shard_map/psum | solution.py:81
  162.0 41.2 %psum.22 = f32[8,128]{1,0:T(8,128)S(1)} all-reduce(f32[8,128]{1,0:T(8,128)S(1)} %fusion.47), channel_id=1, replica_groups=mesh['group'=1,'path'=32] {'path'}, use_global_device_ids=true, to_apply=%region_3.4 | all-reduce | flops 1024 | bytes 8192 | tf_op jit(solution)/shard_map/psum | solution.py:84
  203.8 5.4 %fusion.10 = f32[128,960]{0,1:T(8,128)S(1)} fusion(f32[8,256,960]{1,2,0:T(8,128)} %copy-done.1, f32[8,960]{1,0:T(8,128)S(1)} %get-tuple-element.12, f32[8,960]{1,0:T(8,128)S(1)} %get-tuple-element.13, f32[8,128]{1,0:T(8,128)S(1)} %broadcast_multiply_fusion, f32[8,128,256]{1,2,0:T(8,128)S(1)} %get-tuple-element.23, f32[8,128]{1,0:T(8,128)S(1)} %copy-done.13, ...), kind=kOutput, calls=%fused_computation.16 | convolution fusion | flops 511696896 | bytes 9482240 | tf_op jit(solution)/shard_map/inp,imp->nm/dot_general | solution.py:100
  209.4 1.2 gather_fusion
  210.8 6.4 %fusion = (f32[8,960]{1,0:T(8,128)S(1)}, f32[8,256,960]{1,2,0:T(8,128)S(1)}) fusion(f32[8,256,960]{1,2,0:T(8,128)} %copy-done.1, f32[8,960]{1,0:T(8,128)S(1)} %get-tuple-element.12, bf16[128,960,1]{0,1,2:T(8,128)(2,1)S(1)} %fusion.17, f32[8,128]{1,0:T(8,128)} %copy-done.15, f32[8,128]{1,0:T(8,128)} %param.25, f32[8,128,256]{1,2,0:T(8,128)S(1)} %get-tuple-element.23, ...), kind=kOutput, calls=%fused_computation.3 | convolution fusion | flops 511566336 | bytes 17100800 | tf_op jit(solution)/shard_map/nm,inp->imp/dot_general | solution.py:86
  217.4 7.6 %fusion.14 = f32[8,32,256]{2,1,0:T(8,128)S(1)} fusion(f32[8,256,960]{1,2,0:T(8,128)S(1)} %get-tuple-element.25, f32[8,256,960]{1,2,0:T(8,128)S(1)} %bitcast.190, f32[8,960]{1,0:T(8,128)S(1)} %copy-done.4, f32[8,960]{1,0:T(8,128)S(1)} %get-tuple-element.12, f32[8,960]{1,0:T(8,128)S(1)} %copy-done.3, f32[32,960]{1,0:T(8,128)S(1)} %copy-done), kind=kOutput, calls=%fused_computation.19 | convolution fusion | flops 762904576 | bytes 16205824 | tf_op jit(solution)/shard_map/fm,imp->ifp/dot_general | solution.py:89
  225.7 39.6 %all-reduce.2 = (f32[960]{0:T(1024)S(1)}, f32[256]{0:T(256)S(1)}) all-reduce(f32[960]{0:T(1024)S(1)} %negate_multiply_fusion, f32[256]{0:T(256)S(1)} %multiply_reduce_fusion), channel_id=1, replica_groups=mesh['group'=1,'path'=32] {'path'}, use_global_device_ids=true, to_apply=%region_6.7 | all-reduce | flops 1216 | bytes 9728 | tf_op jit(solution)/shard_map/psum | solution.py:97
  265.3 4.7 %fusion.5 = f32[1,960]{1,0:T(1,128)} fusion(f32[960,1]{0,1:T(1,128)S(1)} %bitcast.194, f32[960,960]{1,0:T(8,128)} %param.19), kind=kOutput, calls=%fused_computation.9 | convolution fusion | flops 11059200 | bytes 3694080 | tf_op jit(solution)/shard_map/dot_general | solution.py:98
  (65 shorter events, 5.9 us)
Async XLA Ops:
  0.6 108.9 %copy-start = (f32[32,960]{1,0:T(8,128)S(1)}, f32[32,960]{1,0:T(8,128)}, u32[]{:S(2)}) copy-start(f32[32,960]{1,0:T(8,128)} %param.17) | copy-start | bytes 368644
  0.7 123.9 %copy-start.16 = (s32[8]{0:T(128)}, s32[8]{0:T(128)S(1)}, u32[]{:S(2)}) copy-start(s32[8]{0:T(128)S(1)} %fusion.46) | copy-start | bytes 100
  0.7 123.9 %copy-start.18 = (f32[8]{0:T(128)}, f32[8]{0:T(128)S(1)}, u32[]{:S(2)}) copy-start(f32[8]{0:T(128)S(1)} %convert_multiply_fusion.1) | copy-start | bytes 100
  44.8 158.3 %copy-start.14 = (f32[8,128]{1,0:T(8,128)}, f32[8,128]{1,0:T(8,128)S(1)}, u32[]{:S(2)}) copy-start(f32[8,128]{1,0:T(8,128)S(1)} %fusion.18) | copy-start | bytes 12292
  44.8 79.7 %copy-start.5 = (s32[960]{0:T(1024)}, s32[960]{0:T(1024)S(1)}, u32[]{:S(2)}) copy-start(s32[960]{0:T(1024)S(1)} %fusion.44) | copy-start | bytes 11524
  44.9 79.7 %copy-start.7 = (f32[960]{0:T(1024)}, f32[960]{0:T(1024)S(1)}, u32[]{:S(2)}) copy-start(f32[960]{0:T(1024)S(1)} %convert_multiply_fusion) | copy-start | bytes 11524
  50.3 74.3 %copy-start.9 = (f32[960]{0:T(1024)}, f32[960]{0:T(1024)S(1)}, u32[]{:S(2)}) copy-start(f32[960]{0:T(1024)S(1)} %neg.24) | copy-start | bytes 11524
  53.5 149.7 %copy-start.2 = (f32[8,960]{1,0:T(8,128)}, f32[8,960]{1,0:T(8,128)S(1)}, u32[]{:S(2)}) copy-start(f32[8,960]{1,0:T(8,128)S(1)} %get-tuple-element.13) | copy-start | bytes 92164
  109.6 52.1 %copy-start.13 = (f32[8,128]{1,0:T(8,128)S(1)}, f32[8,128]{1,0:T(8,128)}, u32[]{:S(2)}) copy-start(f32[8,128]{1,0:T(8,128)} %param.25) | copy-start | bytes 12292
  116.1 3.1 %copy-start.1 = (f32[8,256,960]{1,2,0:T(8,128)}, f32[8,256,960]{1,2,0:T(8,128)S(1)}, u32[]{:S(2)}) copy-start(f32[8,256,960]{1,2,0:T(8,128)S(1)} %fusion.23) | copy-start | bytes 23592964
  161.6 41.5 %copy-start.11 = (f32[8,128]{1,0:T(8,128)}, f32[8,128]{1,0:T(8,128)S(1)}, u32[]{:S(2)}) copy-start(f32[8,128]{1,0:T(8,128)S(1)} %broadcast_multiply_fusion.1) | copy-start | bytes 12292
  203.2 0.6 copy-start.15
  210.6 6.7 %slice-start = ((s8[7864320]{0:T(1024)(128)(4,1)}), s8[4194304]{0:T(1024)(128)(4,1)S(1)}, s32[]{:S(2)}) async-start(s8[7864320]{0:T(1024)(128)(4,1)} %bitcast.189), calls=%async_computation | async-start | bytes 8388608
  210.8 6.5 %slice-start.1 = ((s8[7864320]{0:T(1024)(128)(4,1)}), s8[3670016]{0:T(1024)(128)(4,1)S(1)}, s32[]{:S(2)}) async-start(s8[7864320]{0:T(1024)(128)(4,1)} %bitcast.189), calls=%async_computation.1 | async-start | bytes 7340032
  210.8 6.5 %copy-start.3 = (f32[8,960]{1,0:T(8,128)S(1)}, f32[8,960]{1,0:T(8,128)}, u32[]{:S(2)}) copy-start(f32[8,960]{1,0:T(8,128)} %copy-done.2) | copy-start | bytes 92164
  210.8 6.5 %copy-start.4 = (f32[8,960]{1,0:T(8,128)S(1)}, f32[8,960]{1,0:T(8,128)}, u32[]{:S(2)}) copy-start(f32[8,960]{1,0:T(8,128)} %get-tuple-element.11) | copy-start | bytes 92164
  217.3 7.6 %copy-start.12 = (f32[32,256]{1,0:T(8,128)S(1)}, f32[32,256]{1,0:T(8,128)}, u32[]{:S(2)}) copy-start(f32[32,256]{1,0:T(8,128)} %param.15) | copy-start | bytes 98308
  217.3 8.3 %copy-start.6 = (s32[960]{0:T(1024)S(1)}, s32[960]{0:T(1024)}, u32[]{:S(2)}) copy-start(s32[960]{0:T(1024)} %copy-done.5) | copy-start | bytes 11524
  217.3 8.3 %copy-start.8 = (f32[960]{0:T(1024)S(1)}, f32[960]{0:T(1024)}, u32[]{:S(2)}) copy-start(f32[960]{0:T(1024)} %copy-done.7) | copy-start | bytes 11524
  217.3 8.3 %copy-start.10 = (f32[960]{0:T(1024)S(1)}, f32[960]{0:T(1024)}, u32[]{:S(2)}) copy-start(f32[960]{0:T(1024)} %copy-done.9) | copy-start | bytes 11524
  217.3 8.3 %copy-start.17 = (s32[8]{0:T(128)S(1)}, s32[8]{0:T(128)}, u32[]{:S(2)}) copy-start(s32[8]{0:T(128)} %copy-done.16) | copy-start | bytes 100
  217.4 8.3 %copy-start.19 = (f32[8]{0:T(128)S(1)}, f32[8]{0:T(128)}, u32[]{:S(2)}) copy-start(f32[8]{0:T(128)} %copy-done.18) | copy-start | bytes 100
where the time goes:
time: 272 us; the launch traced here: 271 us
  blocking collectives  201 us (74%)
  matrix products  42.6 us (16%)
  other arithmetic  17.4 us (6%)
  local copies, waits for them, and re-layouts  8.13 us (3%)
    all_gather x1, blocking collectives, per_device(): lax.all_gather(set_ids, 'path', axis=0, tiled=True)  41.9 us
    all_gather x1, blocking collectives, per_device(): lax.all_gather(live_flows, 'path', axis=0, tiled=True)  41.7 us
    psum x1, blocking collectives, per_device(): mean_slope = lax.psum(jnp.sum(slope, axis=2), 'path') / paths_all  41.2 us
    psum x1, blocking collectives, per_device(): rate_total = lax.psum(rate_adjoint, 'path')  39.6 us
    psum x1, blocking collectives, per_device(): mean_value = lax.psum(jnp.sum(values, axis=2), 'path') / paths_all  37 us
    unnamed x8, other arithmetic  12 us
    dot_general x1, matrix products, per_device(): jnp.einsum('fm,imp->ifp', factor_load, feat_adjoint * feat_exact * loadin...  7.57 us
    dot_general x1, matrix products, per_device(): shift = jnp.einsum('fm,ifp->imp', factor_load, states, precision=highest)  6.46 us

commit v1 on v0

--- a/solution.py
+++ b/solution.py
@@ -10,6 +10,12 @@
 HORIZON_YEARS = 30.0
 SHARPNESS = 4.0
 LOSS_RATE = 0.6
+BASE = 128
+
+
+def share(block):
+    copies = jnp.broadcast_to(block[None], (lax.axis_size("path"),) + block.shape)
+    return lax.all_to_all(copies, "path", 0, 0)
 
 
 def curve_terms(knots, spline_jac, date_count, knot_count):
@@ -62,10 +68,11 @@
     )
     set_ids = trade_set[:, 0]
     labels = jnp.arange(set_count, dtype=jnp.int32)
-    all_flows, all_sets = (
-        lax.all_gather(live_flows, "path", axis=0, tiled=True),
-        lax.all_gather(set_ids, "path", axis=0, tiled=True),
-    )
+    digits = jnp.stack([set_ids // BASE, set_ids % BASE], axis=1).astype(jnp.bfloat16)
+    gathered = share(jnp.concatenate([live_flows, digits], axis=1)).reshape(-1, knot_count + 2)
+    all_flows = gathered[:, :knot_count]
+    all_digits = gathered[:, knot_count:].astype(jnp.int32)
+    all_sets = all_digits[:, 0] * BASE + all_digits[:, 1]
     member = (labels[:, None] == all_sets[None, :]).astype(jnp.bfloat16)
     net_flows = jnp.dot(member, all_flows, preferred_element_type=jnp.float32).astype(jnp.bfloat16)
     counter = (
@@ -78,10 +85,10 @@
     feat_exact = discount[:, :, None] * bond_term
     features = feat_exact.astype(jnp.bfloat16)
     values = jnp.einsum("nm,imp->inp", net_flows, features, preferred_element_type=jnp.float32)
-    mean_value = lax.psum(jnp.sum(values, axis=2), "path") / paths_all
+    mean_value = jnp.sum(share(jnp.sum(values, axis=2)), axis=0) / paths_all
     shifted = values - mean_value[:, :, None] + base_value[:, :, None]
     slope = weight[:, :, None] * jax.nn.sigmoid(SHARPNESS * shifted)
-    mean_slope = lax.psum(jnp.sum(slope, axis=2), "path") / paths_all
+    mean_slope = jnp.sum(share(jnp.sum(slope, axis=2)), axis=0) / paths_all
     set_adjoint = (slope - mean_slope[:, :, None]).astype(jnp.bfloat16)
     feat_adjoint = jnp.einsum(
         "nm,inp->imp", net_flows, set_adjoint, preferred_element_type=jnp.float32
@@ -94,15 +101,23 @@
     )
     discount_grad = jnp.sum(feat_adjoint * bond_term, axis=2)
     rate_adjoint = -jnp.sum(discount_grad * discount * horizon, axis=0) / paths_all
-    rate_total = lax.psum(rate_adjoint, "path")
-    knot_grad = jnp.dot(spline_jac.T, rate_total, precision=highest)
     load_sums = (
         jnp.einsum("inp,imp->nm", set_adjoint, features, preferred_element_type=jnp.float32)
         / paths_all
     )
-    set_rows = load_sums[all_sets]
-    trade_part = jnp.sum(all_flows.astype(jnp.float32) * set_rows, axis=1)
-    alloc = lax.psum_scatter(trade_part, "path", scatter_dimension=0, tiled=True)
+    spread = jnp.dot(member.T, load_sums, precision=highest)
+    trade_part = jnp.sum(all_flows.astype(jnp.float32) * spread, axis=1)
+    shard_count = lax.axis_size("path")
+    packed = jnp.concatenate(
+        [
+            jnp.broadcast_to(rate_adjoint[None], (shard_count, knot_count)),
+            trade_part.reshape(shard_count, -1),
+        ],
+        axis=1,
+    )
+    summed = jnp.sum(lax.all_to_all(packed[:, None], "path", 0, 0), axis=0)[0]
+    rate_total, alloc = summed[:knot_count], summed[knot_count:]
+    knot_grad = jnp.dot(spline_jac.T, rate_total, precision=highest)
     decay_factor = math.exp(-MEAN_REV * STEP_YEARS)
     carried = later_adjoint + state_local[date_count - 1]
     for index in reversed(range(date_count - 1)):

time: 272 us -> 109 us (0.40)
  blocking collectives: 201 us -> 0 us
  starting transfers between devices: 0 us -> 18.5 us
  waiting for transfers between devices: 0 us -> 16.1 us
  matrix products: 42.6 us -> 49.7 us
    psum x3 -> x0, blocking collectives: 118 us -> none  [the longest x1 41.2 us: per_device(): mean_slope = lax.psum(jnp.sum(slope, axis=2), 'path') / paths_all]
    all_gather x2 -> x0, blocking collectives: 83.6 us -> none  [the longest x1 41.9 us: per_device(): lax.all_gather(set_ids, 'path', axis=0, tiled=True)]
    all_to_all x0 -> x4, starting transfers between devices: none -> 18.5 us  [the longest x3 15.7 us: share(): return lax.all_to_all(copies, 'path', 0, 0)]
    all_to_all x0 -> x4, waiting for transfers between devices: none -> 16.1 us  [the longest x3 16.1 us: share(): return lax.all_to_all(copies, 'path', 0, 0)]
    unnamed x47 -> x11, local copies, waits for them, and re-layouts: 5.08 us -> 0.24 us
    dot_general x1, matrix products: 7.57 us -> 11 us  [per_device(): jnp.einsum('fm,imp->ifp', factor_load, feat_adjoint * feat_exact * loadin...]
    broadcast_in_dim x0 -> x4, local copies, waits for them, and re-layouts: none -> 2.9 us  [the longest x3 2.17 us: share(): jnp.broadcast_to(block[None], (lax.axis_size('path'),) + block.shape)]
    unnamed x8 -> x7, other arithmetic: 12 us -> 11.7 us
  transfers between devices with their start and end apart: 0 -> 4, of which waited for: 0 -> 2; matrix products, arithmetic and copies ran while one was open for 0% -> 38% of each run, Pallas kernels for 0% -> 0%
where the time goes in v1:
time: 109 us; the launch traced here: 108 us
  matrix products  49.7 us (46%)
  starting transfers between devices  18.5 us (17%)
  other arithmetic  17 us (16%)
  waiting for transfers between devices  16.1 us (15%)
  local copies, waits for them, and re-layouts  5.64 us (5%)
    all_to_all x3, waiting for transfers between devices, share(): return lax.all_to_all(copies, 'path', 0, 0)  16.1 us
    all_to_all x3, starting transfers between devices, share(): return lax.all_to_all(copies, 'path', 0, 0)  15.7 us
    unnamed x7, other arithmetic  11.7 us
    dot_general x1, matrix products, per_device(): jnp.einsum('fm,imp->ifp', factor_load, feat_adjoint * feat_exact * loadin...  11 us
    dot_general x1, matrix products, per_device(): shift = jnp.einsum('fm,ifp->imp', factor_load, states, precision=highest)  8.5 us
    dot_general x1, matrix products, per_device(): jnp.einsum('nm,inp->imp', net_flows, set_adjoint, preferred_element_type=...  7.05 us
    dot_general x1, matrix products, per_device(): jnp.einsum('nm,imp->inp', net_flows, features, preferred_element_type=jnp...  6.58 us
    dot_general x1, matrix products, curve_terms(): zero_rate = jnp.dot(spline_jac, knots, precision=lax.Precision.HIGHEST)  5.44 us
  transfers between devices with their start and end apart: 4, of which 2 were waited for; matrix products, arithmetic and copies ran while one was open for 38% of the time, Pallas kernels for 0%

profile of v1, /device:TPU:0, one launch (start us, length us, event | category | flops | bytes accessed | tf_op | source)
XLA Modules:
  0.0 107.8 jit_solution(13556078259256242564)
XLA Ops:
  1.5 0.8 fusion.45
  2.4 0.9 broadcast_in_dim.19
  3.3 7.3 %all-to-all-start = ((bf16[32,8,962]{2,1,0:T(8,128)(2,1)}), bf16[32,8,962]{2,1,0:T(8,128)(2,1)S(1)}, u32[]{:S(2)}, u32[]{:S(2)}) async-start(bf16[32,8,962]{2,1,0:T(8,128)(2,1)} %broadcast_in_dim.19), calls=%async_computation | async-start | bytes 1048576 | tf_op jit(solution)/shard_map/all_to_all | solution.py:18
  10.7 5.4 %fusion.56 = f32[1,960]{1,0:T(1,128)S(1)} fusion(f32[960,960]{1,0:T(8,128)} %param.19, f32[960,1]{0,1:T(1,128)} %bitcast.200), kind=kOutput, calls=%fused_computation.110 | convolution fusion | flops 11059200 | bytes 3694080 | tf_op jit(solution)/shard_map/dot_general | solution.py:22
  16.1 1.6 %fusion.54 = (f32[1]{0:T(128)}, f32[1]{0:T(128)}, f32[1]{0:T(128)}, f32[1]{0:T(128)}, f32[1]{0:T(128)}, /*index=5*/f32[1]{0:T(128)}, f32[1]{0:T(128)}, f32[1]{0:T(128)}) fusion(f32[8]{0:T(128)} %param.16), kind=kLoop, calls=%fused_computation.108 | loop fusion | bytes 64 | tf_op jit(solution)/shard_map/slice | solution.py:39
  17.7 1.4 %bitcast_dynamic-update-slice_fusion.7 = f32[8,32,256]{2,1,0:T(8,128)S(1)} fusion(f32[8,32,256]{2,1,0:T(8,128)} %param.13, f32[]{:T(128)} %bitcast.4, f32[32,256]{1,0:T(8,128)} %param.14), kind=kLoop, calls=%fused_computation.78 | loop fusion | flops 24575 | bytes 98308
  19.2 2.1 %bitcast_dynamic-update-slice_fusion.6 = (f32[8,32,256]{2,1,0:T(8,128)S(1)}, f32[32,256]{1,0:T(8,128)S(1)}) fusion(f32[8,32,256]{2,1,0:T(8,128)S(1)} %bitcast_dynamic-update-slice_fusion.7, f32[8,32,256]{2,1,0:T(8,128)} %param.13, f32[]{:T(128)} %bitcast.7, f32[]{:T(128)} %bitcast.4, f32[32,256]{1,0:T(8,128)} %param.14), kind=kLoop, calls=%fused_computation.76 | loop fusion | flops 49152 | bytes 163848
  21.2 1.3 %bitcast_dynamic-update-slice_fusion.5 = f32[8,32,256]{2,1,0:T(8,128)S(1)} fusion(f32[8,32,256]{2,1,0:T(8,128)S(1)} %get-tuple-element.7, f32[8,32,256]{2,1,0:T(8,128)} %param.13, f32[]{:T(128)} %bitcast.10, f32[32,256]{1,0:T(8,128)S(1)} %get-tuple-element.8), kind=kLoop, calls=%fused_computation.74 | loop fusion | flops 24576 | bytes 98308
  22.6 2.0 %bitcast_dynamic-update-slice_fusion.4 = (f32[8,32,256]{2,1,0:T(8,128)S(1)}, f32[32,256]{1,0:T(8,128)S(1)}) fusion(f32[8,32,256]{2,1,0:T(8,128)S(1)} %bitcast_dynamic-update-slice_fusion.5, f32[8,32,256]{2,1,0:T(8,128)} %param.13, f32[]{:T(128)} %bitcast.13, f32[]{:T(128)} %bitcast.10, f32[32,256]{1,0:T(8,128)S(1)} %get-tuple-element.8), kind=kLoop, calls=%fused_computation.72 | loop fusion | flops 49152 | bytes 163848
  24.6 1.4 %bitcast_dynamic-update-slice_fusion.3 = f32[8,32,256]{2,1,0:T(8,128)S(1)} fusion(f32[8,32,256]{2,1,0:T(8,128)S(1)} %get-tuple-element.5, f32[8,32,256]{2,1,0:T(8,128)} %param.13, f32[]{:T(128)} %bitcast.16, f32[32,256]{1,0:T(8,128)S(1)} %get-tuple-element.6), kind=kLoop, calls=%fused_computation.70 | loop fusion | flops 24576 | bytes 98308
  26.0 2.1 %bitcast_dynamic-update-slice_fusion.2 = (f32[8,32,256]{2,1,0:T(8,128)S(1)}, f32[32,256]{1,0:T(8,128)S(1)}) fusion(f32[8,32,256]{2,1,0:T(8,128)S(1)} %bitcast_dynamic-update-slice_fusion.3, f32[8,32,256]{2,1,0:T(8,128)} %param.13, f32[]{:T(128)} %bitcast.19, f32[]{:T(128)} %bitcast.16, f32[32,256]{1,0:T(8,128)S(1)} %get-tuple-element.6), kind=kLoop, calls=%fused_computation.68 | loop fusion | flops 49152 | bytes 163848
  28.1 1.4 %bitcast_dynamic-update-slice_fusion.1 = f32[8,32,256]{2,1,0:T(8,128)S(1)} fusion(f32[8,32,256]{2,1,0:T(8,128)S(1)} %get-tuple-element.3, f32[8,32,256]{2,1,0:T(8,128)} %param.13, f32[]{:T(128)} %bitcast.22, f32[32,256]{1,0:T(8,128)S(1)} %get-tuple-element.4), kind=kLoop, calls=%fused_computation.66 | loop fusion | flops 24576 | bytes 98308
  29.5 2.0 %bitcast_dynamic-update-slice_fusion = f32[8,32,256]{2,1,0:T(8,128)S(1)} fusion(f32[8,32,256]{2,1,0:T(8,128)S(1)} %bitcast_dynamic-update-slice_fusion.1, f32[8,32,256]{2,1,0:T(8,128)} %param.13, f32[]{:T(128)} %bitcast.25, f32[]{:T(128)} %bitcast.22, f32[32,256]{1,0:T(8,128)S(1)} %get-tuple-element.4), kind=kLoop, calls=%fused_computation.64 | loop fusion | flops 49152 | bytes 131080 | tf_op jit(solution)/shard_map/stack | solution.py:41
  31.6 8.5 %fusion.25 = f32[8,256,960]{1,2,0:T(8,128)} fusion(f32[8,32,256]{2,1,0:T(8,128)S(1)} %bitcast_dynamic-update-slice_fusion, f32[32,960]{1,0:T(8,128)S(1)} %copy-done), kind=kOutput, calls=%fused_computation.32 | convolution fusion | flops 754974720 | bytes 8249344 | tf_op jit(solution)/shard_map/fm,ifp->imp/dot_general | solution.py:83
  40.8 6.6 %fusion.55 = (f32[8,128]{1,0:T(8,128)S(1)}, f32[8,128,256]{1,2,0:T(8,128)S(1)}) fusion(bf16[128,960,1]{0,1,2:T(8,128)(2,1)S(1)} %fusion.18, f32[8,256,960]{1,2,0:T(8,128)} %fusion.25, f32[8,960]{1,0:T(8,128)S(1)} %get-tuple-element.10, f32[8,960]{1,0:T(8,128)S(1)} %get-tuple-element.11), kind=kOutput, calls=%fused_computation.109 | convolution fusion | flops 509475840 | bytes 9224192 | tf_op jit(solution)/shard_map/nm,imp->inp/dot_general | solution.py:87
  48.0 5.8 %all-to-all-start.1 = ((f32[32,8,128]{2,1,0:T(8,128)}), f32[32,8,128]{2,1,0:T(8,128)S(1)}, u32[]{:S(2)}, u32[]{:S(2)}) async-start(f32[32,8,128]{2,1,0:T(8,128)} %broadcast_in_dim.20), calls=%async_computation.1 | async-start | bytes 262144 | tf_op jit(solution)/shard_map/all_to_all | solution.py:18
  54.0 8.1 %all-to-all-done.1 = f32[32,8,128]{2,1,0:T(8,128)S(1)} async-done(((f32[32,8,128]{2,1,0:T(8,128)}), f32[32,8,128]{2,1,0:T(8,128)S(1)}, u32[]{:S(2)}, u32[]{:S(2)}) %all-to-all-start.1) | async-done | bytes 131104 | tf_op jit(solution)/shard_map/all_to_all | solution.py:18
  63.1 2.6 %all-to-all-start.2 = ((f32[32,8,128]{2,1,0:T(8,128)}), f32[32,8,128]{2,1,0:T(8,128)S(1)}, u32[]{:S(2)}, u32[]{:S(2)}) async-start(f32[32,8,128]{2,1,0:T(8,128)} %broadcast_in_dim.21), calls=%async_computation.2 | async-start | bytes 262144 | tf_op jit(solution)/shard_map/all_to_all | solution.py:18
  65.9 8.0 %all-to-all-done.2 = f32[32,8,128]{2,1,0:T(8,128)S(1)} async-done(((f32[32,8,128]{2,1,0:T(8,128)}), f32[32,8,128]{2,1,0:T(8,128)S(1)}, u32[]{:S(2)}, u32[]{:S(2)}) %all-to-all-start.2) | async-done | bytes 131104 | tf_op jit(solution)/shard_map/all_to_all | solution.py:18
  73.9 5.4 %fusion.11 = f32[128,960]{0,1:T(8,128)S(1)} fusion(f32[8,256,960]{1,2,0:T(8,128)} %fusion.25, f32[8,960]{1,0:T(8,128)S(1)} %get-tuple-element.10, f32[8,960]{1,0:T(8,128)S(1)} %get-tuple-element.11, f32[8,128]{1,0:T(8,128)S(1)} %broadcast_multiply_fusion, f32[8,128,256]{1,2,0:T(8,128)S(1)} %get-tuple-element.23, f32[8,128]{1,0:T(8,128)S(1)} %copy-done.2, ...), kind=kOutput, calls=%fused_computation.17 | convolution fusion | flops 511696896 | bytes 9482240 | tf_op jit(solution)/shard_map/inp,imp->nm/dot_general | solution.py:105
  79.3 7.1 %fusion = (f32[8,960]{1,0:T(8,128)S(1)}, f32[8,256,960]{1,2,0:T(8,128)}) fusion(f32[8,256,960]{1,2,0:T(8,128)} %fusion.25, f32[8,960]{1,0:T(8,128)S(1)} %get-tuple-element.10, bf16[128,960,1]{0,1,2:T(8,128)(2,1)S(1)} %fusion.18, f32[8,128]{1,0:T(8,128)S(1)} %broadcast_multiply_fusion, f32[8,128]{1,0:T(8,128)S(1)} %copy-done.2, ...), kind=kOutput, calls=%fused_computation.2 | convolution fusion | flops 511566336 | bytes 17100800 | tf_op jit(solution)/shard_map/nm,inp->imp/dot_general | solution.py:93
  88.0 2.7 %all-to-all-start.3 = ((f32[32,1,968]{2,1,0:T(1,128)}), f32[32,1,968]{2,1,0:T(1,128)S(1)}, u32[]{:S(2)}, u32[]{:S(2)}) async-start(f32[32,1,968]{2,1,0:T(1,128)} %broadcast_in_dim.23), calls=%async_computation.3 | async-start | bytes 262144 | tf_op jit(solution)/shard_map/all_to_all | solution.py:118
  90.7 11.0 %fusion.15 = f32[8,32,256]{2,1,0:T(8,128)S(1)} fusion(f32[8,256,960]{1,2,0:T(8,128)} %get-tuple-element.25, f32[8,256,960]{1,2,0:T(8,128)} %fusion.25, f32[8,960]{1,0:T(8,128)S(1)} %get-tuple-element.9, f32[8,960]{1,0:T(8,128)S(1)} %get-tuple-element.10, f32[8,960]{1,0:T(8,128)S(1)} %get-tuple-element.11, f32[32,960]{1,0:T(8,128)S(1)} %copy-done), kind=kOutput, calls=%fused_computation.20 | convolution fusion | flops 762904576 | bytes 16205824 | tf_op jit(solution)/shard_map/fm,imp->ifp/dot_general | solution.py:96
  103.1 4.7 %fusion.5 = f32[1,960]{1,0:T(1,128)} fusion(f32[960,960]{1,0:T(8,128)} %param.19, f32[1,968]{1,0:T(1,128)S(1)} %bitcast.198), kind=kOutput, calls=%fused_computation.8 | convolution fusion | flops 11059200 | bytes 3694112 | tf_op jit(solution)/shard_map/dot_general | solution.py:120
  (44 shorter events, 6.7 us)
Async XLA Ops:
  0.6 31.0 %copy-start = (f32[32,960]{1,0:T(8,128)S(1)}, f32[32,960]{1,0:T(8,128)}, u32[]{:S(2)}) copy-start(f32[32,960]{1,0:T(8,128)} %param.17) | copy-start | bytes 368644
  3.3 36.9 %all-to-all-start = ((bf16[32,8,962]{2,1,0:T(8,128)(2,1)}), bf16[32,8,962]{2,1,0:T(8,128)(2,1)S(1)}, u32[]{:S(2)}, u32[]{:S(2)}) async-start(bf16[32,8,962]{2,1,0:T(8,128)(2,1)} %broadcast_in_dim.19), calls=%async_computation | async-start | bytes 1048576 | tf_op jit(solution)/shard_map/all_to_all | solution.py:18
  31.6 22.2 %copy-start.3 = (f32[8,64]{1,0:T(8,128)S(1)}, f32[8,64]{1,0:T(8,128)}, u32[]{:S(2)}) copy-start(f32[8,64]{1,0:T(8,128)} %param.24) | copy-start | bytes 6148
  31.6 22.2 %copy-start.4 = (s32[128,1]{0,1:T(1,128)S(1)}, s32[128,1]{0,1:T(1,128)}, u32[]{:S(2)}) copy-start(s32[128,1]{0,1:T(1,128)} %param.23) | copy-start | bytes 1540
  31.6 30.5 %copy-start.2 = (f32[8,128]{1,0:T(8,128)S(1)}, f32[8,128]{1,0:T(8,128)}, u32[]{:S(2)}) copy-start(f32[8,128]{1,0:T(8,128)} %param.25) | copy-start | bytes 12292
  48.0 14.0 %all-to-all-start.1 = ((f32[32,8,128]{2,1,0:T(8,128)}), f32[32,8,128]{2,1,0:T(8,128)S(1)}, u32[]{:S(2)}, u32[]{:S(2)}) async-start(f32[32,8,128]{2,1,0:T(8,128)} %broadcast_in_dim.20), calls=%async_computation.1 | async-start | bytes 262144 | tf_op jit(solution)/shard_map/all_to_all | solution.py:18
  63.1 10.8 %all-to-all-start.2 = ((f32[32,8,128]{2,1,0:T(8,128)}), f32[32,8,128]{2,1,0:T(8,128)S(1)}, u32[]{:S(2)}, u32[]{:S(2)}) async-start(f32[32,8,128]{2,1,0:T(8,128)} %broadcast_in_dim.21), calls=%async_computation.2 | async-start | bytes 262144 | tf_op jit(solution)/shard_map/all_to_all | solution.py:18
  88.0 14.5 %all-to-all-start.3 = ((f32[32,1,968]{2,1,0:T(1,128)}), f32[32,1,968]{2,1,0:T(1,128)S(1)}, u32[]{:S(2)}, u32[]{:S(2)}) async-start(f32[32,1,968]{2,1,0:T(1,128)} %broadcast_in_dim.23), calls=%async_computation.3 | async-start | bytes 262144 | tf_op jit(solution)/shard_map/all_to_all | solution.py:118
  90.7 11.1 %copy-start.1 = (f32[32,256]{1,0:T(8,128)S(1)}, f32[32,256]{1,0:T(8,128)}, u32[]{:S(2)}) copy-start(f32[32,256]{1,0:T(8,128)} %param.15) | copy-start | bytes 98308

commit v2 on v0

v2 whole, which is shorter than its diff:
```python
import functools
import math

import jax
import jax.numpy as jnp
from jax import lax
from jax.experimental import pallas as pl
from jax.experimental.pallas import tpu as pltpu
from jax.sharding import PartitionSpec as P

MEAN_REV = 0.05
STEP_YEARS = 0.25
HORIZON_YEARS = 30.0
SHARPNESS = 4.0
LOSS_RATE = 0.6
BASE = 128
LANES = 128
DECAY = math.exp(-MEAN_REV * STEP_YEARS)
HIGHEST = lax.Precision.HIGHEST
F32 = jnp.float32
BF16 = jnp.bfloat16


def round_up(size, step):
    return -(-size // step) * step


def exchange(copies):
    return lax.all_to_all(copies, "path", 0, 0)


def split(value, terms):
    parts = []
    for _ in range(terms):
        part = value.astype(BF16)
        parts.append(part)
        value = value - part.astype(F32)
    return parts


def contract(lhs, rhs, lhs_dim, rhs_dim, precision=None):
    return lax.dot_general(
        lhs,
        rhs,
        (((lhs_dim,), (rhs_dim,)), ((), ())),
        precision=precision,
        preferred_element_type=F32,
    )


def date_rows(date, knot_count):
    point = lax.broadcasted_iota(jnp.int32, (1, knot_count), 1) + 1
    alive = 120 * point > knot_count * (date + 1)
    maturity = HORIZON_YEARS * point.astype(F32) / knot_count
    fixing = STEP_YEARS * (date + 1).astype(F32)
    horizon = jnp.where(alive, maturity - fixing, 0.0)
    loading = (1.0 - jnp.exp(-MEAN_REV * horizon)) / MEAN_REV
    return alive, horizon, loading


def member_rows(flows, knot_count, set_count):
    digits = flows[:, knot_count : knot_count + 2].astype(F32)
    sets = (digits[:, 0:1] * BASE + digits[:, 1:2]).astype(jnp.int32)
    labels = lax.broadcasted_iota(jnp.int32, (flows.shape[0], set_count), 1)
    return sets == labels


def prep_kernel(end_ref, set_ref, cash_ref, out_ref):
    shards, trades, width = out_ref.shape
    knot_count = cash_ref.shape[1]
    row = lax.broadcasted_iota(jnp.int32, (trades, width), 0)
    point = lax.broadcasted_iota(jnp.int32, (trades, width), 1)
    ends = jnp.zeros((trades, width), jnp.int32)
    sets = jnp.zeros((trades, width), jnp.int32)
    for trade in range(trades):
        ends = jnp.where(row == trade, end_ref[trade], ends)
        sets = jnp.where(row == trade, set_ref[trade, 0], sets)
    cash = jnp.concatenate(
        [cash_ref[...].astype(F32), jnp.zeros((trades, width - knot_count), F32)], axis=1
    )
    high = lax.shift_right_logical(sets, BASE.bit_length() - 1)
    low = sets & (BASE - 1)
    flows = jnp.where(point < jnp.minimum(ends, knot_count), cash, 0.0)
    flows = jnp.where(point == knot_count, high.astype(F32), flows)
    flows = jnp.where(point == knot_count + 1, low.astype(F32), flows).astype(BF16)
    for shard in range(shards):
        out_ref[shard] = flows


def curve_kernel(knots_ref, jac_ref, cpty_ref, prob_ref, rate_ref, weight_ref):
    knot_count = jac_ref.shape[0]
    column = jnp.sum(jac_ref[...] * knots_ref[...], axis=1, keepdims=True)
    rate_ref[...] = jnp.broadcast_to(column, (knot_count, LANES)).T[0:1]
    sets, counterparties = cpty_ref.shape[0], prob_ref.shape[1]
    labels = lax.broadcasted_iota(jnp.int32, (sets, counterparties), 1)
    chosen = (cpty_ref[...] == labels).astype(F32)
    weight_ref[...] = LOSS_RATE * contract(prob_ref[...], chosen, 1, 1, HIGHEST)


def feature_kernel(vol_ref, normals_ref, start_ref, load_ref, rate_ref, exact_ref, feat_ref, state, stacked):
    date = pl.program_id(0)
    knot_count = load_ref.shape[1]

    @pl.when(date == 0)
    def _():
        state[...] = start_ref[...]
        high, middle, low = split(load_ref[...], 3)
        stacked[...] = jnp.concatenate([high, middle, high, middle, low, high], axis=0)

    now = DECAY * state[...] + vol_ref[date] * normals_ref[0]
    state[...] = now
    high, middle, low = split(now, 3)
    terms = jnp.concatenate([high, high, middle, middle, high, low], axis=0)
    alive, horizon, loading = date_rows(date, knot_count)
    discount = jnp.where(alive, jnp.exp(-rate_ref[...] * horizon), 0.0)
    shift = contract(terms, stacked[...], 0, 0)
    exact = discount * jnp.exp(-loading * shift)
    exact_ref[0] = exact
    feat_ref[0] = exact.astype(BF16)


def value_kernel(flows_ref, feat_ref, values_ref, net_ref, out_ref, sums):
    date = pl.program_id(0)
    knot_count = feat_ref.shape[2]

    @pl.when(date == 0)
    def _():
        flows = flows_ref[...]
        member = member_rows(flows, knot_count, net_ref.shape[0]).astype(BF16)
        net_ref[...] = contract(member, flows[:, :knot_count], 0, 0).astype(BF16)

    values = contract(feat_ref[0], net_ref[...], 1, 1)
    values_ref[0] = values
    sums[pl.ds(date, 1), :] = jnp.sum(values, axis=0, keepdims=True)

    @pl.when(date == pl.num_programs(0) - 1)
    def _():
        out_ref[...] = jnp.broadcast_to(sums[...][None], out_ref.shape)


def slope_kernel(paths, arrived_ref, values_ref, weight_ref, base_ref, slope_ref, out_ref, sums):
    mean = jnp.sum(arrived_ref[...], axis=0) / paths
    for date in range(values_ref.shape[0]):
        row = slice(date, date + 1)
        shifted = values_ref[date] - mean[row] + base_ref[row, :]
        slope = weight_ref[row, :] * jax.nn.sigmoid(SHARPNESS * shifted)
        slope_ref[date] = slope
        sums[row, :] = jnp.sum(slope, axis=0, keepdims=True)
    out_ref[...] = jnp.broadcast_to(sums[...][None], out_ref.shape)


def adjoint_kernel(paths, arrived_ref, slope_ref, exact_ref, net_ref, flows_ref, blend_ref, out_ref, mean, rate, loads):
    date = pl.program_id(0)
    knot_count = exact_ref.shape[2]

    @pl.when(date == 0)
    def _():
        mean[...] = jnp.sum(arrived_ref[...], axis=0) / paths
        blend_ref[...] = jnp.zeros_like(blend_ref)
        rate[...] = jnp.zeros_like(rate)
        loads[...] = jnp.zeros_like(loads)

    _, horizon, loading = date_rows(date, knot_count)
    factor = loading * jnp.exp(-MEAN_REV * STEP_YEARS * (date + 1).astype(F32))
    exact = exact_ref[0]
    adjoint = (slope_ref[0] - mean[pl.ds(date, 1), :]).astype(BF16)
    product = contract(adjoint, net_ref[...], 1, 0) * exact
    blend_ref[...] += factor * product
    rate[...] += horizon * jnp.sum(product.reshape(-1, 8, knot_count), axis=0)
    loads[...] += contract(adjoint, exact.astype(BF16), 0, 0)

    @pl.when(date == pl.num_programs(0) - 1)
    def _():
        flows = flows_ref[...]
        member = member_rows(flows, knot_count, net_ref.shape[0])
        shares = jnp.zeros(member.shape, F32)
        for part in split(loads[...], 3):
            shares = shares + contract(flows[:, :knot_count], part, 1, 1)
        trades = jnp.sum(jnp.where(member, shares, 0.0).T, axis=0, keepdims=True) / paths
        total = -jnp.sum(rate[...], axis=0, keepdims=True) / paths
        shards, _, width = out_ref.shape
        gap = jnp.zeros((1, width - knot_count - trades.shape[1]), F32)
        row = jnp.concatenate([total, gap, trades], axis=1)
        out_ref[...] = jnp.broadcast_to(row[None], out_ref.shape)


def start_kernel(dates, blend_ref, load_ref, later_ref, out_ref):
    carried = contract(load_ref[...], blend_ref[...], 1, 1, HIGHEST)
    out_ref[...] = math.exp(-MEAN_REV * STEP_YEARS * dates) * later_ref[...] - carried


def final_kernel(index_ref, arrived_ref, jac_ref, knot_ref, alloc_ref):
    knot_count = jac_ref.shape[0]
    trades = alloc_ref.shape[1]
    row = jnp.sum(arrived_ref[...], axis=0)
    parts = row[:, round_up(knot_count, LANES) :]
    total = parts.shape[1]
    parts = jnp.broadcast_to(parts, (8, total))
    offset = index_ref[0] * trades
    alloc_ref[...] = pltpu.roll(parts, lax.rem(total - offset, total), 1)[0:1, :trades]
    column = jnp.broadcast_to(row[:, :knot_count], (LANES, knot_count)).T
    for first in range(0, knot_count, LANES):
        size = min(LANES, knot_count - first)
        cut = slice(first, first + size)
        knot_ref[:, cut] = jnp.sum(jac_ref[:, cut] * column[:, :size], axis=0, keepdims=True)


VMEM = pl.BlockSpec(memory_space=pltpu.VMEM)
SMEM = pl.BlockSpec(memory_space=pltpu.SMEM)


def whole(shape):
    return pl.BlockSpec(shape, lambda date: (0,) * len(shape))


def dated(shape):
    return pl.BlockSpec((1,) + shape, lambda date: (date,) + (0,) * len(shape))


def shaped(shape, dtype=F32):
    return jax.ShapeDtypeStruct(shape, dtype)


def cost(flops, moved):
    return pl.CostEstimate(flops=flops, bytes_accessed=moved, transcendentals=0)


def per_device(
    normals,
    start_state,
    later_adjoint,
    vol,
    factor_load,
    knots,
    spline_jac,
    cashflows,
    trade_set,
    trade_end,
    set_cpty,
    default_prob,
    base_value,
):
    dates, factors, paths = normals.shape
    knot_count = knots.shape[0]
    sets = base_value.shape[1]
    shards = lax.axis_size("path")
    trades = cashflows.shape[0]
    all_trades = trades * shards
    all_paths = paths * shards
    width = round_up(knot_count + 2, LANES)
    work = 2 * dates * paths * knot_count

    copies = pl.pallas_call(
        prep_kernel,
        out_shape=shaped((shards, trades, width), BF16),
        in_specs=[SMEM, SMEM, VMEM],
        out_specs=VMEM,
        name="prep",
    )(trade_end, trade_set, cashflows)
    flows = exchange(copies).reshape(all_trades, width)

    zero_rate, weight = pl.pallas_call(
        curve_kernel,
        out_shape=(shaped((1, knot_count)), shaped((dates, sets))),
        in_specs=[VMEM] * 4,
        out_specs=(VMEM, VMEM),
        cost_estimate=cost(2 * knot_count**2, 4 * knot_count**2),
        name="curve",
    )(knots.reshape(1, knot_count), spline_jac, set_cpty, default_prob)

    exact, features = pl.pallas_call(
        feature_kernel,
        out_shape=(
            shaped((dates, paths, knot_count)),
            shaped((dates, paths, knot_count), BF16),
        ),
        grid=(dates,),
        in_specs=[
            SMEM,
            dated((factors, paths)),
            whole((factors, paths)),
            whole((factors, knot_count)),
            whole((1, knot_count)),
        ],
        out_specs=(dated((paths, knot_count)), dated((paths, knot_count))),
        scratch_shapes=[
            pltpu.VMEM((factors, paths), F32),
            pltpu.VMEM((6 * factors, knot_count), BF16),
        ],
        cost_estimate=cost(6 * factors * work, 4 * work),
        name="features",
    )(vol, normals, start_state, factor_load, zero_rate)

    values, net_flows, copies = pl.pallas_call(
        value_kernel,
        out_shape=(
            shaped((dates, paths, sets)),
            shaped((sets, knot_count), BF16),
            shaped((shards, dates, sets)),
        ),
        grid=(dates,),
        in_specs=[whole((all_trades, width)), dated((paths, knot_count))],
        out_specs=(
            dated((paths, sets)),
            whole((sets, knot_count)),
            whole((shards, dates, sets)),
        ),
        scratch_shapes=[pltpu.VMEM((dates, sets), F32)],
        cost_estimate=cost(sets * work, 2 * work),
        name="values",
    )(flows, features)

    slope, copies = pl.pallas_call(
        functools.partial(slope_kernel, all_paths),
        out_shape=(shaped((dates, paths, sets)), shaped((shards, dates, sets))),
        in_specs=[VMEM] * 4,
        out_specs=(VMEM, VMEM),
        scratch_shapes=[pltpu.VMEM((dates, sets), F32)],
        cost_estimate=cost(16 * dates * paths * sets, 8 * dates * paths * sets),
        name="slopes",
    )(exchange(copies), values, weight, base_value)

    row_width = round_up(knot_count, LANES) + all_trades
    blend, copies = pl.pallas_call(
        functools.partial(adjoint_kernel, all_paths),
        out_shape=(shaped((paths, knot_count)), shaped((shards, 1, row_width))),
        grid=(dates,),
        in_specs=[
            whole((shards, dates, sets)),
            dated((paths, sets)),
            dated((paths, knot_count)),
            whole((sets, knot_count)),
            whole((all_trades, width)),
        ],
        out_specs=(whole((paths, knot_count)), whole((shards, 1, row_width))),
        scratch_shapes=[
            pltpu.VMEM((dates, sets), F32),
            pltpu.VMEM((8, knot_count), F32),
            pltpu.VMEM((sets, knot_count), F32),
        ],
        cost_estimate=cost(2 * sets * work, 4 * work),
        name="adjoint",
    )(exchange(copies), slope, exact, net_flows, flows)

    arrived = exchange(copies)
    start_adjoint = pl.pallas_call(
        functools.partial(start_kernel, dates),
        out_shape=shaped((factors, paths)),
        in_specs=[VMEM] * 3,
        out_specs=VMEM,
        cost_estimate=cost(2 * factors * paths * knot_count, 4 * paths * knot_count),
        name="start",
    )(blend, factor_load, later_adjoint)

    index = lax.axis_index("path").astype(jnp.int32).reshape(1)
    knot_grad, alloc = pl.pallas_call(
        final_kernel,
        out_shape=(shaped((1, knot_count)), shaped((1, trades))),
        in_specs=[SMEM, VMEM, VMEM],
        out_specs=(VMEM, VMEM),
        cost_estimate=cost(2 * knot_count**2, 4 * knot_count**2),
        name="final",
    )(index, arrived, spline_jac)
    return knot_grad.reshape(knot_count), alloc.reshape(trades), start_adjoint


def solution(mesh):
    in_specs = (
        P(None, None, ("group", "path")),
        P(None, ("group", "path")),
        P(None, ("group", "path")),
        P(),
        P(),
        P(),
        P(),
        P(("group", "path"), None),
        P(("group", "path"), None),
        P(("group", "path")),
        P("group", None),
        P(),
        P(None, "group"),
    )
    out_specs = (P("group"), P(("group", "path")), P(None, ("group", "path")))
    return jax.shard_map(
        per_device, mesh=mesh, in_specs=in_specs, out_specs=out_specs, check_vma=False
    )
```

time: 272 us -> 86.2 us (0.32)
  blocking collectives: 201 us -> 22.9 us
  matrix products: 42.6 us -> 0 us
  Pallas kernels: 0 us -> 38.7 us
  other arithmetic: 17.4 us -> 0 us
  starting transfers between devices: 0 us -> 9.9 us
  waiting for transfers between devices: 0 us -> 8.76 us
  local copies, waits for them, and re-layouts: 8.13 us -> 4.17 us
    psum x3 -> x0, blocking collectives: 118 us -> none  [the longest x1 41.2 us: per_device(): mean_slope = lax.psum(jnp.sum(slope, axis=2), 'path') / paths_all]
    all_gather x2 -> x0, blocking collectives: 83.6 us -> none  [the longest x1 41.9 us: per_device(): lax.all_gather(set_ids, 'path', axis=0, tiled=True)]
    dot_general x9 -> x0, matrix products: 42.6 us -> none  [the longest x1 7.57 us: per_device(): jnp.einsum('fm,imp->ifp', factor_load, feat_adjoint * feat_exact * loadin...]
    pallas_call x0 -> x8, Pallas kernels: none -> 38.7 us  [the longest x1 9.41 us: per_device(): pl.pallas_call(functools.partial(adjoint_kernel, all_paths), out_shape=(s...]
    all_to_all x0 -> x2, blocking collectives: none -> 22.9 us  [exchange(): return lax.all_to_all(copies, 'path', 0, 0)]
    unnamed x8 -> x0, other arithmetic: 12 us -> none
    all_to_all x0 -> x2, starting transfers between devices: none -> 9.9 us  [exchange(): return lax.all_to_all(copies, 'path', 0, 0)]
    all_to_all x0 -> x2, waiting for transfers between devices: none -> 8.76 us  [exchange(): return lax.all_to_all(copies, 'path', 0, 0)]
  transfers between devices with their start and end apart: 0 -> 2, of which waited for: 0 -> 2; matrix products, arithmetic and copies ran while one was open for 0% -> 2% of each run, Pallas kernels for 0% -> 17%
where the time goes in v2:
time: 86.2 us; the launch traced here: 85.1 us
  Pallas kernels  38.7 us (45%)
  blocking collectives  22.9 us (27%)
  starting transfers between devices  9.9 us (11%)
  waiting for transfers between devices  8.76 us (10%)
  local copies, waits for them, and re-layouts  4.17 us (5%)
    all_to_all x2, blocking collectives, exchange(): return lax.all_to_all(copies, 'path', 0, 0)  22.9 us
    all_to_all x2, starting transfers between devices, exchange(): return lax.all_to_all(copies, 'path', 0, 0)  9.9 us
    pallas_call x1, Pallas kernels, per_device(): pl.pallas_call(functools.partial(adjoint_kernel, all_paths), out_shape=(s...  9.41 us
    all_to_all x2, waiting for transfers between devices, exchange(): return lax.all_to_all(copies, 'path', 0, 0)  8.76 us
    pallas_call x1, Pallas kernels, per_device(): pl.pallas_call(feature_kernel, out_shape=(shaped((dates, paths, knot_coun...  7.93 us
    pallas_call x1, Pallas kernels, per_device(): pl.pallas_call(value_kernel, out_shape=(shaped((dates, paths, sets)), sha...  7.73 us
    unnamed x6, local copies, waits for them, and re-layouts  4.17 us
    pallas_call x1, Pallas kernels, per_device(): pl.pallas_call(final_kernel, out_shape=(shaped((1, knot_count)), shaped((...  3.22 us
  transfers between devices with their start and end apart: 2, of which 2 were waited for; matrix products, arithmetic and copies ran while one was open for 2% of the time, Pallas kernels for 17%

profile of v2, /device:TPU:0, one launch (start us, length us, event | category | flops | bytes accessed | tf_op | source)
XLA Modules:
  0.0 85.1 jit_solution(6539996429997424146)
XLA Ops:
  0.6 1.3 %copy.16.set_ref = s32[8,1]{1,0:T(8,128)} copy(s32[8,1]{0,1:T(1,128)} %param.21) | data formatting | bytes 64 | tf_op args[8]
  2.0 1.6 %prep.1 = bf16[32,8,1024]{2,1,0:T(8,128)(2,1)} custom-call(s32[8]{0:T(128)} %end_ref.1, s32[8,1]{1,0:T(8,128)} %copy.16.set_ref, bf16[8,960]{1,0:T(8,128)(2,1)} %cash_ref.1), custom_call_target="tpu_custom_call" | custom-call | tf_op jit(solution)/shard_map/prep/pallas_call | solution.py:253
  3.6 7.3 %all-to-all-start = ((bf16[32,8,1024]{2,1,0:T(8,128)(2,1)}), bf16[32,8,1024]{2,1,0:T(8,128)(2,1)S(1)}, u32[]{:S(2)}, u32[]{:S(2)}) async-start(bf16[32,8,1024]{2,1,0:T(8,128)(2,1)} %prep.1), calls=%async_computation | async-start | bytes 1048576 | tf_op jit(solution)/shard_map/all_to_all | solution.py:29
  10.9 1.4 %copy.17.cpty_ref = s32[128,1]{1,0:T(8,128)} copy(s32[128,1]{0,1:T(1,128)} %param.23) | data formatting | bytes 1024 | tf_op args[10]
  12.3 3.2 %curve.1 = (f32[1,960]{1,0:T(1,128)}, f32[8,128]{1,0:T(8,128)}) custom-call(f32[1,960]{1,0:T(1,128)} %bitcast.7, f32[960,960]{1,0:T(8,128)} %jac_ref.3, s32[128,1]{1,0:T(8,128)} %copy.17.cpty_ref, f32[8,64]{1,0:T(8,128)} %prob_ref.1), custom_call_target="tpu_custom_call" | custom-call | flops 1843200 | bytes 3686400 | tf_op jit(solution)/shard_map/curve/pallas_call | solution.py:262
  15.5 7.9 %features.1 = (f32[8,256,960]{2,1,0:T(8,128)}, bf16[8,256,960]{2,1,0:T(8,128)(2,1)}) custom-call(f32[8]{0:T(128)} %vol_ref.1, f32[8,32,256]{2,1,0:T(8,128)} %normals_ref.1, f32[32,256]{1,0:T(8,128)} %start_ref.1, f32[32,960]{1,0:T(8,128)} %load_ref.3, f32[1,960]{1,0:T(1,128)} %get-tuple-element.16.rate_ref), custom_call_target="tpu_custom_call" | custom-call | flops 754974720 | bytes 15728640 | tf_op jit(solution)/shard_map/features/pallas_call | solution.py:271
  23.4 3.1 %all-to-all-done = bf16[32,8,1024]{2,1,0:T(8,128)(2,1)S(1)} async-done(((bf16[32,8,1024]{2,1,0:T(8,128)(2,1)}), bf16[32,8,1024]{2,1,0:T(8,128)(2,1)S(1)}, u32[]{:S(2)}, u32[]{:S(2)}) %all-to-all-start) | async-done | bytes 524320 | tf_op jit(solution)/shard_map/all_to_all | solution.py:29
  26.5 0.0 copy-start
  26.5 0.8 copy-done
  27.3 7.7 %values.1 = (f32[8,256,128]{2,1,0:T(8,128)}, bf16[128,960]{1,0:T(8,128)(2,1)}, f32[32,8,128]{2,1,0:T(8,128)}) custom-call(bf16[256,1024]{1,0:T(8,128)(2,1)} %bitcast.5, bf16[8,256,960]{2,1,0:T(8,128)(2,1)} %get-tuple-element.17.feat_ref), custom_call_target="tpu_custom_call" | custom-call | flops 503316480 | bytes 7864320 | tf_op jit(solution)/shard_map/values/pallas_call | solution.py:294
  35.1 11.5 %all_to_all.20.arrived_ref = f32[32,8,128]{2,1,0:T(8,128)} all-to-all(f32[32,8,128]{2,1,0:T(8,128)} %get-tuple-element.18), channel_id=1, replica_groups=mesh['group'=1,'path'=32] {'path'}, dimensions={0} | all-to-all | bytes 262144 | tf_op jit(solution)/shard_map/all_to_all | solution.py:29
  46.5 2.6 %slopes.1 = (f32[8,256,128]{2,1,0:T(8,128)}, f32[32,8,128]{2,1,0:T(8,128)}) custom-call(f32[32,8,128]{2,1,0:T(8,128)} %all_to_all.20.arrived_ref, f32[8,256,128]{2,1,0:T(8,128)} %get-tuple-element.19.values_ref, f32[8,128]{1,0:T(8,128)} %get-tuple-element.20.weight_ref, f32[8,128]{1,0:T(8,128)} %base_ref.1), custom_call_target="tpu_custom_call" | custom-call | flops 4194304 | bytes 2097152 | tf_op jit(solution)/shard_map/slopes/pallas_call | solution.py:313
  49.1 11.5 %all_to_all.21.arrived_ref = f32[32,8,128]{2,1,0:T(8,128)} all-to-all(f32[32,8,128]{2,1,0:T(8,128)} %get-tuple-element.21), channel_id=1, replica_groups=mesh['group'=1,'path'=32] {'path'}, dimensions={0} | all-to-all | bytes 262144 | tf_op jit(solution)/shard_map/all_to_all | solution.py:29
  60.6 9.4 %adjoint.1 = (f32[256,960]{1,0:T(8,128)}, f32[32,1,1280]{2,1,0:T(1,128)}) custom-call(f32[32,8,128]{2,1,0:T(8,128)} %all_to_all.21.arrived_ref, f32[8,256,128]{2,1,0:T(8,128)} %get-tuple-element.22.slope_ref, f32[8,256,960]{2,1,0:T(8,128)} %get-tuple-element.23.exact_ref, bf16[128,960]{1,0:T(8,128)(2,1)} %get-tuple-element.24.net_ref, bf16[256,1024]{1,0:T(8,128)(2,1)} %bitcast.6), custom_call_target="tpu_custom_call" | custom-call | flops 1006632960 | bytes 15728640 | tf_op jit(solution)/shard_map/adjoint/pallas_call | solution.py:324
  70.0 2.6 %all-to-all-start.3 = ((f32[32,1,1280]{2,1,0:T(1,128)}), f32[32,1,1280]{2,1,0:T(1,128)S(1)}, u32[]{:S(2)}, u32[]{:S(2)}) async-start(f32[32,1,1280]{2,1,0:T(1,128)} %get-tuple-element.25), calls=%async_computation.3 | async-start | bytes 327680 | tf_op jit(solution)/shard_map/all_to_all | solution.py:29
  72.6 2.9 %start.1 = f32[32,256]{1,0:T(8,128)} custom-call(f32[256,960]{1,0:T(8,128)} %get-tuple-element.28.blend_ref, f32[32,960]{1,0:T(8,128)} %load_ref.3, f32[32,256]{1,0:T(8,128)} %later_ref.1), custom_call_target="tpu_custom_call" | custom-call | flops 15728640 | bytes 983040 | tf_op jit(solution)/shard_map/start/pallas_call | solution.py:346
  75.6 5.7 %all-to-all-done.3.arrived_ref = f32[32,1,1280]{2,1,0:T(1,128)S(1)} async-done(((f32[32,1,1280]{2,1,0:T(1,128)}), f32[32,1,1280]{2,1,0:T(1,128)S(1)}, u32[]{:S(2)}, u32[]{:S(2)}) %all-to-all-start.3) | async-done | bytes 163872 | tf_op jit(solution)/shard_map/all_to_all | solution.py:29
  81.2 0.0 copy-start.1
  81.2 0.7 copy-done.1
  81.9 3.2 %final.1 = (f32[1,960]{1,0:T(1,128)}, f32[1,8]{1,0:T(1,128)}) custom-call(s32[1]{0:T(128)} %bitcast.index_ref, f32[32,1,1280]{2,1,0:T(1,128)} %copy-done.1, f32[960,960]{1,0:T(8,128)} %jac_ref.3), custom_call_target="tpu_custom_call" | custom-call | flops 1843200 | bytes 3686400 | tf_op jit(solution)/shard_map/final/pallas_call | solution.py:356
Async XLA Ops:
  3.6 22.9 %all-to-all-start = ((bf16[32,8,1024]{2,1,0:T(8,128)(2,1)}), bf16[32,8,1024]{2,1,0:T(8,128)(2,1)S(1)}, u32[]{:S(2)}, u32[]{:S(2)}) async-start(bf16[32,8,1024]{2,1,0:T(8,128)(2,1)} %prep.1), calls=%async_computation | async-start | bytes 1048576 | tf_op jit(solution)/shard_map/all_to_all | solution.py:29
  26.5 0.8 copy-start
  70.0 11.2 %all-to-all-start.3 = ((f32[32,1,1280]{2,1,0:T(1,128)}), f32[32,1,1280]{2,1,0:T(1,128)S(1)}, u32[]{:S(2)}, u32[]{:S(2)}) async-start(f32[32,1,1280]{2,1,0:T(1,128)} %get-tuple-element.25), calls=%async_computation.3 | async-start | bytes 327680 | tf_op jit(solution)/shard_map/all_to_all | solution.py:29
  81.2 0.7 copy-start.1

commit v3 on v2

v3 whole, which is shorter than its diff:
```python
import functools
import math

import jax
import jax.numpy as jnp
from jax import lax
from jax.experimental import pallas as pl
from jax.experimental.pallas import tpu as pltpu
from jax.sharding import PartitionSpec as P

MEAN_REV = 0.05
STEP_YEARS = 0.25
HORIZON_YEARS = 30.0
SHARPNESS = 4.0
LOSS_RATE = 0.6
BASE = 128
LANES = 128
DECAY = math.exp(-MEAN_REV * STEP_YEARS)
HIGHEST = lax.Precision.HIGHEST
F32 = jnp.float32
BF16 = jnp.bfloat16


def round_up(size, step):
    return -(-size // step) * step


def exchange(copies):
    return lax.all_to_all(copies, "path", 0, 0)


def split(value, terms):
    parts = []
    for _ in range(terms):
        part = value.astype(BF16)
        parts.append(part)
        value = value - part.astype(F32)
    return parts


def contract(lhs, rhs, lhs_dim, rhs_dim, precision=None):
    return lax.dot_general(
        lhs,
        rhs,
        (((lhs_dim,), (rhs_dim,)), ((), ())),
        precision=precision,
        preferred_element_type=F32,
    )


def date_rows(date, knot_count):
    point = lax.broadcasted_iota(jnp.int32, (1, knot_count), 1) + 1
    alive = 120 * point > knot_count * (date + 1)
    maturity = HORIZON_YEARS * point.astype(F32) / knot_count
    fixing = STEP_YEARS * (date + 1).astype(F32)
    horizon = jnp.where(alive, maturity - fixing, 0.0)
    loading = (1.0 - jnp.exp(-MEAN_REV * horizon)) / MEAN_REV
    return alive, horizon, loading


def member_rows(flows, knot_count, set_count):
    digits = flows[:, knot_count : knot_count + 2].astype(F32)
    sets = (digits[:, 0:1] * BASE + digits[:, 1:2]).astype(jnp.int32)
    labels = lax.broadcasted_iota(jnp.int32, (flows.shape[0], set_count), 1)
    return sets == labels


def prep_kernel(end_ref, set_ref, cash_ref, out_ref):
    shards, trades, width = out_ref.shape
    knot_count = cash_ref.shape[1]
    row = lax.broadcasted_iota(jnp.int32, (trades, width), 0)
    point = lax.broadcasted_iota(jnp.int32, (trades, width), 1)
    ends = jnp.zeros((trades, width), jnp.int32)
    sets = jnp.zeros((trades, width), jnp.int32)
    for trade in range(trades):
        ends = jnp.where(row == trade, end_ref[trade], ends)
        sets = jnp.where(row == trade, set_ref[trade], sets)
    cash = jnp.concatenate(
        [cash_ref[...].astype(F32), jnp.zeros((trades, width - knot_count), F32)], axis=1
    )
    high = lax.shift_right_logical(sets, BASE.bit_length() - 1)
    low = sets & (BASE - 1)
    flows = jnp.where(point < jnp.minimum(ends, knot_count), cash, 0.0)
    flows = jnp.where(point == knot_count, high.astype(F32), flows)
    flows = jnp.where(point == knot_count + 1, low.astype(F32), flows).astype(BF16)
    for shard in range(shards):
        out_ref[shard] = flows


def curve_kernel(knots_ref, jac_ref, cpty_ref, prob_ref, rate_ref, weight_ref):
    knot_count = jac_ref.shape[0]
    column = jnp.sum(jac_ref[...] * knots_ref[...], axis=1, keepdims=True)
    rate_ref[...] = jnp.broadcast_to(column, (knot_count, LANES)).T[0:1]
    labels = lax.broadcasted_iota(jnp.int32, (prob_ref.shape[1], cpty_ref.shape[1]), 0)
    chosen = (cpty_ref[...] == labels).astype(F32)
    weight_ref[...] = LOSS_RATE * contract(prob_ref[...], chosen, 1, 0, HIGHEST)


def feature_kernel(
    vol_ref, normals_ref, start_ref, load_ref, rate_ref,
    exact_ref, feat_ref, exact_sum_ref, feat_sum_ref, state, stacked,
):
    date = pl.program_id(0)
    knot_count = load_ref.shape[1]

    @pl.when(date == 0)
    def _():
        state[...] = start_ref[...]
        high, middle, low = split(load_ref[...], 3)
        stacked[...] = jnp.concatenate([high, middle, high, middle, low, high], axis=0)

    now = DECAY * state[...] + vol_ref[date] * normals_ref[0]
    state[...] = now
    high, middle, low = split(now, 3)
    terms = jnp.concatenate([high, high, middle, middle, high, low], axis=0)
    alive, horizon, loading = date_rows(date, knot_count)
    discount = jnp.where(alive, jnp.exp(-rate_ref[...] * horizon), 0.0)
    shift = contract(terms, stacked[...], 0, 0)
    exact = discount * jnp.exp(-loading * shift)
    exact_ref[0] = exact
    rounded = exact.astype(BF16)
    feat_ref[0] = rounded
    row = pl.ds(date, 1)
    exact_sum_ref[row, :] = jnp.sum(exact, axis=0, keepdims=True)
    feat_sum_ref[row, :] = jnp.sum(rounded.astype(F32), axis=0, keepdims=True)


def net_kernel(flows_ref, feat_sum_ref, net_ref, out_ref):
    knot_count, sets = net_ref.shape
    flows = flows_ref[...]
    member = member_rows(flows, knot_count, sets).astype(BF16)
    net = contract(flows[:, :knot_count], member, 0, 0).astype(BF16)
    net_ref[...] = net
    sums = jnp.zeros(out_ref.shape[1:], F32)
    for part in split(feat_sum_ref[...], 3):
        sums = sums + contract(part, net, 1, 0)
    out_ref[...] = jnp.broadcast_to(sums[None], out_ref.shape)


def value_kernel(flows_ref, net_ref, feat_ref, values_ref, rows_ref):
    values_ref[0] = contract(feat_ref[0], net_ref[...], 1, 0)

    @pl.when(pl.program_id(0) == 0)
    def _():
        sets, knot_count = rows_ref.shape
        flows = flows_ref[...]
        member = member_rows(flows, knot_count, sets).astype(BF16)
        rows_ref[...] = contract(member, flows[:, :knot_count], 0, 0).astype(BF16)


def slope_of(values, mean, base, weight):
    return weight * jax.nn.sigmoid(SHARPNESS * (values - mean + base))


def slope_kernel(paths, arrived_ref, values_ref, weight_ref, base_ref, mean_ref, sums_ref, out_ref):
    mean_ref[...] = jnp.sum(arrived_ref[...], axis=0) / paths
    for date in range(values_ref.shape[0]):
        row = slice(date, date + 1)
        slope = slope_of(values_ref[date], mean_ref[row, :], base_ref[row, :], weight_ref[row, :])
        sums_ref[row, :] = jnp.sum(slope, axis=0, keepdims=True)
    out_ref[...] = jnp.broadcast_to(sums_ref[...][None], out_ref.shape)


def adjoint_kernel(
    mean_ref, sums_ref, weight_ref, base_ref, feat_sum_ref, values_ref, exact_ref, net_ref, flows_ref,
    blend_ref, rate_ref, trades_ref, cross_ref, rate, loads,
):
    date = pl.program_id(0)
    paths, knot_count = blend_ref.shape

    @pl.when(date == 0)
    def _():
        blend_ref[...] = jnp.zeros_like(blend_ref)
        rate[...] = jnp.zeros_like(rate)
        loads[...] = jnp.zeros_like(loads)

    _, horizon, loading = date_rows(date, knot_count)
    factor = loading * jnp.exp(-MEAN_REV * STEP_YEARS * (date + 1).astype(F32))
    exact = exact_ref[0]
    row = pl.ds(date, 1)
    slope = slope_of(values_ref[0], mean_ref[row, :], base_ref[row, :], weight_ref[row, :])
    adjoint = (slope - sums_ref[row, :] / paths).astype(BF16)
    product = contract(adjoint, net_ref[...], 1, 0) * exact
    blend_ref[...] += factor * product
    rate[...] += horizon * jnp.sum(product.reshape(-1, 8, knot_count), axis=0)
    loads[...] += contract(adjoint, exact.astype(BF16), 0, 0)

    @pl.when(date == pl.num_programs(0) - 1)
    def _():
        flows = flows_ref[...]
        member = member_rows(flows, knot_count, net_ref.shape[0])
        flows = flows[:, :knot_count]
        shares = jnp.zeros(member.shape, F32)
        for part in split(loads[...], 3):
            shares = shares + contract(flows, part, 1, 1)
        trades_ref[...] = jnp.sum(jnp.where(member, shares, 0.0).T, axis=0, keepdims=True)
        rate_ref[...] = jnp.sum(rate[...], axis=0, keepdims=True)
        cross = jnp.zeros(cross_ref.shape, F32)
        for part in split(feat_sum_ref[...], 3):
            cross = cross + contract(part, flows, 1, 1)
        cross_ref[...] = cross


def finish_kernel(
    paths, local, arrived_ref, sums_ref, exact_sum_ref, net_ref, flows_ref, rate_ref, trades_ref, cross_ref,
    shift_ref, out_ref,
):
    sets, knot_count = net_ref.shape
    gap = sums_ref[...] / local - jnp.sum(arrived_ref[...], axis=0) / paths
    flows = flows_ref[...]
    member = member_rows(flows, knot_count, sets).astype(BF16)
    spread = jnp.zeros(cross_ref.shape, F32)
    adjoint = jnp.zeros(shift_ref.shape, F32)
    for part in split(gap, 3):
        spread = spread + contract(part, member, 1, 1)
        adjoint = adjoint + contract(part, net_ref[...], 1, 0)
    total = rate_ref[...]
    for date in range(shift_ref.shape[0]):
        row = slice(date, date + 1)
        _, horizon, loading = date_rows(jnp.int32(date), knot_count)
        shift_ref[row, :] = loading * math.exp(-MEAN_REV * STEP_YEARS * (date + 1)) * adjoint[row]
        total = total + horizon * adjoint[row] * exact_sum_ref[row, :]
    trades = trades_ref[...] + jnp.sum(spread * cross_ref[...], axis=0, keepdims=True)
    shards, _, width = out_ref.shape
    pad = jnp.zeros((1, width - knot_count - trades.shape[1]), F32)
    row = jnp.concatenate([-total / paths, pad, trades / paths], axis=1)
    out_ref[...] = jnp.broadcast_to(row[None], out_ref.shape)


def start_kernel(blend_ref, shift_ref, exact_ref, load_ref, later_ref, out_ref, blend):
    date = pl.program_id(0)
    dates = shift_ref.shape[0]

    @pl.when(date == 0)
    def _():
        blend[...] = blend_ref[...]

    blend[...] += shift_ref[pl.ds(date, 1), :] * exact_ref[0]

    @pl.when(date == dates - 1)
    def _():
        carried = contract(load_ref[...], blend[...], 1, 1, HIGHEST)
        out_ref[...] = math.exp(-MEAN_REV * STEP_YEARS * dates) * later_ref[...] - carried


def final_kernel(index_ref, arrived_ref, jac_ref, knot_ref, alloc_ref):
    knot_count = jac_ref.shape[0]
    trades = alloc_ref.shape[1]
    row = jnp.sum(arrived_ref[...], axis=0)
    parts = row[:, round_up(knot_count, LANES) :]
    total = parts.shape[1]
    parts = jnp.broadcast_to(parts, (8, total))
    offset = index_ref[0] * trades
    alloc_ref[...] = pltpu.roll(parts, lax.rem(total - offset, total), 1)[0:1, :trades]
    column = jnp.broadcast_to(row[:, :knot_count], (LANES, knot_count)).T
    for first in range(0, knot_count, LANES):
        size = min(LANES, knot_count - first)
        cut = slice(first, first + size)
        knot_ref[:, cut] = jnp.sum(jac_ref[:, cut] * column[:, :size], axis=0, keepdims=True)


VMEM = pl.BlockSpec(memory_space=pltpu.VMEM)
SMEM = pl.BlockSpec(memory_space=pltpu.SMEM)


def shaped(shape, dtype=F32):
    return jax.ShapeDtypeStruct(shape, dtype)


def held(array):
    size = array.dtype.itemsize
    rows = array.shape[-2] if len(array.shape) > 1 else 1
    lead = math.prod(array.shape[:-2])
    return lead * round_up(rows, 8) * round_up(array.shape[-1], LANES) * size


def run(name, kernel, out_shape, operands, scalars=0, dates=0, dated=(), scratch=(), flops=0, spare=8 << 20):
    arrays = list(operands) + list(out_shape)
    room = sum(held(array) for array in scratch) + spare
    specs = []
    for place, array in enumerate(arrays):
        if place < scalars:
            specs.append(SMEM)
        elif not dates:
            specs.append(VMEM)
            room += held(array)
        elif place in dated:
            tail = array.shape[1:]
            specs.append(pl.BlockSpec((1,) + tail, lambda date, n=len(tail): (date,) + (0,) * n))
            room += 2 * held(array) // dates
        else:
            specs.append(pl.BlockSpec(array.shape, lambda date, n=len(array.shape): (0,) * n))
            room += 2 * held(array)
    moved = sum(held(array) for array in arrays)
    return pl.pallas_call(
        kernel,
        out_shape=tuple(out_shape),
        grid=(dates,) if dates else (),
        in_specs=specs[: len(operands)],
        out_specs=tuple(specs[len(operands) :]),
        scratch_shapes=[pltpu.VMEM(array.shape, array.dtype) for array in scratch],
        compiler_params=pltpu.CompilerParams(vmem_limit_bytes=min(room, 60 << 20)),
        cost_estimate=pl.CostEstimate(flops=flops, bytes_accessed=moved, transcendentals=0),
        name=name,
    )(*operands)


def per_device(
    normals,
    start_state,
    later_adjoint,
    vol,
    factor_load,
    knots,
    spline_jac,
    cashflows,
    trade_set,
    trade_end,
    set_cpty,
    default_prob,
    base_value,
):
    dates, factors, paths = normals.shape
    knot_count = knots.shape[0]
    sets = base_value.shape[1]
    shards = lax.axis_size("path")
    trades = cashflows.shape[0]
    all_trades = trades * shards
    all_paths = paths * shards
    width = round_up(knot_count + 2, LANES)
    work = 2 * dates * paths * knot_count
    grid_rows = shaped((dates, knot_count))
    set_rows = shaped((dates, sets))
    set_copies = shaped((shards, dates, sets))

    (copies,) = run(
        "prep",
        prep_kernel,
        [shaped((shards, trades, width), BF16)],
        [trade_end, trade_set.reshape(trades), cashflows],
        scalars=2,
    )
    arrived = exchange(copies)

    zero_rate, weight = run(
        "curve",
        curve_kernel,
        [shaped((1, knot_count)), set_rows],
        [knots.reshape(1, knot_count), spline_jac, set_cpty.reshape(1, sets), default_prob],
        flops=2 * knot_count**2,
    )
    exact, features, exact_sums, feat_sums = run(
        "features",
        feature_kernel,
        [
            shaped((dates, paths, knot_count)),
            shaped((dates, paths, knot_count), BF16),
            grid_rows,
            grid_rows,
        ],
        [vol, normals, start_state, factor_load, zero_rate],
        scalars=1,
        dates=dates,
        dated=(1, 5, 6),
        scratch=[shaped((factors, paths)), shaped((6 * factors, knot_count), BF16)],
        flops=6 * factors * work,
    )

    flows = arrived.reshape(all_trades, width)
    net_columns, copies = run(
        "net",
        net_kernel,
        [shaped((knot_count, sets), BF16), set_copies],
        [flows, feat_sums],
        flops=2 * sets * all_trades * knot_count,
    )
    arrived = exchange(copies)
    values, net_rows = run(
        "values",
        value_kernel,
        [shaped((dates, paths, sets)), shaped((sets, knot_count), BF16)],
        [flows, net_columns, features],
        dates=dates,
        dated=(2, 3),
        flops=sets * work,
    )
    mean, slope_sums, copies = run(
        "slopes",
        functools.partial(slope_kernel, all_paths),
        [set_rows, set_rows, set_copies],
        [arrived, values, weight, base_value],
        flops=16 * dates * paths * sets,
    )
    arrived = exchange(copies)
    blend, rate, trade_parts, cross = run(
        "adjoint",
        adjoint_kernel,
        [
            shaped((paths, knot_count)),
            shaped((1, knot_count)),
            shaped((1, all_trades)),
            shaped((dates, all_trades)),
        ],
        [mean, slope_sums, weight, base_value, feat_sums, values, exact, net_rows, flows],
        dates=dates,
        dated=(5, 6),
        scratch=[shaped((8, knot_count)), shaped((sets, knot_count))],
        flops=2 * sets * work,
    )
    row_width = round_up(knot_count, LANES) + all_trades
    shift, copies = run(
        "finish",
        functools.partial(finish_kernel, all_paths, paths),
        [grid_rows, shaped((shards, 1, row_width))],
        [arrived, slope_sums, exact_sums, net_rows, flows, rate, trade_parts, cross],
        flops=6 * sets * dates * knot_count,
    )
    arrived = exchange(copies)
    (start_adjoint,) = run(
        "start",
        start_kernel,
        [shaped((factors, paths))],
        [blend, shift, exact, factor_load, later_adjoint],
        dates=dates,
        dated=(2,),
        scratch=[shaped((paths, knot_count))],
        flops=2 * factors * paths * knot_count,
    )
    index = lax.axis_index("path").astype(jnp.int32).reshape(1)
    knot_grad, alloc = run(
        "final",
        final_kernel,
        [shaped((1, knot_count)), shaped((1, trades))],
        [index, arrived, spline_jac],
        scalars=1,
        flops=2 * knot_count**2,
    )
    return knot_grad.reshape(knot_count), alloc.reshape(trades), start_adjoint


def solution(mesh):
    in_specs = (
        P(None, None, ("group", "path")),
        P(None, ("group", "path")),
        P(None, ("group", "path")),
        P(),
        P(),
        P(),
        P(),
        P(("group", "path"), None),
        P(("group", "path"), None),
        P(("group", "path")),
        P("group", None),
        P(),
        P(None, "group"),
    )
    out_specs = (P("group"), P(("group", "path")), P(None, ("group", "path")))
    return jax.shard_map(
        per_device, mesh=mesh, in_specs=in_specs, out_specs=out_specs, check_vma=False
    )
```

time: 86.2 us -> 72.9 us (0.85)
  blocking collectives: 22.9 us -> 0 us
  local copies, waits for them, and re-layouts: 4.17 us -> 22.5 us
  Pallas kernels: 38.7 us -> 21.5 us
  starting transfers between devices: 9.9 us -> 20.6 us
  waiting for transfers between devices: 8.76 us -> 6.79 us
    all_to_all x2 -> x0, blocking collectives: 22.9 us -> none  [exchange(): return lax.all_to_all(copies, 'path', 0, 0)]
    unnamed x6 -> x38, local copies, waits for them, and re-layouts: 4.17 us -> 22.5 us
    pallas_call x8 -> x10, Pallas kernels: 38.7 us -> 21.5 us  [run(): pl.pallas_call(kernel, out_shape=tuple(out_shape), grid=(dates,) if dates...]
    all_to_all x2 -> x4, starting transfers between devices: 9.9 us -> 20.6 us  [exchange(): return lax.all_to_all(copies, 'path', 0, 0)]
    all_to_all x2 -> x4, waiting for transfers between devices: 8.76 us -> 6.79 us  [exchange(): return lax.all_to_all(copies, 'path', 0, 0)]
  transfers between devices with their start and end apart: 2 -> 4, of which waited for: 2 -> 4; matrix products, arithmetic and copies ran while one was open for 2% -> 0% of each run, Pallas kernels for 17% -> 21%
where the time goes in v3:
time: 72.9 us; the launch traced here: 72.3 us
  local copies, waits for them, and re-layouts  22.5 us (31%)
  Pallas kernels  21.5 us (29%)
  starting transfers between devices  20.6 us (28%)
  waiting for transfers between devices  6.79 us (9%)
  between operations  0.81 us (1%)
    unnamed x38, local copies, waits for them, and re-layouts  22.5 us
    pallas_call x10, Pallas kernels, run(): pl.pallas_call(kernel, out_shape=tuple(out_shape), grid=(dates,) if dates...  21.5 us
    all_to_all x4, starting transfers between devices, exchange(): return lax.all_to_all(copies, 'path', 0, 0)  20.6 us
    all_to_all x4, waiting for transfers between devices, exchange(): return lax.all_to_all(copies, 'path', 0, 0)  6.79 us
  transfers between devices with their start and end apart: 4, of which 4 were waited for; matrix products, arithmetic and copies ran while one was open for 0% of the time, Pallas kernels for 21%

profile of v3, /device:TPU:0, one launch (start us, length us, event | category | flops | bytes accessed | tf_op | source)
XLA Modules:
  0.0 72.3 jit_solution(13133427272430020567)
XLA Ops:
  0.7 0.7 %copy-done.10 = bf16[8,960]{1,0:T(8,128)(2,1)S(1)} copy-done((bf16[8,960]{1,0:T(8,128)(2,1)S(1)}, bf16[8,960]{1,0:T(8,128)(2,1)}, u32[]{:S(2)}) %copy-start.10) | copy-done | bytes 15384
  2.7 1.4 %prep.1 = bf16[32,8,1024]{2,1,0:T(8,128)(2,1)} custom-call(s32[8]{0:T(128)S(1)} %copy-done.14, s32[8]{0:T(128)S(1)} %bitcast.13, bf16[8,960]{1,0:T(8,128)(2,1)S(1)} %copy-done.10), custom_call_target="tpu_custom_call" | custom-call | bytes 548864 | tf_op jit(solution)/shard_map/prep/pallas_call | solution.py:295
  4.2 7.3 %all-to-all-start = ((bf16[32,8,1024]{2,1,0:T(8,128)(2,1)}), bf16[32,8,1024]{2,1,0:T(8,128)(2,1)S(1)}, u32[]{:S(2)}, u32[]{:S(2)}) async-start(bf16[32,8,1024]{2,1,0:T(8,128)(2,1)} %prep.1), calls=%async_computation | async-start | bytes 1048576 | tf_op jit(solution)/shard_map/all_to_all | solution.py:29
  11.5 2.1 %copy-done.3 = f32[960,960]{1,0:T(8,128)S(1)} copy-done((f32[960,960]{1,0:T(8,128)S(1)}, f32[960,960]{1,0:T(8,128)}, u32[]{:S(2)}) %copy-start.3) | copy-done | bytes 3686424
  16.1 4.9 %features.1 = (f32[8,256,960]{2,1,0:T(8,128)S(1)}, bf16[8,256,960]{2,1,0:T(8,128)(2,1)S(1)}, f32[8,960]{1,0:T(8,128)S(1)}, f32[8,960]{1,0:T(8,128)S(1)}) custom-call(f32[8]{0:T(128)S(1)} %copy-done.18, f32[8,32,256]{2,1,0:T(8,128)S(1)} %copy-done.16, f32[32,256]{1,0:T(8,128)S(1)} %copy-done.17, f32[32,960]{1,0:T(8,128)S(1)} %copy-done.7, ...), custom_call_target="tpu_custom_call" | custom-call | flops 754974720 | bytes 13111296 | tf_op jit(solution)/shard_map/features/pallas_call | solution.py:295
  21.1 3.3 %copy-done = f32[8,256,960]{2,1,0:T(8,128)} copy-done((f32[8,256,960]{2,1,0:T(8,128)}, f32[8,256,960]{2,1,0:T(8,128)S(1)}, u32[]{:S(2)}) %copy-start) | copy-done | bytes 7864344
  24.3 2.0 %copy-done.5 = bf16[8,256,960]{2,1,0:T(8,128)(2,1)} copy-done((bf16[8,256,960]{2,1,0:T(8,128)(2,1)}, bf16[8,256,960]{2,1,0:T(8,128)(2,1)S(1)}, u32[]{:S(2)}) %copy-start.5) | copy-done | bytes 3932184
  26.3 0.8 %all-to-all-done = bf16[32,8,1024]{2,1,0:T(8,128)(2,1)S(1)} async-done(((bf16[32,8,1024]{2,1,0:T(8,128)(2,1)}), bf16[32,8,1024]{2,1,0:T(8,128)(2,1)S(1)}, u32[]{:S(2)}, u32[]{:S(2)}) %all-to-all-start) | async-done | bytes 524320 | tf_op jit(solution)/shard_map/all_to_all | solution.py:29
  27.1 1.5 %net.1 = (bf16[960,128]{1,0:T(8,128)(2,1)S(1)}, f32[32,8,128]{2,1,0:T(8,128)}) custom-call(bf16[256,1024]{1,0:T(8,128)(2,1)S(1)} %bitcast.7, f32[8,960]{1,0:T(8,128)S(1)} %get-tuple-element.25.feat_sum_ref), custom_call_target="tpu_custom_call" | custom-call | flops 62914560 | bytes 933888 | tf_op jit(solution)/shard_map/net/pallas_call | solution.py:295
  28.7 5.0 %all-to-all-start.1 = ((f32[32,8,128]{2,1,0:T(8,128)}), f32[32,8,128]{2,1,0:T(8,128)S(1)}, u32[]{:S(2)}, u32[]{:S(2)}) async-start(f32[32,8,128]{2,1,0:T(8,128)} %get-tuple-element.26), calls=%async_computation.1 | async-start | bytes 262144 | tf_op jit(solution)/shard_map/all_to_all | solution.py:29
  33.7 2.2 %copy-done.6 = bf16[8,256,960]{2,1,0:T(8,128)(2,1)S(1)} copy-done((bf16[8,256,960]{2,1,0:T(8,128)(2,1)S(1)}, bf16[8,256,960]{2,1,0:T(8,128)(2,1)}, u32[]{:S(2)}) %copy-start.6) | copy-done | bytes 3932184
  35.9 2.8 %values.1 = (f32[8,256,128]{2,1,0:T(8,128)S(1)}, bf16[128,960]{1,0:T(8,128)(2,1)S(1)}) custom-call(bf16[256,1024]{1,0:T(8,128)(2,1)S(1)} %bitcast.8, bf16[960,128]{1,0:T(8,128)(2,1)S(1)} %get-tuple-element.27.net_ref, bf16[8,256,960]{2,1,0:T(8,128)(2,1)S(1)} %copy-done.6), custom_call_target="tpu_custom_call" | custom-call | flops 503316480 | bytes 6275072 | tf_op jit(solution)/shard_map/values/pallas_call | solution.py:295
  38.7 3.2 %all-to-all-done.1.arrived_ref = f32[32,8,128]{2,1,0:T(8,128)S(1)} async-done(((f32[32,8,128]{2,1,0:T(8,128)}), f32[32,8,128]{2,1,0:T(8,128)S(1)}, u32[]{:S(2)}, u32[]{:S(2)}) %all-to-all-start.1) | async-done | bytes 131104 | tf_op jit(solution)/shard_map/all_to_all | solution.py:29
  41.9 1.0 %slopes.1 = (f32[8,128]{1,0:T(8,128)S(1)}, f32[8,128]{1,0:T(8,128)S(1)}, f32[32,8,128]{2,1,0:T(8,128)}) custom-call(f32[32,8,128]{2,1,0:T(8,128)S(1)} %all-to-all-done.1.arrived_ref, f32[8,256,128]{2,1,0:T(8,128)S(1)} %get-tuple-element.29.values_ref, f32[8,128]{1,0:T(8,128)S(1)} %get-tuple-element.30.weight_ref, f32[8,128]{1,0:T(8,128)S(1)} %copy-done.9), custom_call_target="tpu_custom_call" | custom-call | flops 4194304 | bytes 1327104 | tf_op jit(solution)/shard_map/slopes/pallas_call | solution.py:295
  42.9 2.6 %all-to-all-start.2 = ((f32[32,8,128]{2,1,0:T(8,128)}), f32[32,8,128]{2,1,0:T(8,128)S(1)}, u32[]{:S(2)}, u32[]{:S(2)}) async-start(f32[32,8,128]{2,1,0:T(8,128)} %get-tuple-element.31), calls=%async_computation.2 | async-start | bytes 262144 | tf_op jit(solution)/shard_map/all_to_all | solution.py:29
  45.5 3.4 %copy-done.1 = f32[8,256,960]{2,1,0:T(8,128)S(1)} copy-done((f32[8,256,960]{2,1,0:T(8,128)S(1)}, f32[8,256,960]{2,1,0:T(8,128)}, u32[]{:S(2)}) %copy-start.1) | copy-done | bytes 7864344
  48.9 4.6 %adjoint.1 = (f32[256,960]{1,0:T(8,128)S(1)}, f32[1,960]{1,0:T(1,128)S(1)}, f32[1,256]{1,0:T(1,128)S(1)}, f32[8,256]{1,0:T(8,128)S(1)}) custom-call(f32[8,128]{1,0:T(8,128)S(1)} %get-tuple-element.35.mean_ref, f32[8,128]{1,0:T(8,128)S(1)} %get-tuple-element.32.sums_ref, f32[8,128]{1,0:T(8,128)S(1)} %get-tuple-element.30.weight_ref, f32[8,128]{1,0:T(8,128)S(1)} %copy-done.9, ...), custom_call_target="tpu_custom_call" | custom-call | flops 1006632960 | bytes 11370496 | tf_op jit(solution)/shard_map/adjoint/pallas_call | solution.py:295
  53.7 1.2 %finish.1 = (f32[8,960]{1,0:T(8,128)S(1)}, f32[32,1,1280]{2,1,0:T(1,128)}) custom-call(f32[32,8,128]{2,1,0:T(8,128)S(1)} %all-to-all-done.2.arrived_ref, f32[8,128]{1,0:T(8,128)S(1)} %get-tuple-element.32.sums_ref, f32[8,960]{1,0:T(8,128)S(1)} %get-tuple-element.33.exact_sum_ref, bf16[128,960]{1,0:T(8,128)(2,1)S(1)} %get-tuple-element.34.net_ref, ...), custom_call_target="tpu_custom_call" | custom-call | flops 5898240 | bytes 2347008 | tf_op jit(solution)/shard_map/finish/pallas_call | solution.py:295
  54.9 5.6 %all-to-all-start.3 = ((f32[32,1,1280]{2,1,0:T(1,128)}), f32[32,1,1280]{2,1,0:T(1,128)S(1)}, u32[]{:S(2)}, u32[]{:S(2)}) async-start(f32[32,1,1280]{2,1,0:T(1,128)} %get-tuple-element.40), calls=%async_computation.3 | async-start | bytes 327680 | tf_op jit(solution)/shard_map/all_to_all | solution.py:29
  60.5 3.4 %copy-done.2 = f32[8,256,960]{2,1,0:T(8,128)S(1)} copy-done((f32[8,256,960]{2,1,0:T(8,128)S(1)}, f32[8,256,960]{2,1,0:T(8,128)}, u32[]{:S(2)}) %copy-start.2) | copy-done | bytes 7864344
  63.9 2.7 %start.1 = f32[32,256]{1,0:T(8,128)} custom-call(f32[256,960]{1,0:T(8,128)S(1)} %get-tuple-element.43.blend_ref, f32[8,960]{1,0:T(8,128)S(1)} %get-tuple-element.44.shift_ref, f32[8,256,960]{2,1,0:T(8,128)S(1)} %copy-done.2, f32[32,960]{1,0:T(8,128)S(1)} %copy-done.7, f32[32,256]{1,0:T(8,128)S(1)} %copy-done.8), custom_call_target="tpu_custom_call" | custom-call | flops 15728640 | bytes 9666560 | tf_op jit(solution)/shard_map/start/pallas_call | solution.py:295
  66.6 2.5 %all-to-all-done.3.arrived_ref = f32[32,1,1280]{2,1,0:T(1,128)S(1)} async-done(((f32[32,1,1280]{2,1,0:T(1,128)}), f32[32,1,1280]{2,1,0:T(1,128)S(1)}, u32[]{:S(2)}, u32[]{:S(2)}) %all-to-all-start.3) | async-done | bytes 163872 | tf_op jit(solution)/shard_map/all_to_all | solution.py:29
  69.1 2.1 %copy-done.4 = f32[960,960]{1,0:T(8,128)S(1)} copy-done((f32[960,960]{1,0:T(8,128)S(1)}, f32[960,960]{1,0:T(8,128)}, u32[]{:S(2)}) %copy-start.4) | copy-done | bytes 3686424
  71.3 1.0 %final.1 = (f32[1,960]{1,0:T(1,128)}, f32[1,8]{1,0:T(1,128)}) custom-call(s32[1]{0:T(128)} %bitcast.index_ref, f32[32,1,1280]{2,1,0:T(1,128)S(1)} %all-to-all-done.3.arrived_ref, f32[960,960]{1,0:T(8,128)S(1)} %copy-done.4), custom_call_target="tpu_custom_call" | custom-call | flops 1843200 | bytes 5283840 | tf_op jit(solution)/shard_map/final/pallas_call | solution.py:295
  (32 shorter events, 4.0 us)
Async XLA Ops:
  0.6 15.5 %copy-start.7 = (f32[32,960]{1,0:T(8,128)S(1)}, f32[32,960]{1,0:T(8,128)}, u32[]{:S(2)}) copy-start(f32[32,960]{1,0:T(8,128)} %load_ref.3) | copy-start | bytes 368644
  0.6 0.8 %copy-start.10 = (bf16[8,960]{1,0:T(8,128)(2,1)S(1)}, bf16[8,960]{1,0:T(8,128)(2,1)}, u32[]{:S(2)}) copy-start(bf16[8,960]{1,0:T(8,128)(2,1)} %cash_ref.1) | copy-start | bytes 46084
  1.4 0.7 copy-start.14
  2.1 0.7 copy-start.15
  2.7 13.4 %copy-start.16 = (f32[8,32,256]{2,1,0:T(8,128)S(1)}, f32[8,32,256]{2,1,0:T(8,128)}, u32[]{:S(2)}) copy-start(f32[8,32,256]{2,1,0:T(8,128)} %normals_ref.1) | copy-start | bytes 786436
  2.7 13.4 %copy-start.17 = (f32[32,256]{1,0:T(8,128)S(1)}, f32[32,256]{1,0:T(8,128)}, u32[]{:S(2)}) copy-start(f32[32,256]{1,0:T(8,128)} %start_ref.1) | copy-start | bytes 98308
  2.7 13.4 %copy-start.18 = (f32[8]{0:T(128)S(1)}, f32[8]{0:T(128)}, u32[]{:S(2)}) copy-start(f32[8]{0:T(128)} %vol_ref.1) | copy-start | bytes 100
  4.2 22.9 %all-to-all-start = ((bf16[32,8,1024]{2,1,0:T(8,128)(2,1)}), bf16[32,8,1024]{2,1,0:T(8,128)(2,1)S(1)}, u32[]{:S(2)}, u32[]{:S(2)}) async-start(bf16[32,8,1024]{2,1,0:T(8,128)(2,1)} %prep.1), calls=%async_computation | async-start | bytes 1048576 | tf_op jit(solution)/shard_map/all_to_all | solution.py:29
  11.5 2.1 %copy-start.3 = (f32[960,960]{1,0:T(8,128)S(1)}, f32[960,960]{1,0:T(8,128)}, u32[]{:S(2)}) copy-start(f32[960,960]{1,0:T(8,128)} %jac_ref.3) | copy-start | bytes 11059204
  13.6 0.7 copy-start.11
  14.3 0.7 copy-start.12
  15.0 0.7 copy-start.13
  16.1 25.8 %copy-start.9 = (f32[8,128]{1,0:T(8,128)S(1)}, f32[8,128]{1,0:T(8,128)}, u32[]{:S(2)}) copy-start(f32[8,128]{1,0:T(8,128)} %base_ref.3) | copy-start | bytes 12292
  21.0 3.3 %copy-start = (f32[8,256,960]{2,1,0:T(8,128)}, f32[8,256,960]{2,1,0:T(8,128)S(1)}, u32[]{:S(2)}) copy-start(f32[8,256,960]{2,1,0:T(8,128)S(1)} %get-tuple-element.36.exact_ref) | copy-start | bytes 23592964
  24.3 2.0 %copy-start.5 = (bf16[8,256,960]{2,1,0:T(8,128)(2,1)}, bf16[8,256,960]{2,1,0:T(8,128)(2,1)S(1)}, u32[]{:S(2)}) copy-start(bf16[8,256,960]{2,1,0:T(8,128)(2,1)S(1)} %get-tuple-element.28.feat_ref) | copy-start | bytes 11796484
  28.7 13.3 %all-to-all-start.1 = ((f32[32,8,128]{2,1,0:T(8,128)}), f32[32,8,128]{2,1,0:T(8,128)S(1)}, u32[]{:S(2)}, u32[]{:S(2)}) async-start(f32[32,8,128]{2,1,0:T(8,128)} %get-tuple-element.26), calls=%async_computation.1 | async-start | bytes 262144 | tf_op jit(solution)/shard_map/all_to_all | solution.py:29
  33.7 2.2 %copy-start.6 = (bf16[8,256,960]{2,1,0:T(8,128)(2,1)S(1)}, bf16[8,256,960]{2,1,0:T(8,128)(2,1)}, u32[]{:S(2)}) copy-start(bf16[8,256,960]{2,1,0:T(8,128)(2,1)} %copy-done.5) | copy-start | bytes 11796484
  42.9 10.8 %all-to-all-start.2 = ((f32[32,8,128]{2,1,0:T(8,128)}), f32[32,8,128]{2,1,0:T(8,128)S(1)}, u32[]{:S(2)}, u32[]{:S(2)}) async-start(f32[32,8,128]{2,1,0:T(8,128)} %get-tuple-element.31), calls=%async_computation.2 | async-start | bytes 262144 | tf_op jit(solution)/shard_map/all_to_all | solution.py:29
  45.5 3.4 %copy-start.1 = (f32[8,256,960]{2,1,0:T(8,128)S(1)}, f32[8,256,960]{2,1,0:T(8,128)}, u32[]{:S(2)}) copy-start(f32[8,256,960]{2,1,0:T(8,128)} %copy-done) | copy-start | bytes 23592964
  48.9 11.6 %copy-start.8 = (f32[32,256]{1,0:T(8,128)S(1)}, f32[32,256]{1,0:T(8,128)}, u32[]{:S(2)}) copy-start(f32[32,256]{1,0:T(8,128)} %later_ref.1) | copy-start | bytes 98308
  54.9 14.3 %all-to-all-start.3 = ((f32[32,1,1280]{2,1,0:T(1,128)}), f32[32,1,1280]{2,1,0:T(1,128)S(1)}, u32[]{:S(2)}, u32[]{:S(2)}) async-start(f32[32,1,1280]{2,1,0:T(1,128)} %get-tuple-element.40), calls=%async_computation.3 | async-start | bytes 327680 | tf_op jit(solution)/shard_map/all_to_all | solution.py:29
  60.5 3.4 %copy-start.2 = (f32[8,256,960]{2,1,0:T(8,128)S(1)}, f32[8,256,960]{2,1,0:T(8,128)}, u32[]{:S(2)}) copy-start(f32[8,256,960]{2,1,0:T(8,128)} %copy-done) | copy-start | bytes 23592964
  69.1 2.1 %copy-start.4 = (f32[960,960]{1,0:T(8,128)S(1)}, f32[960,960]{1,0:T(8,128)}, u32[]{:S(2)}) copy-start(f32[960,960]{1,0:T(8,128)} %jac_ref.3) | copy-start | bytes 11059204

commit v4 on v3

--- a/solution.py
+++ b/solution.py
@@ -15,6 +15,8 @@
 LOSS_RATE = 0.6
 BASE = 128
 LANES = 128
+LARGE = 58 << 20
+MIDDLE = 50 << 20
 DECAY = math.exp(-MEAN_REV * STEP_YEARS)
 HIGHEST = lax.Precision.HIGHEST
 F32 = jnp.float32
@@ -46,6 +48,29 @@
         precision=precision,
         preferred_element_type=F32,
     )
+
+
+def folded(parts, rows):
+    total = parts[:rows]
+    for first in range(rows, parts.shape[0], rows):
+        total = total + parts[first : first + rows]
+    return total
+
+
+def stack(value):
+    return jnp.concatenate(split(value, 3), axis=0)
+
+
+def each(count, body):
+    def step(index, carry):
+        body(index)
+        return carry
+
+    lax.fori_loop(0, count, step, 0)
+
+
+def copy_of(source, target, sems, index):
+    return pltpu.make_async_copy(source.at[index], target.at[index], sems.at[index])
 
 
 def date_rows(date, knot_count):
@@ -98,31 +123,36 @@
 
 def feature_kernel(
     vol_ref, normals_ref, start_ref, load_ref, rate_ref,
-    exact_ref, feat_ref, exact_sum_ref, feat_sum_ref, state, stacked,
+    exact_hbm, feat_hbm, exact_sum_ref, feat_sum_ref,
+    exact_buf, feat_buf, exact_sems, feat_sems, state, stacked,
 ):
-    date = pl.program_id(0)
+    dates = normals_ref.shape[0]
     knot_count = load_ref.shape[1]
-
-    @pl.when(date == 0)
-    def _():
-        state[...] = start_ref[...]
-        high, middle, low = split(load_ref[...], 3)
-        stacked[...] = jnp.concatenate([high, middle, high, middle, low, high], axis=0)
-
-    now = DECAY * state[...] + vol_ref[date] * normals_ref[0]
-    state[...] = now
-    high, middle, low = split(now, 3)
-    terms = jnp.concatenate([high, high, middle, middle, high, low], axis=0)
-    alive, horizon, loading = date_rows(date, knot_count)
-    discount = jnp.where(alive, jnp.exp(-rate_ref[...] * horizon), 0.0)
-    shift = contract(terms, stacked[...], 0, 0)
-    exact = discount * jnp.exp(-loading * shift)
-    exact_ref[0] = exact
-    rounded = exact.astype(BF16)
-    feat_ref[0] = rounded
-    row = pl.ds(date, 1)
-    exact_sum_ref[row, :] = jnp.sum(exact, axis=0, keepdims=True)
-    feat_sum_ref[row, :] = jnp.sum(rounded.astype(F32), axis=0, keepdims=True)
+    state[...] = start_ref[...]
+    high, middle, low = split(load_ref[...], 3)
+    stacked[...] = jnp.concatenate([high, middle, high, middle, low, high], axis=0)
+
+    def one(date):
+        now = DECAY * state[...] + vol_ref[date] * normals_ref[date]
+        state[...] = now
+        high, middle, low = split(now, 3)
+        terms = jnp.concatenate([high, high, middle, middle, high, low], axis=0)
+        alive, horizon, loading = date_rows(date, knot_count)
+        discount = jnp.where(alive, jnp.exp(-rate_ref[...] * horizon), 0.0)
+        shift = contract(terms, stacked[...], 0, 0)
+        exact = discount * jnp.exp(-loading * shift)
+        exact_buf[date] = exact
+        rounded = exact.astype(BF16)
+        feat_buf[date] = rounded
+        copy_of(exact_buf, exact_hbm, exact_sems, date).start()
+        copy_of(feat_buf, feat_hbm, feat_sems, date).start()
+        row = pl.ds(date, 1)
+        exact_sum_ref[row, :] = jnp.sum(exact, axis=0, keepdims=True)
+        feat_sum_ref[row, :] = jnp.sum(rounded.astype(F32), axis=0, keepdims=True)
+
+    each(dates, one)
+    each(dates, lambda date: copy_of(exact_buf, exact_hbm, exact_sems, date).wait())
+    each(dates, lambda date: copy_of(feat_buf, feat_hbm, feat_sems, date).wait())
 
 
 def net_kernel(flows_ref, feat_sum_ref, net_ref, out_ref):
@@ -131,21 +161,23 @@
     member = member_rows(flows, knot_count, sets).astype(BF16)
     net = contract(flows[:, :knot_count], member, 0, 0).astype(BF16)
     net_ref[...] = net
-    sums = jnp.zeros(out_ref.shape[1:], F32)
-    for part in split(feat_sum_ref[...], 3):
-        sums = sums + contract(part, net, 1, 0)
+    sums = folded(contract(stack(feat_sum_ref[...]), net, 1, 0), out_ref.shape[1])
     out_ref[...] = jnp.broadcast_to(sums[None], out_ref.shape)
 
 
-def value_kernel(flows_ref, net_ref, feat_ref, values_ref, rows_ref):
-    values_ref[0] = contract(feat_ref[0], net_ref[...], 1, 0)
-
-    @pl.when(pl.program_id(0) == 0)
-    def _():
-        sets, knot_count = rows_ref.shape
-        flows = flows_ref[...]
-        member = member_rows(flows, knot_count, sets).astype(BF16)
-        rows_ref[...] = contract(member, flows[:, :knot_count], 0, 0).astype(BF16)
+def value_kernel(flows_ref, net_ref, feat_hbm, values_ref, rows_ref, feat_buf, sems):
+    dates = values_ref.shape[0]
+    each(dates, lambda date: copy_of(feat_hbm, feat_buf, sems, date).start())
+    sets, knot_count = rows_ref.shape
+    flows = flows_ref[...]
+    member = member_rows(flows, knot_count, sets).astype(BF16)
+    rows_ref[...] = contract(member, flows[:, :knot_count], 0, 0).astype(BF16)
+
+    def one(date):
+        copy_of(feat_hbm, feat_buf, sems, date).wait()
+        values_ref[date] = contract(feat_buf[date], net_ref[...], 1, 0)
+
+    each(dates, one)
 
 
 def slope_of(values, mean, base, weight):
@@ -162,43 +194,39 @@
 
 
 def adjoint_kernel(
-    mean_ref, sums_ref, weight_ref, base_ref, feat_sum_ref, values_ref, exact_ref, net_ref, flows_ref,
-    blend_ref, rate_ref, trades_ref, cross_ref, rate, loads,
+    mean_ref, sums_ref, weight_ref, base_ref, feat_sum_ref, values_ref, net_ref, flows_ref, exact_hbm,
+    blend_ref, rate_ref, trades_ref, cross_ref, exact_buf, sems, rate, loads,
 ):
-    date = pl.program_id(0)
+    dates = values_ref.shape[0]
     paths, knot_count = blend_ref.shape
-
-    @pl.when(date == 0)
-    def _():
-        blend_ref[...] = jnp.zeros_like(blend_ref)
-        rate[...] = jnp.zeros_like(rate)
-        loads[...] = jnp.zeros_like(loads)
-
-    _, horizon, loading = date_rows(date, knot_count)
-    factor = loading * jnp.exp(-MEAN_REV * STEP_YEARS * (date + 1).astype(F32))
-    exact = exact_ref[0]
-    row = pl.ds(date, 1)
-    slope = slope_of(values_ref[0], mean_ref[row, :], base_ref[row, :], weight_ref[row, :])
-    adjoint = (slope - sums_ref[row, :] / paths).astype(BF16)
-    product = contract(adjoint, net_ref[...], 1, 0) * exact
-    blend_ref[...] += factor * product
-    rate[...] += horizon * jnp.sum(product.reshape(-1, 8, knot_count), axis=0)
-    loads[...] += contract(adjoint, exact.astype(BF16), 0, 0)
-
-    @pl.when(date == pl.num_programs(0) - 1)
-    def _():
-        flows = flows_ref[...]
-        member = member_rows(flows, knot_count, net_ref.shape[0])
-        flows = flows[:, :knot_count]
-        shares = jnp.zeros(member.shape, F32)
-        for part in split(loads[...], 3):
-            shares = shares + contract(flows, part, 1, 1)
-        trades_ref[...] = jnp.sum(jnp.where(member, shares, 0.0).T, axis=0, keepdims=True)
-        rate_ref[...] = jnp.sum(rate[...], axis=0, keepdims=True)
-        cross = jnp.zeros(cross_ref.shape, F32)
-        for part in split(feat_sum_ref[...], 3):
-            cross = cross + contract(part, flows, 1, 1)
-        cross_ref[...] = cross
+    each(dates, lambda date: copy_of(exact_hbm, exact_buf, sems, date).start())
+    blend_ref[...] = jnp.zeros_like(blend_ref)
+    rate[...] = jnp.zeros_like(rate)
+    loads[...] = jnp.zeros_like(loads)
+    flows = flows_ref[...]
+    member = member_rows(flows, knot_count, net_ref.shape[0])
+    flows = flows[:, :knot_count]
+    cross_ref[...] = folded(contract(stack(feat_sum_ref[...]), flows, 1, 1), dates)
+
+    def one(date):
+        _, horizon, loading = date_rows(date, knot_count)
+        factor = loading * jnp.exp(-MEAN_REV * STEP_YEARS * (date + 1).astype(F32))
+        row = pl.ds(date, 1)
+        slope = slope_of(values_ref[date], mean_ref[row, :], base_ref[row, :], weight_ref[row, :])
+        adjoint = (slope - sums_ref[row, :] / paths).astype(BF16)
+        copy_of(exact_hbm, exact_buf, sems, date).wait()
+        exact = exact_buf[date]
+        product = contract(adjoint, net_ref[...], 1, 0) * exact
+        blend_ref[...] += factor * product
+        rate[...] += horizon * jnp.sum(product.reshape(-1, 8, knot_count), axis=0)
+        loads[...] += contract(adjoint, exact.astype(BF16), 0, 0)
+
+    each(dates, one)
+    shares = jnp.zeros(member.shape, F32)
+    for part in split(loads[...], 3):
+        shares = shares + contract(flows, part, 1, 1)
+    trades_ref[...] = jnp.sum(jnp.where(member, shares, 0.0).T, axis=0, keepdims=True)
+    rate_ref[...] = jnp.sum(rate[...], axis=0, keepdims=True)
 
 
 def finish_kernel(
@@ -209,11 +237,9 @@
     gap = sums_ref[...] / local - jnp.sum(arrived_ref[...], axis=0) / paths
     flows = flows_ref[...]
     member = member_rows(flows, knot_count, sets).astype(BF16)
-    spread = jnp.zeros(cross_ref.shape, F32)
-    adjoint = jnp.zeros(shift_ref.shape, F32)
-    for part in split(gap, 3):
-        spread = spread + contract(part, member, 1, 1)
-        adjoint = adjoint + contract(part, net_ref[...], 1, 0)
+    terms = stack(gap)
+    spread = folded(contract(terms, member, 1, 1), gap.shape[0])
+    adjoint = folded(contract(terms, net_ref[...], 1, 0), gap.shape[0])
     total = rate_ref[...]
     for date in range(shift_ref.shape[0]):
         row = slice(date, date + 1)
@@ -227,36 +253,44 @@
     out_ref[...] = jnp.broadcast_to(row[None], out_ref.shape)
 
 
-def start_kernel(blend_ref, shift_ref, exact_ref, load_ref, later_ref, out_ref, blend):
-    date = pl.program_id(0)
+def start_kernel(blend_ref, shift_ref, load_ref, later_ref, exact_hbm, out_ref, exact_buf, sems, blend):
     dates = shift_ref.shape[0]
-
-    @pl.when(date == 0)
-    def _():
-        blend[...] = blend_ref[...]
-
-    blend[...] += shift_ref[pl.ds(date, 1), :] * exact_ref[0]
-
-    @pl.when(date == dates - 1)
-    def _():
-        carried = contract(load_ref[...], blend[...], 1, 1, HIGHEST)
-        out_ref[...] = math.exp(-MEAN_REV * STEP_YEARS * dates) * later_ref[...] - carried
-
-
-def final_kernel(index_ref, arrived_ref, jac_ref, knot_ref, alloc_ref):
-    knot_count = jac_ref.shape[0]
+    each(dates, lambda date: copy_of(exact_hbm, exact_buf, sems, date).start())
+    blend[...] = blend_ref[...]
+
+    def one(date):
+        copy_of(exact_hbm, exact_buf, sems, date).wait()
+        blend[...] += shift_ref[pl.ds(date, 1), :] * exact_buf[date]
+
+    each(dates, one)
+    carried = contract(load_ref[...], blend[...], 1, 1, HIGHEST)
+    out_ref[...] = math.exp(-MEAN_REV * STEP_YEARS * dates) * later_ref[...] - carried
+
+
+def final_kernel(index_ref, arrived_ref, jac_hbm, knot_ref, alloc_ref, jac_buf, sems, column, total):
+    blocks, rows, knot_count = jac_hbm.shape
+    each(blocks, lambda block: copy_of(jac_hbm, jac_buf, sems, block).start())
+    row = jnp.sum(arrived_ref[...], axis=0)
     trades = alloc_ref.shape[1]
-    row = jnp.sum(arrived_ref[...], axis=0)
     parts = row[:, round_up(knot_count, LANES) :]
-    total = parts.shape[1]
-    parts = jnp.broadcast_to(parts, (8, total))
+    count = parts.shape[1]
     offset = index_ref[0] * trades
-    alloc_ref[...] = pltpu.roll(parts, lax.rem(total - offset, total), 1)[0:1, :trades]
-    column = jnp.broadcast_to(row[:, :knot_count], (LANES, knot_count)).T
-    for first in range(0, knot_count, LANES):
-        size = min(LANES, knot_count - first)
-        cut = slice(first, first + size)
-        knot_ref[:, cut] = jnp.sum(jac_ref[:, cut] * column[:, :size], axis=0, keepdims=True)
+    parts = jnp.broadcast_to(parts, (8, count))
+    alloc_ref[...] = pltpu.roll(parts, lax.rem(count - offset, count), 1)[0:1, :trades]
+    column[...] = jnp.broadcast_to(row[:, :knot_count], (LANES, knot_count)).T
+    total[...] = jnp.zeros_like(total)
+
+    def one(block):
+        copy_of(jac_hbm, jac_buf, sems, block).wait()
+        part = column[pl.ds(pl.multiple_of(block * rows, rows), rows), :]
+        for first in range(0, knot_count, LANES):
+            size = min(LANES, knot_count - first)
+            cut = slice(first, first + size)
+            scaled = jac_buf[block, :, cut] * part[:, :size]
+            total[:, cut] += jnp.sum(scaled.reshape(-1, total.shape[0], size), axis=0)
+
+    each(blocks, one)
+    knot_ref[...] = jnp.sum(total[...], axis=0, keepdims=True)
 
 
 VMEM = pl.BlockSpec(memory_space=pltpu.VMEM)
@@ -274,32 +308,28 @@
     return lead * round_up(rows, 8) * round_up(array.shape[-1], LANES) * size
 
 
-def run(name, kernel, out_shape, operands, scalars=0, dates=0, dated=(), scratch=(), flops=0, spare=8 << 20):
+def run(name, kernel, out_shape, operands, scalars=0, hbm=(), scratch=(), copies=(), flops=0, grant=0):
     arrays = list(operands) + list(out_shape)
-    room = sum(held(array) for array in scratch) + spare
+    room = sum(held(array) for array in scratch) + (8 << 20)
     specs = []
     for place, array in enumerate(arrays):
         if place < scalars:
             specs.append(SMEM)
-        elif not dates:
+        elif place in hbm:
+            specs.append(pl.BlockSpec(memory_space=pltpu.HBM))
+        else:
             specs.append(VMEM)
             room += held(array)
-        elif place in dated:
-            tail = array.shape[1:]
-            specs.append(pl.BlockSpec((1,) + tail, lambda date, n=len(tail): (date,) + (0,) * n))
-            room += 2 * held(array) // dates
-        else:
-            specs.append(pl.BlockSpec(array.shape, lambda date, n=len(array.shape): (0,) * n))
-            room += 2 * held(array)
     moved = sum(held(array) for array in arrays)
     return pl.pallas_call(
         kernel,
         out_shape=tuple(out_shape),
-        grid=(dates,) if dates else (),
         in_specs=specs[: len(operands)],
         out_specs=tuple(specs[len(operands) :]),
-        scratch_shapes=[pltpu.VMEM(array.shape, array.dtype) for array in scratch],
-        compiler_params=pltpu.CompilerParams(vmem_limit_bytes=min(room, 60 << 20)),
+        scratch_shapes=[pltpu.VMEM(array.shape, array.dtype) for array in scratch[: len(copies)]]
+        + [pltpu.SemaphoreType.DMA((count,)) for count in copies]
+        + [pltpu.VMEM(array.shape, array.dtype) for array in scratch[len(copies) :]],
+        compiler_params=pltpu.CompilerParams(vmem_limit_bytes=grant or room),
         cost_estimate=pl.CostEstimate(flops=flops, bytes_accessed=moved, transcendentals=0),
         name=name,
     )(*operands)
@@ -339,6 +369,7 @@
         [shaped((shards, trades, width), BF16)],
         [trade_end, trade_set.reshape(trades), cashflows],
         scalars=2,
+        grant=LARGE,
     )
     arrived = exchange(copies)
 
@@ -348,6 +379,7 @@
         [shaped((1, knot_count)), set_rows],
         [knots.reshape(1, knot_count), spline_jac, set_cpty.reshape(1, sets), default_prob],
         flops=2 * knot_count**2,
+        grant=LARGE,
     )
     exact, features, exact_sums, feat_sums = run(
         "features",
@@ -360,10 +392,16 @@
         ],
         [vol, normals, start_state, factor_load, zero_rate],
         scalars=1,
-        dates=dates,
-        dated=(1, 5, 6),
-        scratch=[shaped((factors, paths)), shaped((6 * factors, knot_count), BF16)],
+        hbm=(5, 6),
+        scratch=[
+            shaped((dates, paths, knot_count)),
+            shaped((dates, paths, knot_count), BF16),
+            shaped((factors, paths)),
+            shaped((6 * factors, knot_count), BF16),
+        ],
+        copies=(dates, dates),
         flops=6 * factors * work,
+        grant=MIDDLE,
     )
 
     flows = arrived.reshape(all_trades, width)
@@ -380,9 +418,11 @@
         value_kernel,
         [shaped((dates, paths, sets)), shaped((sets, knot_count), BF16)],
         [flows, net_columns, features],
-        dates=dates,
-        dated=(2, 3),
+        hbm=(2,),
+        scratch=[shaped((dates, paths, knot_count), BF16)],
+        copies=(dates,),
         flops=sets * work,
+        grant=MIDDLE,
     )
     mean, slope_sums, copies = run(
         "slopes",
@@ -401,11 +441,16 @@
             shaped((1, all_trades)),
             shaped((dates, all_trades)),
         ],
-        [mean, slope_sums, weight, base_value, feat_sums, values, exact, net_rows, flows],
-        dates=dates,
-        dated=(5, 6),
-        scratch=[shaped((8, knot_count)), shaped((sets, knot_count))],
+        [mean, slope_sums, weight, base_value, feat_sums, values, net_rows, flows, exact],
+        hbm=(8,),
+        scratch=[
+            shaped((dates, paths, knot_count)),
+            shaped((8, knot_count)),
+            shaped((sets, knot_count)),
+        ],
+        copies=(dates,),
         flops=2 * sets * work,
+        grant=MIDDLE,
     )
     row_width = round_up(knot_count, LANES) + all_trades
     shift, copies = run(
@@ -420,20 +465,30 @@
         "start",
         start_kernel,
         [shaped((factors, paths))],
-        [blend, shift, exact, factor_load, later_adjoint],
-        dates=dates,
-        dated=(2,),
-        scratch=[shaped((paths, knot_count))],
+        [blend, shift, factor_load, later_adjoint, exact],
+        hbm=(4,),
+        scratch=[shaped((dates, paths, knot_count)), shaped((paths, knot_count))],
+        copies=(dates,),
         flops=2 * factors * paths * knot_count,
-    )
+        grant=MIDDLE,
+    )
+    blocks = next(count for count in (8, 4, 2, 1) if knot_count % (8 * count) == 0)
     index = lax.axis_index("path").astype(jnp.int32).reshape(1)
     knot_grad, alloc = run(
         "final",
         final_kernel,
         [shaped((1, knot_count)), shaped((1, trades))],
-        [index, arrived, spline_jac],
+        [index, arrived, spline_jac.reshape(blocks, knot_count // blocks, knot_count)],
         scalars=1,
+        hbm=(2,),
+        scratch=[
+            shaped((blocks, knot_count // blocks, knot_count)),
+            shaped((knot_count, LANES)),
+            shaped((8, knot_count)),
+        ],
+        copies=(blocks,),
         flops=2 * knot_count**2,
+        grant=52 << 20,
     )
     return knot_grad.reshape(knot_count), alloc.reshape(trades), start_adjoint
 

time: 72.9 us -> 65.9 us (0.904)
  local copies, waits for them, and re-layouts: 22.5 us -> 0.71 us
  Pallas kernels: 21.5 us -> 31.5 us
  waiting for transfers between devices: 6.79 us -> 16.3 us
  starting transfers between devices: 20.6 us -> 16.1 us
    unnamed x38 -> x16, local copies, waits for them, and re-layouts: 22.5 us -> 0.71 us
    pallas_call x10, Pallas kernels: 21.5 us -> 31.5 us  [run(): pl.pallas_call(kernel, out_shape=tuple(out_shape), in_specs=specs[:len(op...]
    all_to_all x4, waiting for transfers between devices: 6.79 us -> 16.3 us  [exchange(): return lax.all_to_all(copies, 'path', 0, 0)]
    all_to_all x4, starting transfers between devices: 20.6 us -> 16.1 us  [exchange(): return lax.all_to_all(copies, 'path', 0, 0)]
  transfers between devices with their start and end apart: 4 -> 4, of which waited for: 4 -> 4; matrix products, arithmetic and copies ran while one was open for 0% -> 0% of each run, Pallas kernels for 21% -> 36%
where the time goes in v4:
time: 65.9 us; the launch traced here: 65.4 us
  Pallas kernels  31.5 us (48%)
  waiting for transfers between devices  16.3 us (25%)
  starting transfers between devices  16.1 us (24%)
  between operations  0.78 us (1%)
  local copies, waits for them, and re-layouts  0.71 us (1%)
    pallas_call x10, Pallas kernels, run(): pl.pallas_call(kernel, out_shape=tuple(out_shape), in_specs=specs[:len(op...  31.5 us
    all_to_all x4, waiting for transfers between devices, exchange(): return lax.all_to_all(copies, 'path', 0, 0)  16.3 us
    all_to_all x4, starting transfers between devices, exchange(): return lax.all_to_all(copies, 'path', 0, 0)  16.1 us
  transfers between devices with their start and end apart: 4, of which 4 were waited for; matrix products, arithmetic and copies ran while one was open for 0% of the time, Pallas kernels for 36%

profile of v4, /device:TPU:0, one launch (start us, length us, event | category | flops | bytes accessed | tf_op | source)
XLA Modules:
  0.0 65.4 jit_solution(11434887123686159599)
XLA Ops:
  0.7 1.7 %prep.1 = bf16[32,8,1024]{2,1,0:T(8,128)(2,1)} custom-call(s32[8]{0:T(128)} %end_ref.1, s32[8]{0:T(128)} %bitcast.15, bf16[8,960]{1,0:T(8,128)(2,1)} %cash_ref.1), custom_call_target="tpu_custom_call" | custom-call | bytes 548864 | tf_op jit(solution)/shard_map/prep/pallas_call | solution.py:324
  2.4 7.3 %all-to-all-start = ((bf16[32,8,1024]{2,1,0:T(8,128)(2,1)}), bf16[32,8,1024]{2,1,0:T(8,128)(2,1)S(1)}, u32[]{:S(2)}, u32[]{:S(2)}) async-start(bf16[32,8,1024]{2,1,0:T(8,128)(2,1)} %prep.1), calls=%async_computation | async-start | bytes 1048576 | tf_op jit(solution)/shard_map/all_to_all | solution.py:31
  9.7 3.2 %curve.1 = (f32[1,960]{1,0:T(1,128)}, f32[8,128]{1,0:T(8,128)}) custom-call(f32[1,960]{1,0:T(1,128)} %bitcast.13, f32[960,960]{1,0:T(8,128)} %jac_ref.1, s32[1,128]{1,0:T(1,128)} %bitcast.14, f32[8,64]{1,0:T(8,128)} %prob_ref.1), custom_call_target="tpu_custom_call" | custom-call | flops 1843200 | bytes 4009984 | tf_op jit(solution)/shard_map/curve/pallas_call | solution.py:324
  12.9 0.0 copy-done.7
  12.9 0.0 copy-done
  12.9 0.0 copy-start.6
  12.9 0.7 %copy-done.6 = f32[1,960]{1,0:T(1,128)S(1)} copy-done((f32[1,960]{1,0:T(1,128)S(1)}, f32[1,960]{1,0:T(1,128)}, u32[]{:S(2)}) %copy-start.6) | copy-done | bytes 3864
  13.6 6.1 %features.1 = (f32[8,256,960]{2,1,0:T(8,128)}, bf16[8,256,960]{2,1,0:T(8,128)(2,1)}, f32[8,960]{1,0:T(8,128)S(1)}, f32[8,960]{1,0:T(8,128)S(1)}) custom-call(f32[8]{0:T(128)S(1)} %copy-done.7, f32[8,32,256]{2,1,0:T(8,128)S(1)} %copy-done.4, f32[32,256]{1,0:T(8,128)S(1)} %copy-done.5, f32[32,960]{1,0:T(8,128)S(1)} %copy-done, f32[1,960]{1,0:T(1,128)S(1)} %copy-done.6), custom_call_target="tpu_custom_call" | custom-call | flops 754974720 | bytes 13111296 | tf_op jit(solution)/shard_map/features/pallas_call | solution.py:324
  19.8 5.6 %all-to-all-done = bf16[32,8,1024]{2,1,0:T(8,128)(2,1)S(1)} async-done(((bf16[32,8,1024]{2,1,0:T(8,128)(2,1)}), bf16[32,8,1024]{2,1,0:T(8,128)(2,1)S(1)}, u32[]{:S(2)}, u32[]{:S(2)}) %all-to-all-start) | async-done | bytes 524320 | tf_op jit(solution)/shard_map/all_to_all | solution.py:31
  25.3 1.3 %net.1 = (bf16[960,128]{1,0:T(8,128)(2,1)S(1)}, f32[32,8,128]{2,1,0:T(8,128)}) custom-call(bf16[256,1024]{1,0:T(8,128)(2,1)S(1)} %bitcast.8, f32[8,960]{1,0:T(8,128)S(1)} %get-tuple-element.25.feat_sum_ref), custom_call_target="tpu_custom_call" | custom-call | flops 62914560 | bytes 933888 | tf_op jit(solution)/shard_map/net/pallas_call | solution.py:324
  26.7 3.0 %all-to-all-start.1 = ((f32[32,8,128]{2,1,0:T(8,128)}), f32[32,8,128]{2,1,0:T(8,128)S(1)}, u32[]{:S(2)}, u32[]{:S(2)}) async-start(f32[32,8,128]{2,1,0:T(8,128)} %get-tuple-element.26), calls=%async_computation.1 | async-start | bytes 262144 | tf_op jit(solution)/shard_map/all_to_all | solution.py:31
  29.7 3.4 %values.1 = (f32[8,256,128]{2,1,0:T(8,128)S(1)}, bf16[128,960]{1,0:T(8,128)(2,1)S(1)}) custom-call(bf16[256,1024]{1,0:T(8,128)(2,1)S(1)} %bitcast.9, bf16[960,128]{1,0:T(8,128)(2,1)S(1)} %get-tuple-element.27.net_ref, bf16[8,256,960]{2,1,0:T(8,128)(2,1)} %get-tuple-element.28.feat_hbm), custom_call_target="tpu_custom_call" | custom-call | flops 503316480 | bytes 6275072 | tf_op jit(solution)/shard_map/values/pallas_call | solution.py:324
  33.1 4.8 %all-to-all-done.1.arrived_ref = f32[32,8,128]{2,1,0:T(8,128)S(1)} async-done(((f32[32,8,128]{2,1,0:T(8,128)}), f32[32,8,128]{2,1,0:T(8,128)S(1)}, u32[]{:S(2)}, u32[]{:S(2)}) %all-to-all-start.1) | async-done | bytes 131104 | tf_op jit(solution)/shard_map/all_to_all | solution.py:31
  37.9 0.0 copy-done.3
  37.9 1.0 %slopes.1 = (f32[8,128]{1,0:T(8,128)S(1)}, f32[8,128]{1,0:T(8,128)S(1)}, f32[32,8,128]{2,1,0:T(8,128)}) custom-call(f32[32,8,128]{2,1,0:T(8,128)S(1)} %all-to-all-done.1.arrived_ref, f32[8,256,128]{2,1,0:T(8,128)S(1)} %get-tuple-element.29.values_ref, f32[8,128]{1,0:T(8,128)S(1)} %copy-done.3, f32[8,128]{1,0:T(8,128)S(1)} %copy-done.2), custom_call_target="tpu_custom_call" | custom-call | flops 4194304 | bytes 1327104 | tf_op jit(solution)/shard_map/slopes/pallas_call | solution.py:324
  38.8 2.6 %all-to-all-start.2 = ((f32[32,8,128]{2,1,0:T(8,128)}), f32[32,8,128]{2,1,0:T(8,128)S(1)}, u32[]{:S(2)}, u32[]{:S(2)}) async-start(f32[32,8,128]{2,1,0:T(8,128)} %get-tuple-element.31), calls=%async_computation.2 | async-start | bytes 262144 | tf_op jit(solution)/shard_map/all_to_all | solution.py:31
  41.4 0.0 copy-start.1
  41.4 5.6 %adjoint.1 = (f32[256,960]{1,0:T(8,128)S(1)}, f32[1,960]{1,0:T(1,128)S(1)}, f32[1,256]{1,0:T(1,128)S(1)}, f32[8,256]{1,0:T(8,128)S(1)}) custom-call(f32[8,128]{1,0:T(8,128)S(1)} %get-tuple-element.35.mean_ref, f32[8,128]{1,0:T(8,128)S(1)} %get-tuple-element.32.sums_ref, f32[8,128]{1,0:T(8,128)S(1)} %copy-done.3, f32[8,128]{1,0:T(8,128)S(1)} %copy-done.2, ...), custom_call_target="tpu_custom_call" | custom-call | flops 1006632960 | bytes 11370496 | tf_op jit(solution)/shard_map/adjoint/pallas_call | solution.py:324
  47.0 2.6 %all-to-all-done.2.arrived_ref = f32[32,8,128]{2,1,0:T(8,128)S(1)} async-done(((f32[32,8,128]{2,1,0:T(8,128)}), f32[32,8,128]{2,1,0:T(8,128)S(1)}, u32[]{:S(2)}, u32[]{:S(2)}) %all-to-all-start.2) | async-done | bytes 131104 | tf_op jit(solution)/shard_map/all_to_all | solution.py:31
  49.6 1.1 %finish.1 = (f32[8,960]{1,0:T(8,128)S(1)}, f32[32,1,1280]{2,1,0:T(1,128)}) custom-call(f32[32,8,128]{2,1,0:T(8,128)S(1)} %all-to-all-done.2.arrived_ref, f32[8,128]{1,0:T(8,128)S(1)} %get-tuple-element.32.sums_ref, f32[8,960]{1,0:T(8,128)S(1)} %get-tuple-element.33.exact_sum_ref, bf16[128,960]{1,0:T(8,128)(2,1)S(1)} %get-tuple-element.34.net_ref, ...), custom_call_target="tpu_custom_call" | custom-call | flops 5898240 | bytes 2347008 | tf_op jit(solution)/shard_map/finish/pallas_call | solution.py:324
  50.7 3.3 %all-to-all-start.3 = ((f32[32,1,1280]{2,1,0:T(1,128)}), f32[32,1,1280]{2,1,0:T(1,128)S(1)}, u32[]{:S(2)}, u32[]{:S(2)}) async-start(f32[32,1,1280]{2,1,0:T(1,128)} %get-tuple-element.40), calls=%async_computation.3 | async-start | bytes 327680 | tf_op jit(solution)/shard_map/all_to_all | solution.py:31
  54.0 5.2 %start.1 = f32[32,256]{1,0:T(8,128)} custom-call(f32[256,960]{1,0:T(8,128)S(1)} %get-tuple-element.43.blend_ref, f32[8,960]{1,0:T(8,128)S(1)} %get-tuple-element.44.shift_ref, f32[32,960]{1,0:T(8,128)S(1)} %copy-done, f32[32,256]{1,0:T(8,128)S(1)} %copy-done.1, f32[8,256,960]{2,1,0:T(8,128)} %get-tuple-element.36.exact_hbm), custom_call_target="tpu_custom_call" | custom-call | flops 15728640 | bytes 9666560 | tf_op jit(solution)/shard_map/start/pallas_call | solution.py:324
  59.2 3.4 %all-to-all-done.3.arrived_ref = f32[32,1,1280]{2,1,0:T(1,128)S(1)} async-done(((f32[32,1,1280]{2,1,0:T(1,128)}), f32[32,1,1280]{2,1,0:T(1,128)S(1)}, u32[]{:S(2)}, u32[]{:S(2)}) %all-to-all-start.3) | async-done | bytes 163872 | tf_op jit(solution)/shard_map/all_to_all | solution.py:31
  62.6 2.8 %final.1 = (f32[1,960]{1,0:T(1,128)}, f32[1,8]{1,0:T(1,128)}) custom-call(s32[1]{0:T(128)} %bitcast.index_ref, f32[32,1,1280]{2,1,0:T(1,128)S(1)} %all-to-all-done.3.arrived_ref, f32[8,120,960]{2,1,0:T(8,128)} %bitcast.12), custom_call_target="tpu_custom_call" | custom-call | flops 1843200 | bytes 5283840 | tf_op jit(solution)/shard_map/final/pallas_call | solution.py:324
  (10 shorter events, 0.0 us)
Async XLA Ops:
  0.6 12.3 %copy-start.4 = (f32[8,32,256]{2,1,0:T(8,128)S(1)}, f32[8,32,256]{2,1,0:T(8,128)}, u32[]{:S(2)}) copy-start(f32[8,32,256]{2,1,0:T(8,128)} %normals_ref.1) | copy-start | bytes 786436
  0.6 12.3 %copy-start.5 = (f32[32,256]{1,0:T(8,128)S(1)}, f32[32,256]{1,0:T(8,128)}, u32[]{:S(2)}) copy-start(f32[32,256]{1,0:T(8,128)} %start_ref.1) | copy-start | bytes 98308
  0.7 12.3 %copy-start.7 = (f32[8]{0:T(128)S(1)}, f32[8]{0:T(128)}, u32[]{:S(2)}) copy-start(f32[8]{0:T(128)} %vol_ref.1) | copy-start | bytes 100
  0.7 12.3 %copy-start = (f32[32,960]{1,0:T(8,128)S(1)}, f32[32,960]{1,0:T(8,128)}, u32[]{:S(2)}) copy-start(f32[32,960]{1,0:T(8,128)} %load_ref.3) | copy-start | bytes 368644
  2.4 22.9 %all-to-all-start = ((bf16[32,8,1024]{2,1,0:T(8,128)(2,1)}), bf16[32,8,1024]{2,1,0:T(8,128)(2,1)S(1)}, u32[]{:S(2)}, u32[]{:S(2)}) async-start(bf16[32,8,1024]{2,1,0:T(8,128)(2,1)} %prep.1), calls=%async_computation | async-start | bytes 1048576 | tf_op jit(solution)/shard_map/all_to_all | solution.py:31
  12.9 0.7 %copy-start.6 = (f32[1,960]{1,0:T(1,128)S(1)}, f32[1,960]{1,0:T(1,128)}, u32[]{:S(2)}) copy-start(f32[1,960]{1,0:T(1,128)} %get-tuple-element.24.rate_ref) | copy-start | bytes 11524
  13.6 24.3 %copy-start.2 = (f32[8,128]{1,0:T(8,128)S(1)}, f32[8,128]{1,0:T(8,128)}, u32[]{:S(2)}) copy-start(f32[8,128]{1,0:T(8,128)} %base_ref.3) | copy-start | bytes 12292
  13.6 24.3 %copy-start.3 = (f32[8,128]{1,0:T(8,128)S(1)}, f32[8,128]{1,0:T(8,128)}, u32[]{:S(2)}) copy-start(f32[8,128]{1,0:T(8,128)} %get-tuple-element.30.weight_ref) | copy-start | bytes 12292
  26.7 11.2 %all-to-all-start.1 = ((f32[32,8,128]{2,1,0:T(8,128)}), f32[32,8,128]{2,1,0:T(8,128)S(1)}, u32[]{:S(2)}, u32[]{:S(2)}) async-start(f32[32,8,128]{2,1,0:T(8,128)} %get-tuple-element.26), calls=%async_computation.1 | async-start | bytes 262144 | tf_op jit(solution)/shard_map/all_to_all | solution.py:31
  38.8 10.8 %all-to-all-start.2 = ((f32[32,8,128]{2,1,0:T(8,128)}), f32[32,8,128]{2,1,0:T(8,128)S(1)}, u32[]{:S(2)}, u32[]{:S(2)}) async-start(f32[32,8,128]{2,1,0:T(8,128)} %get-tuple-element.31), calls=%async_computation.2 | async-start | bytes 262144 | tf_op jit(solution)/shard_map/all_to_all | solution.py:31
  41.4 12.6 %copy-start.1 = (f32[32,256]{1,0:T(8,128)S(1)}, f32[32,256]{1,0:T(8,128)}, u32[]{:S(2)}) copy-start(f32[32,256]{1,0:T(8,128)} %later_ref.1) | copy-start | bytes 98308
  50.7 11.9 %all-to-all-start.3 = ((f32[32,1,1280]{2,1,0:T(1,128)}), f32[32,1,1280]{2,1,0:T(1,128)S(1)}, u32[]{:S(2)}, u32[]{:S(2)}) async-start(f32[32,1,1280]{2,1,0:T(1,128)} %get-tuple-element.40), calls=%async_computation.3 | async-start | bytes 327680 | tf_op jit(solution)/shard_map/all_to_all | solution.py:31

commit v5 on v4

--- a/solution.py
+++ b/solution.py
@@ -17,6 +17,7 @@
 LANES = 128
 LARGE = 58 << 20
 MIDDLE = 50 << 20
+LOG2E = math.log2(math.e)
 DECAY = math.exp(-MEAN_REV * STEP_YEARS)
 HIGHEST = lax.Precision.HIGHEST
 F32 = jnp.float32
@@ -27,8 +28,8 @@
     return -(-size // step) * step
 
 
-def exchange(copies):
-    return lax.all_to_all(copies, "path", 0, 0)
+def exchange(copies, groups=None):
+    return lax.all_to_all(copies, "path", 0, 0, axis_index_groups=groups)
 
 
 def split(value, terms):
@@ -61,12 +62,13 @@
     return jnp.concatenate(split(value, 3), axis=0)
 
 
-def each(count, body):
+def each(count, body, group=1):
     def step(index, carry):
-        body(index)
+        for offset in range(group):
+            body(index * group + offset)
         return carry
 
-    lax.fori_loop(0, count, step, 0)
+    lax.fori_loop(0, count // group, step, 0)
 
 
 def copy_of(source, target, sems, index):
@@ -112,25 +114,43 @@
         out_ref[shard] = flows
 
 
-def curve_kernel(knots_ref, jac_ref, cpty_ref, prob_ref, rate_ref, weight_ref):
-    knot_count = jac_ref.shape[0]
-    column = jnp.sum(jac_ref[...] * knots_ref[...], axis=1, keepdims=True)
-    rate_ref[...] = jnp.broadcast_to(column, (knot_count, LANES)).T[0:1]
-    labels = lax.broadcasted_iota(jnp.int32, (prob_ref.shape[1], cpty_ref.shape[1]), 0)
-    chosen = (cpty_ref[...] == labels).astype(F32)
-    weight_ref[...] = LOSS_RATE * contract(prob_ref[...], chosen, 1, 0, HIGHEST)
-
-
 def feature_kernel(
-    vol_ref, normals_ref, start_ref, load_ref, rate_ref,
-    exact_hbm, feat_hbm, exact_sum_ref, feat_sum_ref,
-    exact_buf, feat_buf, exact_sems, feat_sems, state, stacked,
+    vol_hbm, normals_hbm, start_hbm, load_hbm, knots_hbm, jac_hbm,
+    exact_hbm, feat_sum_ref,
+    exact_buf, jac_buf, exact_sems, jac_sems, sems, normals_ref, state, load_ref, knots_ref, stacked, column, rate_ref, vol_ref,
 ):
     dates = normals_ref.shape[0]
-    knot_count = load_ref.shape[1]
-    state[...] = start_ref[...]
+    blocks, rows, knot_count = jac_hbm.shape
+    inputs = [
+        pltpu.make_async_copy(source, target, sems.at[place])
+        for place, (source, target) in enumerate(
+            ((load_hbm, load_ref), (knots_hbm, knots_ref), (start_hbm, state), (normals_hbm, normals_ref), (vol_hbm, vol_ref))
+        )
+    ]
+    for copy in inputs:
+        copy.start()
+    each(blocks, lambda block: copy_of(jac_hbm, jac_buf, jac_sems, block).start())
+    inputs[0].wait()
     high, middle, low = split(load_ref[...], 3)
     stacked[...] = jnp.concatenate([high, middle, high, middle, low, high], axis=0)
+    for copy in inputs[1:]:
+        copy.wait()
+
+    parts = exact_sems.shape[0] // dates
+    size = exact_buf.shape[1] // parts
+
+    def sent(date, part):
+        cut = pl.ds(part * size, size)
+        sem = exact_sems.at[date * parts + part]
+        return pltpu.make_async_copy(exact_buf.at[date, cut], exact_hbm.at[date, cut], sem)
+
+    def zero_rates(block):
+        copy_of(jac_hbm, jac_buf, jac_sems, block).wait()
+        sums = jnp.sum(jac_buf[block] * knots_ref[...], axis=1, keepdims=True)
+        column[pl.ds(pl.multiple_of(block * rows, rows), rows), :] = jnp.broadcast_to(sums, (rows, LANES))
+
+    each(blocks, zero_rates)
+    rate_ref[...] = column[...].T[0:1]
 
     def one(date):
         now = DECAY * state[...] + vol_ref[date] * normals_ref[date]
@@ -140,42 +160,58 @@
         alive, horizon, loading = date_rows(date, knot_count)
         discount = jnp.where(alive, jnp.exp(-rate_ref[...] * horizon), 0.0)
         shift = contract(terms, stacked[...], 0, 0)
-        exact = discount * jnp.exp(-loading * shift)
+        exact = discount * jnp.exp2((-LOG2E * loading) * shift)
         exact_buf[date] = exact
-        rounded = exact.astype(BF16)
-        feat_buf[date] = rounded
-        copy_of(exact_buf, exact_hbm, exact_sems, date).start()
-        copy_of(feat_buf, feat_hbm, feat_sems, date).start()
+        for part in range(parts):
+            sent(date, part).start()
         row = pl.ds(date, 1)
-        exact_sum_ref[row, :] = jnp.sum(exact, axis=0, keepdims=True)
-        feat_sum_ref[row, :] = jnp.sum(rounded.astype(F32), axis=0, keepdims=True)
-
-    each(dates, one)
-    each(dates, lambda date: copy_of(exact_buf, exact_hbm, exact_sems, date).wait())
-    each(dates, lambda date: copy_of(feat_buf, feat_hbm, feat_sems, date).wait())
-
-
-def net_kernel(flows_ref, feat_sum_ref, net_ref, out_ref):
+        ones = jnp.ones((8, exact.shape[0]), BF16)
+        feat_sum_ref[row, :] = contract(ones, exact.astype(BF16), 1, 0)[0:1]
+
+    each(dates, one, 8)
+    for part in range(parts):
+        each(dates, lambda date, part=part: sent(date, part).wait())
+
+
+def half_kernel(own_ref, feat_sum_ref, half_ref, terms_ref):
+    knot_count, sets = half_ref.shape
+    flows = own_ref[...]
+    member = member_rows(flows, knot_count, sets).astype(BF16)
+    half_ref[...] = contract(flows[:, :knot_count], member, 0, 0)
+    terms_ref[...] = stack(feat_sum_ref[...])
+
+
+def net_kernel(own_ref, other_ref, half_ref, terms_ref, flows_ref, net_ref, out_ref):
     knot_count, sets = net_ref.shape
-    flows = flows_ref[...]
+    flows_ref[...] = jnp.concatenate([own_ref[...], other_ref[...]], axis=0)
+    flows = other_ref[...]
     member = member_rows(flows, knot_count, sets).astype(BF16)
-    net = contract(flows[:, :knot_count], member, 0, 0).astype(BF16)
+    net = (half_ref[...] + contract(flows[:, :knot_count], member, 0, 0)).astype(BF16)
     net_ref[...] = net
-    sums = folded(contract(stack(feat_sum_ref[...]), net, 1, 0), out_ref.shape[1])
+    sums = folded(contract(terms_ref[...], net, 1, 0), out_ref.shape[1])
     out_ref[...] = jnp.broadcast_to(sums[None], out_ref.shape)
 
 
-def value_kernel(flows_ref, net_ref, feat_hbm, values_ref, rows_ref, feat_buf, sems):
+def value_kernel(
+    flows_ref, net_ref, cpty_ref, prob_ref, exact_hbm, values_ref, rows_ref, weight_ref, exact_buf, sems
+):
     dates = values_ref.shape[0]
-    each(dates, lambda date: copy_of(feat_hbm, feat_buf, sems, date).start())
+    each(dates, lambda date: copy_of(exact_hbm, exact_buf, sems, date).start())
+    labels = lax.broadcasted_iota(jnp.int32, (prob_ref.shape[1], cpty_ref.shape[1]), 0)
+    chosen = (cpty_ref[...] == labels).astype(F32)
+    weight_ref[...] = LOSS_RATE * contract(prob_ref[...], chosen, 1, 0, HIGHEST)
     sets, knot_count = rows_ref.shape
-    flows = flows_ref[...]
-    member = member_rows(flows, knot_count, sets).astype(BF16)
-    rows_ref[...] = contract(member, flows[:, :knot_count], 0, 0).astype(BF16)
+    half = flows_ref.shape[0] // 2
+    rows = []
+    for first in (0, half):
+        flows = flows_ref[first : first + half, :]
+        member = member_rows(flows, knot_count, sets).astype(BF16)
+        rows.append(contract(member, flows[:, :knot_count], 0, 0))
+    rows_ref[...] = (rows[0] + rows[1]).astype(BF16)
 
     def one(date):
-        copy_of(feat_hbm, feat_buf, sems, date).wait()
-        values_ref[date] = contract(feat_buf[date], net_ref[...], 1, 0)
+        copy_of(exact_hbm, exact_buf, sems, date).wait()
+        values_ref[date] = contract(exact_buf[date].astype(BF16), net_ref[...], 1, 0)
 
     each(dates, one)
 
@@ -230,7 +266,7 @@
 
 
 def finish_kernel(
-    paths, local, arrived_ref, sums_ref, exact_sum_ref, net_ref, flows_ref, rate_ref, trades_ref, cross_ref,
+    paths, local, parity_ref, arrived_ref, sums_ref, feat_sum_ref, net_ref, flows_ref, rate_ref, trades_ref, cross_ref,
     shift_ref, out_ref,
 ):
     sets, knot_count = net_ref.shape
@@ -245,8 +281,10 @@
         row = slice(date, date + 1)
         _, horizon, loading = date_rows(jnp.int32(date), knot_count)
         shift_ref[row, :] = loading * math.exp(-MEAN_REV * STEP_YEARS * (date + 1)) * adjoint[row]
-        total = total + horizon * adjoint[row] * exact_sum_ref[row, :]
+        total = total + horizon * adjoint[row] * feat_sum_ref[row, :]
     trades = trades_ref[...] + jnp.sum(spread * cross_ref[...], axis=0, keepdims=True)
+    count = trades.shape[1]
+    trades = pltpu.roll(jnp.broadcast_to(trades, (8, count)), parity_ref[0] * (count // 2), 1)[0:1]
     shards, _, width = out_ref.shape
     pad = jnp.zeros((1, width - knot_count - trades.shape[1]), F32)
     row = jnp.concatenate([-total / paths, pad, trades / paths], axis=1)
@@ -274,7 +312,7 @@
     trades = alloc_ref.shape[1]
     parts = row[:, round_up(knot_count, LANES) :]
     count = parts.shape[1]
-    offset = index_ref[0] * trades
+    offset = index_ref[0]
     parts = jnp.broadcast_to(parts, (8, count))
     alloc_ref[...] = pltpu.roll(parts, lax.rem(count - offset, count), 1)[0:1, :trades]
     column[...] = jnp.broadcast_to(row[:, :knot_count], (LANES, knot_count)).T
@@ -308,7 +346,7 @@
     return lead * round_up(rows, 8) * round_up(array.shape[-1], LANES) * size
 
 
-def run(name, kernel, out_shape, operands, scalars=0, hbm=(), scratch=(), copies=(), flops=0, grant=0):
+def run(name, kernel, out_shape, operands, scalars=0, hbm=(), scratch=(), copies=(), buffers=1, smem=(), flops=0, grant=0):
     arrays = list(operands) + list(out_shape)
     room = sum(held(array) for array in scratch) + (8 << 20)
     specs = []
@@ -326,9 +364,10 @@
         out_shape=tuple(out_shape),
         in_specs=specs[: len(operands)],
         out_specs=tuple(specs[len(operands) :]),
-        scratch_shapes=[pltpu.VMEM(array.shape, array.dtype) for array in scratch[: len(copies)]]
+        scratch_shapes=[pltpu.VMEM(array.shape, array.dtype) for array in scratch[:buffers]]
         + [pltpu.SemaphoreType.DMA((count,)) for count in copies]
-        + [pltpu.VMEM(array.shape, array.dtype) for array in scratch[len(copies) :]],
+        + [pltpu.VMEM(array.shape, array.dtype) for array in scratch[buffers:]]
+        + [pltpu.SMEM(array.shape, array.dtype) for array in smem],
         compiler_params=pltpu.CompilerParams(vmem_limit_bytes=grant or room),
         cost_estimate=pl.CostEstimate(flops=flops, bytes_accessed=moved, transcendentals=0),
         name=name,
@@ -366,60 +405,67 @@
     (copies,) = run(
         "prep",
         prep_kernel,
-        [shaped((shards, trades, width), BF16)],
+        [shaped((shards // 2, trades, width), BF16)],
         [trade_end, trade_set.reshape(trades), cashflows],
         scalars=2,
         grant=LARGE,
     )
-    arrived = exchange(copies)
-
-    zero_rate, weight = run(
-        "curve",
-        curve_kernel,
-        [shaped((1, knot_count)), set_rows],
-        [knots.reshape(1, knot_count), spline_jac, set_cpty.reshape(1, sets), default_prob],
-        flops=2 * knot_count**2,
-        grant=LARGE,
-    )
-    exact, features, exact_sums, feat_sums = run(
+    own = exchange(copies, [list(range(side, shards, 2)) for side in range(2)])
+    own = own.reshape(all_trades // 2, width)
+    index = lax.axis_index("path").astype(jnp.int32)
+    parity = lax.rem(index, 2)
+    offset = parity * (all_trades // 2) + lax.div(index, 2) * trades
+    blocks = next(count for count in (8, 4, 2, 1) if knot_count % (8 * count) == 0)
+    jac_blocks = spline_jac.reshape(blocks, knot_count // blocks, knot_count)
+
+    exact, feat_sums = run(
         "features",
         feature_kernel,
-        [
-            shaped((dates, paths, knot_count)),
-            shaped((dates, paths, knot_count), BF16),
-            grid_rows,
-            grid_rows,
-        ],
-        [vol, normals, start_state, factor_load, zero_rate],
-        scalars=1,
-        hbm=(5, 6),
+        [shaped((dates, paths, knot_count)), grid_rows],
+        [vol, normals, start_state, factor_load, knots.reshape(1, knot_count), jac_blocks],
+        hbm=(0, 1, 2, 3, 4, 5, 6),
         scratch=[
             shaped((dates, paths, knot_count)),
-            shaped((dates, paths, knot_count), BF16),
-            shaped((factors, paths)),
+            shaped(jac_blocks.shape),
+            shaped(normals.shape),
+            shaped(start_state.shape),
+            shaped(factor_load.shape),
+            shaped((1, knot_count)),
             shaped((6 * factors, knot_count), BF16),
+            shaped((knot_count, LANES)),
+            shaped((1, knot_count)),
         ],
-        copies=(dates, dates),
+        buffers=2,
+        copies=(dates * (4 if paths % 64 == 0 else 1), blocks, 5),
+        smem=(shaped(vol.shape),),
         flops=6 * factors * work,
-        grant=MIDDLE,
-    )
-
-    flows = arrived.reshape(all_trades, width)
-    net_columns, copies = run(
+        grant=LARGE,
+    )
+
+    own, feat_sums = lax.optimization_barrier((own, feat_sums))
+    other = lax.ppermute(own, "path", [(shard, shard ^ 1) for shard in range(shards)])
+    half, terms = run(
+        "half",
+        half_kernel,
+        [shaped((knot_count, sets)), shaped((3 * dates, knot_count), BF16)],
+        [own, feat_sums],
+        flops=sets * all_trades * knot_count,
+    )
+    flows, net_columns, copies = run(
         "net",
         net_kernel,
-        [shaped((knot_count, sets), BF16), set_copies],
-        [flows, feat_sums],
-        flops=2 * sets * all_trades * knot_count,
+        [shaped((all_trades, width), BF16), shaped((knot_count, sets), BF16), set_copies],
+        [own, other, half, terms],
+        flops=sets * all_trades * knot_count,
     )
     arrived = exchange(copies)
-    values, net_rows = run(
+    values, net_rows, weight = run(
         "values",
         value_kernel,
-        [shaped((dates, paths, sets)), shaped((sets, knot_count), BF16)],
-        [flows, net_columns, features],
-        hbm=(2,),
-        scratch=[shaped((dates, paths, knot_count), BF16)],
+        [shaped((dates, paths, sets)), shaped((sets, knot_count), BF16), set_rows],
+        [flows, net_columns, set_cpty.reshape(1, sets), default_prob, exact],
+        hbm=(4,),
+        scratch=[shaped((dates, paths, knot_count))],
         copies=(dates,),
         flops=sets * work,
         grant=MIDDLE,
@@ -457,7 +503,8 @@
         "finish",
         functools.partial(finish_kernel, all_paths, paths),
         [grid_rows, shaped((shards, 1, row_width))],
-        [arrived, slope_sums, exact_sums, net_rows, flows, rate, trade_parts, cross],
+        [parity.reshape(1), arrived, slope_sums, feat_sums, net_rows, flows, rate, trade_parts, cross],
+        scalars=1,
         flops=6 * sets * dates * knot_count,
     )
     arrived = exchange(copies)
@@ -472,17 +519,15 @@
         flops=2 * factors * paths * knot_count,
         grant=MIDDLE,
     )
-    blocks = next(count for count in (8, 4, 2, 1) if knot_count % (8 * count) == 0)
-    index = lax.axis_index("path").astype(jnp.int32).reshape(1)
     knot_grad, alloc = run(
         "final",
         final_kernel,
         [shaped((1, knot_count)), shaped((1, trades))],
-        [index, arrived, spline_jac.reshape(blocks, knot_count // blocks, knot_count)],
+        [offset.reshape(1), arrived, jac_blocks],
         scalars=1,
         hbm=(2,),
         scratch=[
-            shaped((blocks, knot_count // blocks, knot_count)),
+            shaped(jac_blocks.shape),
             shaped((knot_count, LANES)),
             shaped((8, knot_count)),
         ],

time: 65.9 us -> 63 us (0.956)
  waiting for transfers between devices: 16.3 us -> 12 us
  Pallas kernels: 31.5 us -> 29.9 us
  starting transfers between devices: 16.1 us -> 17.6 us
  local copies, waits for them, and re-layouts: 0.71 us -> 2.12 us
    all_to_all x4, waiting for transfers between devices: 16.3 us -> 11.7 us  [exchange(): return lax.all_to_all(copies, 'path', 0, 0, axis_index_groups=groups)]
    pallas_call x10, Pallas kernels: 31.5 us -> 29.9 us  [run(): pl.pallas_call(kernel, out_shape=tuple(out_shape), in_specs=specs[:len(op...]
    all_to_all x4, starting transfers between devices: 16.1 us -> 17.6 us  [exchange(): return lax.all_to_all(copies, 'path', 0, 0, axis_index_groups=groups)]
    unnamed x16 -> x14, local copies, waits for them, and re-layouts: 0.71 us -> 2.12 us
  transfers between devices with their start and end apart: 4 -> 5, of which waited for: 4 -> 5; matrix products, arithmetic and copies ran while one was open for 0% -> 0% of each run, Pallas kernels for 36% -> 36%
where the time goes in v5:
time: 63 us; the launch traced here: 62.5 us
  Pallas kernels  29.9 us (47%)
  starting transfers between devices  17.6 us (28%)
  waiting for transfers between devices  12 us (19%)
  local copies, waits for them, and re-layouts  2.12 us (3%)
  between operations  0.77 us (1%)
    pallas_call x10, Pallas kernels, run(): pl.pallas_call(kernel, out_shape=tuple(out_shape), in_specs=specs[:len(op...  29.9 us
    all_to_all x4, starting transfers between devices, exchange(): return lax.all_to_all(copies, 'path', 0, 0, axis_index_groups=groups)  17.6 us
    all_to_all x4, waiting for transfers between devices, exchange(): return lax.all_to_all(copies, 'path', 0, 0, axis_index_groups=groups)  11.7 us
    unnamed x14, local copies, waits for them, and re-layouts  2.12 us
  transfers between devices with their start and end apart: 5, of which 5 were waited for; matrix products, arithmetic and copies ran while one was open for 0% of the time, Pallas kernels for 36%

profile of v5, /device:TPU:0, one launch (start us, length us, event | category | flops | bytes accessed | tf_op | source)
XLA Modules:
  0.0 62.5 jit_solution(11880239874351859576)
XLA Ops:
  0.6 1.6 %prep.1 = bf16[16,8,1024]{2,1,0:T(8,128)(2,1)} custom-call(s32[8]{0:T(128)} %end_ref.1, s32[8]{0:T(128)} %bitcast.16, bf16[8,960]{1,0:T(8,128)(2,1)} %cash_ref.1), custom_call_target="tpu_custom_call" | custom-call | bytes 286720 | tf_op jit(solution)/shard_map/prep/pallas_call | solution.py:362
  2.2 8.3 %all-to-all-start = ((bf16[16,8,1024]{2,1,0:T(8,128)(2,1)}), bf16[16,8,1024]{2,1,0:T(8,128)(2,1)S(1)}, u32[]{:S(2)}, u32[]{:S(2)}) async-start(bf16[16,8,1024]{2,1,0:T(8,128)(2,1)} %prep.1), calls=%async_computation | async-start | bytes 524288 | tf_op jit(solution)/shard_map/all_to_all | solution.py:32
  10.5 7.2 %features.1 = (f32[8,256,960]{2,1,0:T(8,128)}, f32[8,960]{1,0:T(8,128)}) custom-call(f32[8]{0:T(128)} %vol_hbm.1, f32[8,32,256]{2,1,0:T(8,128)} %normals_hbm.1, f32[32,256]{1,0:T(8,128)} %start_hbm.1, f32[32,960]{1,0:T(8,128)} %load_ref.1, f32[1,960]{1,0:T(1,128)} %bitcast.15, f32[8,120,960]{2,1,0:T(8,128)} %bitcast.13), custom_call_target="tpu_custom_call" | custom-call | flops 754974720 | bytes 12816384 | tf_op jit(solution)/shard_map/features/pallas_call | solution.py:362
  17.7 2.7 %all-to-all-done = bf16[16,8,1024]{2,1,0:T(8,128)(2,1)S(1)} async-done(((bf16[16,8,1024]{2,1,0:T(8,128)(2,1)}), bf16[16,8,1024]{2,1,0:T(8,128)(2,1)S(1)}, u32[]{:S(2)}, u32[]{:S(2)}) %all-to-all-start) | async-done | bytes 262176 | tf_op jit(solution)/shard_map/all_to_all | solution.py:32
  20.4 0.8 %copy-done.1 = f32[8,960]{1,0:T(8,128)S(1)} copy-done((f32[8,960]{1,0:T(8,128)S(1)}, f32[8,960]{1,0:T(8,128)}, u32[]{:S(2)}) %copy-start.1) | copy-done | bytes 30744
  21.2 0.4 half.1
  21.6 0.3 collective-permute-done.other_ref
  21.9 1.3 %net.1 = (bf16[256,1024]{1,0:T(8,128)(2,1)S(1)}, bf16[960,128]{1,0:T(8,128)(2,1)S(1)}, f32[32,8,128]{2,1,0:T(8,128)}) custom-call(bf16[128,1024]{1,0:T(8,128)(2,1)S(1)} %bitcast.11, bf16[128,1024]{1,0:T(8,128)(2,1)S(1)} %collective-permute-done.other_ref, f32[960,128]{1,0:T(8,128)S(1)} %get-tuple-element.29.half_ref, ...), custom_call_target="tpu_custom_call" | custom-call | flops 31457280 | bytes 1966080 | tf_op jit(solution)/shard_map/net/pallas_call | solution.py:362
  23.2 3.3 %all-to-all-start.1 = ((f32[32,8,128]{2,1,0:T(8,128)}), f32[32,8,128]{2,1,0:T(8,128)S(1)}, u32[]{:S(2)}, u32[]{:S(2)}) async-start(f32[32,8,128]{2,1,0:T(8,128)} %get-tuple-element.31), calls=%async_computation.1 | async-start | bytes 262144 | tf_op jit(solution)/shard_map/all_to_all | solution.py:32
  26.5 0.0 copy-start.5
  26.5 0.7 %copy-done.5 = f32[8,64]{1,0:T(8,128)S(1)} copy-done((f32[8,64]{1,0:T(8,128)S(1)}, f32[8,64]{1,0:T(8,128)}, u32[]{:S(2)}) %copy-start.5) | copy-done | bytes 2072
  27.2 0.7 %copy-done.6 = s32[128,1]{0,1:T(1,128)S(1)} copy-done((s32[128,1]{0,1:T(1,128)S(1)}, s32[128,1]{0,1:T(1,128)}, u32[]{:S(2)}) %copy-start.6) | copy-done | bytes 536
  27.8 3.8 %values.1 = (f32[8,256,128]{2,1,0:T(8,128)S(1)}, bf16[128,960]{1,0:T(8,128)(2,1)S(1)}, f32[8,128]{1,0:T(8,128)S(1)}) custom-call(bf16[256,1024]{1,0:T(8,128)(2,1)S(1)} %get-tuple-element.32.flows_ref, bf16[960,128]{1,0:T(8,128)(2,1)S(1)} %get-tuple-element.33.net_ref, s32[1,128]{1,0:T(1,128)S(1)} %bitcast.12, f32[8,64]{1,0:T(8,128)S(1)} %copy-done.5, ...), custom_call_target="tpu_custom_call" | custom-call | flops 503316480 | bytes 10481664 | tf_op jit(solution)/shard_map/values/pallas_call | solution.py:362
  31.6 0.0 copy-start
  31.6 3.1 %all-to-all-done.1.arrived_ref = f32[32,8,128]{2,1,0:T(8,128)S(1)} async-done(((f32[32,8,128]{2,1,0:T(8,128)}), f32[32,8,128]{2,1,0:T(8,128)S(1)}, u32[]{:S(2)}, u32[]{:S(2)}) %all-to-all-start.1) | async-done | bytes 131104 | tf_op jit(solution)/shard_map/all_to_all | solution.py:32
  34.7 1.0 %slopes.1 = (f32[8,128]{1,0:T(8,128)S(1)}, f32[8,128]{1,0:T(8,128)S(1)}, f32[32,8,128]{2,1,0:T(8,128)}) custom-call(f32[32,8,128]{2,1,0:T(8,128)S(1)} %all-to-all-done.1.arrived_ref, f32[8,256,128]{2,1,0:T(8,128)S(1)} %get-tuple-element.35.values_ref, f32[8,128]{1,0:T(8,128)S(1)} %get-tuple-element.36.weight_ref, f32[8,128]{1,0:T(8,128)S(1)} %copy-done.4), custom_call_target="tpu_custom_call" | custom-call | flops 4194304 | bytes 1327104 | tf_op jit(solution)/shard_map/slopes/pallas_call | solution.py:362
  35.7 2.8 %all-to-all-start.2 = ((f32[32,8,128]{2,1,0:T(8,128)}), f32[32,8,128]{2,1,0:T(8,128)S(1)}, u32[]{:S(2)}, u32[]{:S(2)}) async-start(f32[32,8,128]{2,1,0:T(8,128)} %get-tuple-element.37), calls=%async_computation.2 | async-start | bytes 262144 | tf_op jit(solution)/shard_map/all_to_all | solution.py:32
  38.5 5.6 %adjoint.1 = (f32[256,960]{1,0:T(8,128)S(1)}, f32[1,960]{1,0:T(1,128)S(1)}, f32[1,256]{1,0:T(1,128)S(1)}, f32[8,256]{1,0:T(8,128)S(1)}) custom-call(f32[8,128]{1,0:T(8,128)S(1)} %get-tuple-element.40.mean_ref, f32[8,128]{1,0:T(8,128)S(1)} %get-tuple-element.38.sums_ref, f32[8,128]{1,0:T(8,128)S(1)} %get-tuple-element.36.weight_ref, f32[8,128]{1,0:T(8,128)S(1)} %copy-done.4, ...), custom_call_target="tpu_custom_call" | custom-call | flops 1006632960 | bytes 11370496 | tf_op jit(solution)/shard_map/adjoint/pallas_call | solution.py:362
  44.0 2.6 %all-to-all-done.2.arrived_ref = f32[32,8,128]{2,1,0:T(8,128)S(1)} async-done(((f32[32,8,128]{2,1,0:T(8,128)}), f32[32,8,128]{2,1,0:T(8,128)S(1)}, u32[]{:S(2)}, u32[]{:S(2)}) %all-to-all-start.2) | async-done | bytes 131104 | tf_op jit(solution)/shard_map/all_to_all | solution.py:32
  46.7 1.1 %finish.1 = (f32[8,960]{1,0:T(8,128)S(1)}, f32[32,1,1280]{2,1,0:T(1,128)}) custom-call(s32[1]{0:T(128)} %bitcast.1.parity_ref, f32[32,8,128]{2,1,0:T(8,128)S(1)} %all-to-all-done.2.arrived_ref, f32[8,128]{1,0:T(8,128)S(1)} %get-tuple-element.38.sums_ref, f32[8,960]{1,0:T(8,128)S(1)} %copy-done.2, bf16[128,960]{1,0:T(8,128)(2,1)S(1)} %get-tuple-element.39.net_ref, ...), custom_call_target="tpu_custom_call" | custom-call | flops 5898240 | bytes 2351104 | tf_op jit(solution)/shard_map/finish/pallas_call | solution.py:362
  47.8 3.2 %all-to-all-start.3 = ((f32[32,1,1280]{2,1,0:T(1,128)}), f32[32,1,1280]{2,1,0:T(1,128)S(1)}, u32[]{:S(2)}, u32[]{:S(2)}) async-start(f32[32,1,1280]{2,1,0:T(1,128)} %get-tuple-element.44), calls=%async_computation.3 | async-start | bytes 327680 | tf_op jit(solution)/shard_map/all_to_all | solution.py:32
  51.1 5.3 %start.1 = f32[32,256]{1,0:T(8,128)} custom-call(f32[256,960]{1,0:T(8,128)S(1)} %get-tuple-element.47.blend_ref, f32[8,960]{1,0:T(8,128)S(1)} %get-tuple-element.48.shift_ref, f32[32,960]{1,0:T(8,128)S(1)} %copy-done, f32[32,256]{1,0:T(8,128)S(1)} %copy-done.3, f32[8,256,960]{2,1,0:T(8,128)} %get-tuple-element.34.exact_hbm), custom_call_target="tpu_custom_call" | custom-call | flops 15728640 | bytes 9666560 | tf_op jit(solution)/shard_map/start/pallas_call | solution.py:362
  56.4 3.3 %all-to-all-done.3.arrived_ref = f32[32,1,1280]{2,1,0:T(1,128)S(1)} async-done(((f32[32,1,1280]{2,1,0:T(1,128)}), f32[32,1,1280]{2,1,0:T(1,128)S(1)}, u32[]{:S(2)}, u32[]{:S(2)}) %all-to-all-start.3) | async-done | bytes 163872 | tf_op jit(solution)/shard_map/all_to_all | solution.py:32
  59.7 2.8 %final.1 = (f32[1,960]{1,0:T(1,128)}, f32[1,8]{1,0:T(1,128)}) custom-call(s32[1]{0:T(128)} %bitcast.index_ref, f32[32,1,1280]{2,1,0:T(1,128)S(1)} %all-to-all-done.3.arrived_ref, f32[8,120,960]{2,1,0:T(8,128)} %bitcast.14), custom_call_target="tpu_custom_call" | custom-call | flops 1843200 | bytes 5283840 | tf_op jit(solution)/shard_map/final/pallas_call | solution.py:362
  (10 shorter events, 0.0 us)
Async XLA Ops:
  0.6 34.1 %copy-start.4 = (f32[8,128]{1,0:T(8,128)S(1)}, f32[8,128]{1,0:T(8,128)}, u32[]{:S(2)}) copy-start(f32[8,128]{1,0:T(8,128)} %base_ref.3) | copy-start | bytes 12292
  2.2 18.2 %all-to-all-start = ((bf16[16,8,1024]{2,1,0:T(8,128)(2,1)}), bf16[16,8,1024]{2,1,0:T(8,128)(2,1)S(1)}, u32[]{:S(2)}, u32[]{:S(2)}) async-start(bf16[16,8,1024]{2,1,0:T(8,128)(2,1)} %prep.1), calls=%async_computation | async-start | bytes 524288 | tf_op jit(solution)/shard_map/all_to_all | solution.py:32
  20.4 1.5 %collective-permute-start = (bf16[128,1024]{1,0:T(8,128)(2,1)S(1)}, bf16[128,1024]{1,0:T(8,128)(2,1)S(1)}, u32[]{:S(2)}, u32[]{:S(2)}) collective-permute-start(bf16[128,1024]{1,0:T(8,128)(2,1)S(1)} %bitcast.9), channel_id=1, source_target_pairs={{0,1},{1,0},{2,3},{3,2},{4,5},{5,4},{6,7},{7,6},{8,9},{9,8},{10,11... | collective-permute-start | bytes 786440 | tf_op jit(solution)/shard_map/ppermute | solution.py:446
  20.4 0.8 %copy-start.1 = (f32[8,960]{1,0:T(8,128)S(1)}, f32[8,960]{1,0:T(8,128)}, u32[]{:S(2)}) copy-start(f32[8,960]{1,0:T(8,128)} %get-tuple-element.28.feat_sum_ref) | copy-start | bytes 92164
  21.2 17.3 %copy-start.2 = (f32[8,960]{1,0:T(8,128)S(1)}, f32[8,960]{1,0:T(8,128)}, u32[]{:S(2)}) copy-start(f32[8,960]{1,0:T(8,128)} %get-tuple-element.28.feat_sum_ref) | copy-start | bytes 92164
  23.2 11.5 %all-to-all-start.1 = ((f32[32,8,128]{2,1,0:T(8,128)}), f32[32,8,128]{2,1,0:T(8,128)S(1)}, u32[]{:S(2)}, u32[]{:S(2)}) async-start(f32[32,8,128]{2,1,0:T(8,128)} %get-tuple-element.31), calls=%async_computation.1 | async-start | bytes 262144 | tf_op jit(solution)/shard_map/all_to_all | solution.py:32
  26.5 0.7 %copy-start.5 = (f32[8,64]{1,0:T(8,128)S(1)}, f32[8,64]{1,0:T(8,128)}, u32[]{:S(2)}) copy-start(f32[8,64]{1,0:T(8,128)} %prob_ref.1) | copy-start | bytes 6148
  27.2 0.7 %copy-start.6 = (s32[128,1]{0,1:T(1,128)S(1)}, s32[128,1]{0,1:T(1,128)}, u32[]{:S(2)}) copy-start(s32[128,1]{0,1:T(1,128)} %param.23) | copy-start | bytes 1540
  31.6 19.4 %copy-start = (f32[32,960]{1,0:T(8,128)S(1)}, f32[32,960]{1,0:T(8,128)}, u32[]{:S(2)}) copy-start(f32[32,960]{1,0:T(8,128)} %load_ref.1) | copy-start | bytes 368644
  31.6 19.4 %copy-start.3 = (f32[32,256]{1,0:T(8,128)S(1)}, f32[32,256]{1,0:T(8,128)}, u32[]{:S(2)}) copy-start(f32[32,256]{1,0:T(8,128)} %later_ref.1) | copy-start | bytes 98308
  35.7 11.0 %all-to-all-start.2 = ((f32[32,8,128]{2,1,0:T(8,128)}), f32[32,8,128]{2,1,0:T(8,128)S(1)}, u32[]{:S(2)}, u32[]{:S(2)}) async-start(f32[32,8,128]{2,1,0:T(8,128)} %get-tuple-element.37), calls=%async_computation.2 | async-start | bytes 262144 | tf_op jit(solution)/shard_map/all_to_all | solution.py:32
  47.8 11.9 %all-to-all-start.3 = ((f32[32,1,1280]{2,1,0:T(1,128)}), f32[32,1,1280]{2,1,0:T(1,128)S(1)}, u32[]{:S(2)}, u32[]{:S(2)}) async-start(f32[32,1,1280]{2,1,0:T(1,128)} %get-tuple-element.44), calls=%async_computation.3 | async-start | bytes 327680 | tf_op jit(solution)/shard_map/all_to_all | solution.py:32

commit v6 on v5

--- a/solution.py
+++ b/solution.py
@@ -168,7 +168,7 @@
         ones = jnp.ones((8, exact.shape[0]), BF16)
         feat_sum_ref[row, :] = contract(ones, exact.astype(BF16), 1, 0)[0:1]
 
-    each(dates, one, 8)
+    each(dates, one, dates)
     for part in range(parts):
         each(dates, lambda date, part=part: sent(date, part).wait())
 
@@ -257,7 +257,7 @@
         rate[...] += horizon * jnp.sum(product.reshape(-1, 8, knot_count), axis=0)
         loads[...] += contract(adjoint, exact.astype(BF16), 0, 0)
 
-    each(dates, one)
+    each(dates, one, 2 - dates % 2)
     shares = jnp.zeros(member.shape, F32)
     for part in split(loads[...], 3):
         shares = shares + contract(flows, part, 1, 1)
@@ -291,9 +291,13 @@
     out_ref[...] = jnp.broadcast_to(row[None], out_ref.shape)
 
 
-def start_kernel(blend_ref, shift_ref, load_ref, later_ref, exact_hbm, out_ref, exact_buf, sems, blend):
+def start_kernel(
+    blend_ref, shift_ref, load_ref, later_ref, exact_hbm, jac_hbm, out_ref, kept_ref, exact_buf, sems, jac_sems, blend
+):
     dates = shift_ref.shape[0]
+    kept = kept_ref.shape[0]
     each(dates, lambda date: copy_of(exact_hbm, exact_buf, sems, date).start())
+    each(kept, lambda block: copy_of(jac_hbm, kept_ref, jac_sems, block).start())
     blend[...] = blend_ref[...]
 
     def one(date):
@@ -303,11 +307,18 @@
     each(dates, one)
     carried = contract(load_ref[...], blend[...], 1, 1, HIGHEST)
     out_ref[...] = math.exp(-MEAN_REV * STEP_YEARS * dates) * later_ref[...] - carried
-
-
-def final_kernel(index_ref, arrived_ref, jac_hbm, knot_ref, alloc_ref, jac_buf, sems, column, total):
+    each(kept, lambda block: copy_of(jac_hbm, kept_ref, jac_sems, block).wait())
+
+
+def final_kernel(index_ref, arrived_ref, kept_ref, jac_hbm, knot_ref, alloc_ref, jac_buf, sems, column, total):
     blocks, rows, knot_count = jac_hbm.shape
-    each(blocks, lambda block: copy_of(jac_hbm, jac_buf, sems, block).start())
+    kept = kept_ref.shape[0]
+    missing = blocks - kept
+
+    def fetched(block):
+        return pltpu.make_async_copy(jac_hbm.at[kept + block], jac_buf.at[block], sems.at[block])
+
+    each(missing, lambda block: fetched(block).start())
     row = jnp.sum(arrived_ref[...], axis=0)
     trades = alloc_ref.shape[1]
     parts = row[:, round_up(knot_count, LANES) :]
@@ -318,16 +329,20 @@
     column[...] = jnp.broadcast_to(row[:, :knot_count], (LANES, knot_count)).T
     total[...] = jnp.zeros_like(total)
 
-    def one(block):
-        copy_of(jac_hbm, jac_buf, sems, block).wait()
-        part = column[pl.ds(pl.multiple_of(block * rows, rows), rows), :]
+    def add(source, block, first_block):
+        part = column[pl.ds(pl.multiple_of((first_block + block) * rows, rows), rows), :]
         for first in range(0, knot_count, LANES):
             size = min(LANES, knot_count - first)
             cut = slice(first, first + size)
-            scaled = jac_buf[block, :, cut] * part[:, :size]
+            scaled = source[block, :, cut] * part[:, :size]
             total[:, cut] += jnp.sum(scaled.reshape(-1, total.shape[0], size), axis=0)
 
-    each(blocks, one)
+    def late(block):
+        fetched(block).wait()
+        add(jac_buf, block, kept)
+
+    each(kept, lambda block: add(kept_ref, block, 0))
+    each(missing, late)
     knot_ref[...] = jnp.sum(total[...], axis=0, keepdims=True)
 
 
@@ -508,32 +523,33 @@
         flops=6 * sets * dates * knot_count,
     )
     arrived = exchange(copies)
-    (start_adjoint,) = run(
+    kept = blocks * 4 // 8
+    start_adjoint, kept_blocks = run(
         "start",
         start_kernel,
-        [shaped((factors, paths))],
-        [blend, shift, factor_load, later_adjoint, exact],
-        hbm=(4,),
+        [shaped((factors, paths)), shaped((kept,) + jac_blocks.shape[1:])],
+        [blend, shift, factor_load, later_adjoint, exact, jac_blocks],
+        hbm=(4, 5),
         scratch=[shaped((dates, paths, knot_count)), shaped((paths, knot_count))],
-        copies=(dates,),
+        copies=(dates, kept),
         flops=2 * factors * paths * knot_count,
-        grant=MIDDLE,
+        grant=49<<20,
     )
     knot_grad, alloc = run(
         "final",
         final_kernel,
         [shaped((1, knot_count)), shaped((1, trades))],
-        [offset.reshape(1), arrived, jac_blocks],
+        [offset.reshape(1), arrived, kept_blocks, jac_blocks],
         scalars=1,
-        hbm=(2,),
+        hbm=(3,),
         scratch=[
-            shaped(jac_blocks.shape),
+            shaped((blocks - kept,) + jac_blocks.shape[1:]),
             shaped((knot_count, LANES)),
             shaped((8, knot_count)),
         ],
-        copies=(blocks,),
+        copies=(blocks - kept,),
         flops=2 * knot_count**2,
-        grant=52 << 20,
+        grant=51<<20,
     )
     return knot_grad.reshape(knot_count), alloc.reshape(trades), start_adjoint
 

time: 63 us -> 61.9 us (0.983)
  waiting for transfers between devices: 12 us -> 13.6 us
  local copies, waits for them, and re-layouts: 2.12 us -> 0.79 us
  Pallas kernels: 29.9 us -> 29 us
    all_to_all x4, waiting for transfers between devices: 11.7 us -> 13.3 us  [exchange(): return lax.all_to_all(copies, 'path', 0, 0, axis_index_groups=groups)]
    unnamed x14, local copies, waits for them, and re-layouts: 2.12 us -> 0.79 us
    pallas_call x10, Pallas kernels: 29.9 us -> 29 us  [run(): pl.pallas_call(kernel, out_shape=tuple(out_shape), in_specs=specs[:len(op...]
where the time goes in v6:
time: 61.9 us; the launch traced here: 61.4 us
  Pallas kernels  29 us (47%)
  starting transfers between devices  17.1 us (28%)
  waiting for transfers between devices  13.6 us (22%)
  between operations  0.8 us (1%)
  local copies, waits for them, and re-layouts  0.79 us (1%)
    pallas_call x10, Pallas kernels, run(): pl.pallas_call(kernel, out_shape=tuple(out_shape), in_specs=specs[:len(op...  29 us
    all_to_all x4, starting transfers between devices, exchange(): return lax.all_to_all(copies, 'path', 0, 0, axis_index_groups=groups)  17.1 us
    all_to_all x4, waiting for transfers between devices, exchange(): return lax.all_to_all(copies, 'path', 0, 0, axis_index_groups=groups)  13.3 us
  transfers between devices with their start and end apart: 5, of which 5 were waited for; matrix products, arithmetic and copies ran while one was open for 0% of the time, Pallas kernels for 36%

profile of v6, /device:TPU:0, one launch (start us, length us, event | category | flops | bytes accessed | tf_op | source)
XLA Modules:
  0.0 61.4 jit_solution(11819833103231951914)
XLA Ops:
  0.7 1.6 %prep.1 = bf16[16,8,1024]{2,1,0:T(8,128)(2,1)} custom-call(s32[8]{0:T(128)} %end_ref.1, s32[8]{0:T(128)} %bitcast.17, bf16[8,960]{1,0:T(8,128)(2,1)} %cash_ref.1), custom_call_target="tpu_custom_call" | custom-call | bytes 286720 | tf_op jit(solution)/shard_map/prep/pallas_call | solution.py:377
  2.2 8.3 %all-to-all-start = ((bf16[16,8,1024]{2,1,0:T(8,128)(2,1)}), bf16[16,8,1024]{2,1,0:T(8,128)(2,1)S(1)}, u32[]{:S(2)}, u32[]{:S(2)}) async-start(bf16[16,8,1024]{2,1,0:T(8,128)(2,1)} %prep.1), calls=%async_computation | async-start | bytes 524288 | tf_op jit(solution)/shard_map/all_to_all | solution.py:32
  10.6 7.2 %features.1 = (f32[8,256,960]{2,1,0:T(8,128)}, f32[8,960]{1,0:T(8,128)}) custom-call(f32[8]{0:T(128)} %vol_hbm.1, f32[8,32,256]{2,1,0:T(8,128)} %normals_hbm.1, f32[32,256]{1,0:T(8,128)} %start_hbm.1, f32[32,960]{1,0:T(8,128)} %load_ref.1, f32[1,960]{1,0:T(1,128)} %bitcast.16, f32[8,120,960]{2,1,0:T(8,128)} %bitcast.13), custom_call_target="tpu_custom_call" | custom-call | flops 754974720 | bytes 12816384 | tf_op jit(solution)/shard_map/features/pallas_call | solution.py:377
  17.7 2.7 %all-to-all-done = bf16[16,8,1024]{2,1,0:T(8,128)(2,1)S(1)} async-done(((bf16[16,8,1024]{2,1,0:T(8,128)(2,1)}), bf16[16,8,1024]{2,1,0:T(8,128)(2,1)S(1)}, u32[]{:S(2)}, u32[]{:S(2)}) %all-to-all-start) | async-done | bytes 262176 | tf_op jit(solution)/shard_map/all_to_all | solution.py:32
  20.4 0.8 %copy-done.1 = f32[8,960]{1,0:T(8,128)S(1)} copy-done((f32[8,960]{1,0:T(8,128)S(1)}, f32[8,960]{1,0:T(8,128)}, u32[]{:S(2)}) %copy-start.1) | copy-done | bytes 30744
  21.2 0.4 half.1
  21.6 0.4 collective-permute-done.other_ref
  22.0 1.3 %net.1 = (bf16[256,1024]{1,0:T(8,128)(2,1)S(1)}, bf16[960,128]{1,0:T(8,128)(2,1)S(1)}, f32[32,8,128]{2,1,0:T(8,128)}) custom-call(bf16[128,1024]{1,0:T(8,128)(2,1)S(1)} %bitcast.11, bf16[128,1024]{1,0:T(8,128)(2,1)S(1)} %collective-permute-done.other_ref, f32[960,128]{1,0:T(8,128)S(1)} %get-tuple-element.31.half_ref, ...), custom_call_target="tpu_custom_call" | custom-call | flops 31457280 | bytes 1966080 | tf_op jit(solution)/shard_map/net/pallas_call | solution.py:377
  23.2 3.3 %all-to-all-start.1 = ((f32[32,8,128]{2,1,0:T(8,128)}), f32[32,8,128]{2,1,0:T(8,128)S(1)}, u32[]{:S(2)}, u32[]{:S(2)}) async-start(f32[32,8,128]{2,1,0:T(8,128)} %get-tuple-element.33), calls=%async_computation.1 | async-start | bytes 262144 | tf_op jit(solution)/shard_map/all_to_all | solution.py:32
  26.5 0.0 copy-start.4
  26.5 0.0 copy-start.2
  26.5 3.8 %values.1 = (f32[8,256,128]{2,1,0:T(8,128)S(1)}, bf16[128,960]{1,0:T(8,128)(2,1)S(1)}, f32[8,128]{1,0:T(8,128)S(1)}) custom-call(bf16[256,1024]{1,0:T(8,128)(2,1)S(1)} %get-tuple-element.34.flows_ref, bf16[960,128]{1,0:T(8,128)(2,1)S(1)} %get-tuple-element.35.net_ref, s32[1,128]{1,0:T(1,128)S(1)} %bitcast.12, f32[8,64]{1,0:T(8,128)S(1)} %copy-done.5, ...), custom_call_target="tpu_custom_call" | custom-call | flops 503316480 | bytes 10481664 | tf_op jit(solution)/shard_map/values/pallas_call | solution.py:377
  30.3 4.4 %all-to-all-done.1.arrived_ref = f32[32,8,128]{2,1,0:T(8,128)S(1)} async-done(((f32[32,8,128]{2,1,0:T(8,128)}), f32[32,8,128]{2,1,0:T(8,128)S(1)}, u32[]{:S(2)}, u32[]{:S(2)}) %all-to-all-start.1) | async-done | bytes 131104 | tf_op jit(solution)/shard_map/all_to_all | solution.py:32
  34.7 1.0 %slopes.1 = (f32[8,128]{1,0:T(8,128)S(1)}, f32[8,128]{1,0:T(8,128)S(1)}, f32[32,8,128]{2,1,0:T(8,128)}) custom-call(f32[32,8,128]{2,1,0:T(8,128)S(1)} %all-to-all-done.1.arrived_ref, f32[8,256,128]{2,1,0:T(8,128)S(1)} %get-tuple-element.37.values_ref, f32[8,128]{1,0:T(8,128)S(1)} %get-tuple-element.38.weight_ref, f32[8,128]{1,0:T(8,128)S(1)} %copy-done.4), custom_call_target="tpu_custom_call" | custom-call | flops 4194304 | bytes 1327104 | tf_op jit(solution)/shard_map/slopes/pallas_call | solution.py:377
  35.7 2.6 %all-to-all-start.2 = ((f32[32,8,128]{2,1,0:T(8,128)}), f32[32,8,128]{2,1,0:T(8,128)S(1)}, u32[]{:S(2)}, u32[]{:S(2)}) async-start(f32[32,8,128]{2,1,0:T(8,128)} %get-tuple-element.39), calls=%async_computation.2 | async-start | bytes 262144 | tf_op jit(solution)/shard_map/all_to_all | solution.py:32
  38.3 0.0 copy-start
  38.3 0.0 copy-start.3
  38.3 5.3 %adjoint.1 = (f32[256,960]{1,0:T(8,128)S(1)}, f32[1,960]{1,0:T(1,128)S(1)}, f32[1,256]{1,0:T(1,128)S(1)}, f32[8,256]{1,0:T(8,128)S(1)}) custom-call(f32[8,128]{1,0:T(8,128)S(1)} %get-tuple-element.42.mean_ref, f32[8,128]{1,0:T(8,128)S(1)} %get-tuple-element.40.sums_ref, f32[8,128]{1,0:T(8,128)S(1)} %get-tuple-element.38.weight_ref, f32[8,128]{1,0:T(8,128)S(1)} %copy-done.4, ...), custom_call_target="tpu_custom_call" | custom-call | flops 1006632960 | bytes 11370496 | tf_op jit(solution)/shard_map/adjoint/pallas_call | solution.py:377
  43.6 2.9 %all-to-all-done.2.arrived_ref = f32[32,8,128]{2,1,0:T(8,128)S(1)} async-done(((f32[32,8,128]{2,1,0:T(8,128)}), f32[32,8,128]{2,1,0:T(8,128)S(1)}, u32[]{:S(2)}, u32[]{:S(2)}) %all-to-all-start.2) | async-done | bytes 131104 | tf_op jit(solution)/shard_map/all_to_all | solution.py:32
  46.5 1.2 %finish.1 = (f32[8,960]{1,0:T(8,128)S(1)}, f32[32,1,1280]{2,1,0:T(1,128)}) custom-call(s32[1]{0:T(128)} %bitcast.1.parity_ref, f32[32,8,128]{2,1,0:T(8,128)S(1)} %all-to-all-done.2.arrived_ref, f32[8,128]{1,0:T(8,128)S(1)} %get-tuple-element.40.sums_ref, f32[8,960]{1,0:T(8,128)S(1)} %copy-done.2, bf16[128,960]{1,0:T(8,128)(2,1)S(1)} %get-tuple-element.41.net_ref, ...), custom_call_target="tpu_custom_call" | custom-call | flops 5898240 | bytes 2351104 | tf_op jit(solution)/shard_map/finish/pallas_call | solution.py:377
  47.6 3.0 %all-to-all-start.3 = ((f32[32,1,1280]{2,1,0:T(1,128)}), f32[32,1,1280]{2,1,0:T(1,128)S(1)}, u32[]{:S(2)}, u32[]{:S(2)}) async-start(f32[32,1,1280]{2,1,0:T(1,128)} %get-tuple-element.46), calls=%async_computation.3 | async-start | bytes 327680 | tf_op jit(solution)/shard_map/all_to_all | solution.py:32
  50.6 5.3 %start.1 = (f32[32,256]{1,0:T(8,128)}, f32[4,120,960]{2,1,0:T(8,128)S(1)}) custom-call(f32[256,960]{1,0:T(8,128)S(1)} %get-tuple-element.47.blend_ref, f32[8,960]{1,0:T(8,128)S(1)} %get-tuple-element.48.shift_ref, f32[32,960]{1,0:T(8,128)S(1)} %copy-done, f32[32,256]{1,0:T(8,128)S(1)} %copy-done.3, f32[8,256,960]{2,1,0:T(8,128)} %get-tuple-element.36.exact_hbm, ...), custom_call_target="tpu_custom_call" | custom-call | flops 15728640 | bytes 15564800 | tf_op jit(solution)/shard_map/start/pallas_call | solution.py:377
  55.9 3.3 %all-to-all-done.3.arrived_ref = f32[32,1,1280]{2,1,0:T(1,128)S(1)} async-done(((f32[32,1,1280]{2,1,0:T(1,128)}), f32[32,1,1280]{2,1,0:T(1,128)S(1)}, u32[]{:S(2)}, u32[]{:S(2)}) %all-to-all-start.3) | async-done | bytes 163872 | tf_op jit(solution)/shard_map/all_to_all | solution.py:32
  59.2 2.2 %final.1 = (f32[1,960]{1,0:T(1,128)}, f32[1,8]{1,0:T(1,128)}) custom-call(s32[1]{0:T(128)} %bitcast.index_ref, f32[32,1,1280]{2,1,0:T(1,128)S(1)} %all-to-all-done.3.arrived_ref, f32[4,120,960]{2,1,0:T(8,128)S(1)} %get-tuple-element.49.kept_ref, f32[8,120,960]{2,1,0:T(8,128)} %bitcast.15), custom_call_target="tpu_custom_call" | custom-call | flops 1843200 | bytes 7249920 | tf_op jit(solution)/shard_map/final/pallas_call | solution.py:377
  (10 shorter events, 0.0 us)
Async XLA Ops:
  0.6 25.9 %copy-start.6 = (s32[128,1]{0,1:T(1,128)S(1)}, s32[128,1]{0,1:T(1,128)}, u32[]{:S(2)}) copy-start(s32[128,1]{0,1:T(1,128)} %param.23) | copy-start | bytes 1540
  0.6 25.9 %copy-start.5 = (f32[8,64]{1,0:T(8,128)S(1)}, f32[8,64]{1,0:T(8,128)}, u32[]{:S(2)}) copy-start(f32[8,64]{1,0:T(8,128)} %prob_ref.1) | copy-start | bytes 6148
  2.2 18.2 %all-to-all-start = ((bf16[16,8,1024]{2,1,0:T(8,128)(2,1)}), bf16[16,8,1024]{2,1,0:T(8,128)(2,1)S(1)}, u32[]{:S(2)}, u32[]{:S(2)}) async-start(bf16[16,8,1024]{2,1,0:T(8,128)(2,1)} %prep.1), calls=%async_computation | async-start | bytes 524288 | tf_op jit(solution)/shard_map/all_to_all | solution.py:32
  20.4 1.5 %collective-permute-start = (bf16[128,1024]{1,0:T(8,128)(2,1)S(1)}, bf16[128,1024]{1,0:T(8,128)(2,1)S(1)}, u32[]{:S(2)}, u32[]{:S(2)}) collective-permute-start(bf16[128,1024]{1,0:T(8,128)(2,1)S(1)} %bitcast.9), channel_id=1, source_target_pairs={{0,1},{1,0},{2,3},{3,2},{4,5},{5,4},{6,7},{7,6},{8,9},{9,8},{10,11... | collective-permute-start | bytes 786440 | tf_op jit(solution)/shard_map/ppermute | solution.py:461
  20.4 0.8 %copy-start.1 = (f32[8,960]{1,0:T(8,128)S(1)}, f32[8,960]{1,0:T(8,128)}, u32[]{:S(2)}) copy-start(f32[8,960]{1,0:T(8,128)} %get-tuple-element.30.feat_sum_ref) | copy-start | bytes 92164
  23.2 11.5 %all-to-all-start.1 = ((f32[32,8,128]{2,1,0:T(8,128)}), f32[32,8,128]{2,1,0:T(8,128)S(1)}, u32[]{:S(2)}, u32[]{:S(2)}) async-start(f32[32,8,128]{2,1,0:T(8,128)} %get-tuple-element.33), calls=%async_computation.1 | async-start | bytes 262144 | tf_op jit(solution)/shard_map/all_to_all | solution.py:32
  26.5 8.2 %copy-start.4 = (f32[8,128]{1,0:T(8,128)S(1)}, f32[8,128]{1,0:T(8,128)}, u32[]{:S(2)}) copy-start(f32[8,128]{1,0:T(8,128)} %base_ref.3) | copy-start | bytes 12292
  26.5 11.7 %copy-start.2 = (f32[8,960]{1,0:T(8,128)S(1)}, f32[8,960]{1,0:T(8,128)}, u32[]{:S(2)}) copy-start(f32[8,960]{1,0:T(8,128)} %get-tuple-element.30.feat_sum_ref) | copy-start | bytes 92164
  35.7 10.8 %all-to-all-start.2 = ((f32[32,8,128]{2,1,0:T(8,128)}), f32[32,8,128]{2,1,0:T(8,128)S(1)}, u32[]{:S(2)}, u32[]{:S(2)}) async-start(f32[32,8,128]{2,1,0:T(8,128)} %get-tuple-element.39), calls=%async_computation.2 | async-start | bytes 262144 | tf_op jit(solution)/shard_map/all_to_all | solution.py:32
  38.3 12.3 %copy-start = (f32[32,960]{1,0:T(8,128)S(1)}, f32[32,960]{1,0:T(8,128)}, u32[]{:S(2)}) copy-start(f32[32,960]{1,0:T(8,128)} %load_ref.1) | copy-start | bytes 368644
  38.3 12.3 %copy-start.3 = (f32[32,256]{1,0:T(8,128)S(1)}, f32[32,256]{1,0:T(8,128)}, u32[]{:S(2)}) copy-start(f32[32,256]{1,0:T(8,128)} %later_ref.1) | copy-start | bytes 98308
  47.6 11.6 %all-to-all-start.3 = ((f32[32,1,1280]{2,1,0:T(1,128)}), f32[32,1,1280]{2,1,0:T(1,128)S(1)}, u32[]{:S(2)}, u32[]{:S(2)}) async-start(f32[32,1,1280]{2,1,0:T(1,128)} %get-tuple-element.46), calls=%async_computation.3 | async-start | bytes 327680 | tf_op jit(solution)/shard_map/all_to_all | solution.py:32

commit v7 on v6

--- a/solution.py
+++ b/solution.py
@@ -425,11 +425,14 @@
         scalars=2,
         grant=LARGE,
     )
-    own = exchange(copies, [list(range(side, shards, 2)) for side in range(2)])
+    pairs = shards // 2
+    places = [(2 * pairs - 1 - pair - pairs // 2) % pairs for pair in range(pairs)]
+    own = exchange(copies, [[2 * pair + side for pair in places] for side in range(2)])
     own = own.reshape(all_trades // 2, width)
     index = lax.axis_index("path").astype(jnp.int32)
     parity = lax.rem(index, 2)
-    offset = parity * (all_trades // 2) + lax.div(index, 2) * trades
+    place = lax.rem(2 * pairs - 1 - lax.div(index, 2) - pairs // 2, pairs)
+    offset = parity * (all_trades // 2) + place * trades
     blocks = next(count for count in (8, 4, 2, 1) if knot_count % (8 * count) == 0)
     jac_blocks = spline_jac.reshape(blocks, knot_count // blocks, knot_count)
 
@@ -473,7 +476,7 @@
         [own, other, half, terms],
         flops=sets * all_trades * knot_count,
     )
-    arrived = exchange(copies)
+    arrived = exchange(copies, [list(range(shards))[::-1]])
     values, net_rows, weight = run(
         "values",
         value_kernel,
@@ -492,7 +495,7 @@
         [arrived, values, weight, base_value],
         flops=16 * dates * paths * sets,
     )
-    arrived = exchange(copies)
+    arrived = exchange(copies, [list(range(shards))[::-1]])
     blend, rate, trade_parts, cross = run(
         "adjoint",
         adjoint_kernel,
@@ -522,7 +525,7 @@
         scalars=1,
         flops=6 * sets * dates * knot_count,
     )
-    arrived = exchange(copies)
+    arrived = exchange(copies, [list(range(shards))[::-1]])
     kept = blocks * 4 // 8
     start_adjoint, kept_blocks = run(
         "start",

time: 61.9 us -> 58.9 us (0.952)
  waiting for transfers between devices: 13.6 us -> 10.3 us
    all_to_all x4, waiting for transfers between devices: 13.3 us -> 9.92 us  [exchange(): return lax.all_to_all(copies, 'path', 0, 0, axis_index_groups=groups)]
  transfers between devices with their start and end apart: 5 -> 5, of which waited for: 5 -> 5; matrix products, arithmetic and copies ran while one was open for 0% -> 0% of each run, Pallas kernels for 36% -> 38%
where the time goes in v7:
time: 58.9 us; the launch traced here: 58.4 us
  Pallas kernels  29 us (49%)
  starting transfers between devices  17.5 us (30%)
  waiting for transfers between devices  10.3 us (17%)
  between operations  0.8 us (1%)
  local copies, waits for them, and re-layouts  0.79 us (1%)
    pallas_call x10, Pallas kernels, run(): pl.pallas_call(kernel, out_shape=tuple(out_shape), in_specs=specs[:len(op...  29 us
    all_to_all x4, starting transfers between devices, exchange(): return lax.all_to_all(copies, 'path', 0, 0, axis_index_groups=groups)  17.5 us
    all_to_all x4, waiting for transfers between devices, exchange(): return lax.all_to_all(copies, 'path', 0, 0, axis_index_groups=groups)  9.92 us
  transfers between devices with their start and end apart: 5, of which 5 were waited for; matrix products, arithmetic and copies ran while one was open for 0% of the time, Pallas kernels for 38%

profile of v7, /device:TPU:0, one launch (start us, length us, event | category | flops | bytes accessed | tf_op | source)
XLA Modules:
  0.0 58.4 jit_solution(12193927446033400273)
XLA Ops:
  0.7 1.6 %prep.1 = bf16[16,8,1024]{2,1,0:T(8,128)(2,1)} custom-call(s32[8]{0:T(128)} %end_ref.1, s32[8]{0:T(128)} %bitcast.17, bf16[8,960]{1,0:T(8,128)(2,1)} %cash_ref.1), custom_call_target="tpu_custom_call" | custom-call | bytes 286720 | tf_op jit(solution)/shard_map/prep/pallas_call | solution.py:377
  2.2 8.8 %all-to-all-start = ((bf16[16,8,1024]{2,1,0:T(8,128)(2,1)}), bf16[16,8,1024]{2,1,0:T(8,128)(2,1)S(1)}, u32[]{:S(2)}, u32[]{:S(2)}) async-start(bf16[16,8,1024]{2,1,0:T(8,128)(2,1)} %prep.1), calls=%async_computation | async-start | bytes 524288 | tf_op jit(solution)/shard_map/all_to_all | solution.py:32
  11.0 7.2 %features.1 = (f32[8,256,960]{2,1,0:T(8,128)}, f32[8,960]{1,0:T(8,128)}) custom-call(f32[8]{0:T(128)} %vol_hbm.1, f32[8,32,256]{2,1,0:T(8,128)} %normals_hbm.1, f32[32,256]{1,0:T(8,128)} %start_hbm.1, f32[32,960]{1,0:T(8,128)} %load_ref.1, f32[1,960]{1,0:T(1,128)} %bitcast.16, f32[8,120,960]{2,1,0:T(8,128)} %bitcast.13), custom_call_target="tpu_custom_call" | custom-call | flops 754974720 | bytes 12816384 | tf_op jit(solution)/shard_map/features/pallas_call | solution.py:377
  18.2 0.2 all-to-all-done
  18.4 0.8 %copy-done.1 = f32[8,960]{1,0:T(8,128)S(1)} copy-done((f32[8,960]{1,0:T(8,128)S(1)}, f32[8,960]{1,0:T(8,128)}, u32[]{:S(2)}) %copy-start.1) | copy-done | bytes 30744
  19.2 0.4 half.1
  19.6 0.4 collective-permute-done.other_ref
  20.0 1.3 %net.1 = (bf16[256,1024]{1,0:T(8,128)(2,1)S(1)}, bf16[960,128]{1,0:T(8,128)(2,1)S(1)}, f32[32,8,128]{2,1,0:T(8,128)}) custom-call(bf16[128,1024]{1,0:T(8,128)(2,1)S(1)} %bitcast.11, bf16[128,1024]{1,0:T(8,128)(2,1)S(1)} %collective-permute-done.other_ref, f32[960,128]{1,0:T(8,128)S(1)} %get-tuple-element.31.half_ref, ...), custom_call_target="tpu_custom_call" | custom-call | flops 31457280 | bytes 1966080 | tf_op jit(solution)/shard_map/net/pallas_call | solution.py:377
  21.2 2.9 %all-to-all-start.1 = ((f32[32,8,128]{2,1,0:T(8,128)}), f32[32,8,128]{2,1,0:T(8,128)S(1)}, u32[]{:S(2)}, u32[]{:S(2)}) async-start(f32[32,8,128]{2,1,0:T(8,128)} %get-tuple-element.33), calls=%async_computation.1 | async-start | bytes 262144 | tf_op jit(solution)/shard_map/all_to_all | solution.py:32
  24.2 0.0 copy-start.4
  24.2 0.0 copy-start.2
  24.2 3.8 %values.1 = (f32[8,256,128]{2,1,0:T(8,128)S(1)}, bf16[128,960]{1,0:T(8,128)(2,1)S(1)}, f32[8,128]{1,0:T(8,128)S(1)}) custom-call(bf16[256,1024]{1,0:T(8,128)(2,1)S(1)} %get-tuple-element.34.flows_ref, bf16[960,128]{1,0:T(8,128)(2,1)S(1)} %get-tuple-element.35.net_ref, s32[1,128]{1,0:T(1,128)S(1)} %bitcast.12, f32[8,64]{1,0:T(8,128)S(1)} %copy-done.5, ...), custom_call_target="tpu_custom_call" | custom-call | flops 503316480 | bytes 10481664 | tf_op jit(solution)/shard_map/values/pallas_call | solution.py:377
  28.0 4.1 %all-to-all-done.1.arrived_ref = f32[32,8,128]{2,1,0:T(8,128)S(1)} async-done(((f32[32,8,128]{2,1,0:T(8,128)}), f32[32,8,128]{2,1,0:T(8,128)S(1)}, u32[]{:S(2)}, u32[]{:S(2)}) %all-to-all-start.1) | async-done | bytes 131104 | tf_op jit(solution)/shard_map/all_to_all | solution.py:32
  32.1 1.0 %slopes.1 = (f32[8,128]{1,0:T(8,128)S(1)}, f32[8,128]{1,0:T(8,128)S(1)}, f32[32,8,128]{2,1,0:T(8,128)}) custom-call(f32[32,8,128]{2,1,0:T(8,128)S(1)} %all-to-all-done.1.arrived_ref, f32[8,256,128]{2,1,0:T(8,128)S(1)} %get-tuple-element.37.values_ref, f32[8,128]{1,0:T(8,128)S(1)} %get-tuple-element.38.weight_ref, f32[8,128]{1,0:T(8,128)S(1)} %copy-done.4), custom_call_target="tpu_custom_call" | custom-call | flops 4194304 | bytes 1327104 | tf_op jit(solution)/shard_map/slopes/pallas_call | solution.py:377
  33.1 2.6 %all-to-all-start.2 = ((f32[32,8,128]{2,1,0:T(8,128)}), f32[32,8,128]{2,1,0:T(8,128)S(1)}, u32[]{:S(2)}, u32[]{:S(2)}) async-start(f32[32,8,128]{2,1,0:T(8,128)} %get-tuple-element.39), calls=%async_computation.2 | async-start | bytes 262144 | tf_op jit(solution)/shard_map/all_to_all | solution.py:32
  35.7 0.0 copy-start
  35.7 0.0 copy-start.3
  35.7 5.3 %adjoint.1 = (f32[256,960]{1,0:T(8,128)S(1)}, f32[1,960]{1,0:T(1,128)S(1)}, f32[1,256]{1,0:T(1,128)S(1)}, f32[8,256]{1,0:T(8,128)S(1)}) custom-call(f32[8,128]{1,0:T(8,128)S(1)} %get-tuple-element.42.mean_ref, f32[8,128]{1,0:T(8,128)S(1)} %get-tuple-element.40.sums_ref, f32[8,128]{1,0:T(8,128)S(1)} %get-tuple-element.38.weight_ref, f32[8,128]{1,0:T(8,128)S(1)} %copy-done.4, ...), custom_call_target="tpu_custom_call" | custom-call | flops 1006632960 | bytes 11370496 | tf_op jit(solution)/shard_map/adjoint/pallas_call | solution.py:377
  41.0 2.7 %all-to-all-done.2.arrived_ref = f32[32,8,128]{2,1,0:T(8,128)S(1)} async-done(((f32[32,8,128]{2,1,0:T(8,128)}), f32[32,8,128]{2,1,0:T(8,128)S(1)}, u32[]{:S(2)}, u32[]{:S(2)}) %all-to-all-start.2) | async-done | bytes 131104 | tf_op jit(solution)/shard_map/all_to_all | solution.py:32
  43.7 1.2 %finish.1 = (f32[8,960]{1,0:T(8,128)S(1)}, f32[32,1,1280]{2,1,0:T(1,128)}) custom-call(s32[1]{0:T(128)} %bitcast.1.parity_ref, f32[32,8,128]{2,1,0:T(8,128)S(1)} %all-to-all-done.2.arrived_ref, f32[8,128]{1,0:T(8,128)S(1)} %get-tuple-element.40.sums_ref, f32[8,960]{1,0:T(8,128)S(1)} %copy-done.2, bf16[128,960]{1,0:T(8,128)(2,1)S(1)} %get-tuple-element.41.net_ref, ...), custom_call_target="tpu_custom_call" | custom-call | flops 5898240 | bytes 2351104 | tf_op jit(solution)/shard_map/finish/pallas_call | solution.py:377
  44.8 3.2 %all-to-all-start.3 = ((f32[32,1,1280]{2,1,0:T(1,128)}), f32[32,1,1280]{2,1,0:T(1,128)S(1)}, u32[]{:S(2)}, u32[]{:S(2)}) async-start(f32[32,1,1280]{2,1,0:T(1,128)} %get-tuple-element.46), calls=%async_computation.3 | async-start | bytes 327680 | tf_op jit(solution)/shard_map/all_to_all | solution.py:32
  48.0 5.3 %start.1 = (f32[32,256]{1,0:T(8,128)}, f32[4,120,960]{2,1,0:T(8,128)S(1)}) custom-call(f32[256,960]{1,0:T(8,128)S(1)} %get-tuple-element.47.blend_ref, f32[8,960]{1,0:T(8,128)S(1)} %get-tuple-element.48.shift_ref, f32[32,960]{1,0:T(8,128)S(1)} %copy-done, f32[32,256]{1,0:T(8,128)S(1)} %copy-done.3, f32[8,256,960]{2,1,0:T(8,128)} %get-tuple-element.36.exact_hbm, ...), custom_call_target="tpu_custom_call" | custom-call | flops 15728640 | bytes 15564800 | tf_op jit(solution)/shard_map/start/pallas_call | solution.py:377
  53.3 2.9 %all-to-all-done.3.arrived_ref = f32[32,1,1280]{2,1,0:T(1,128)S(1)} async-done(((f32[32,1,1280]{2,1,0:T(1,128)}), f32[32,1,1280]{2,1,0:T(1,128)S(1)}, u32[]{:S(2)}, u32[]{:S(2)}) %all-to-all-start.3) | async-done | bytes 163872 | tf_op jit(solution)/shard_map/all_to_all | solution.py:32
  56.2 2.2 %final.1 = (f32[1,960]{1,0:T(1,128)}, f32[1,8]{1,0:T(1,128)}) custom-call(s32[1]{0:T(128)} %bitcast.index_ref, f32[32,1,1280]{2,1,0:T(1,128)S(1)} %all-to-all-done.3.arrived_ref, f32[4,120,960]{2,1,0:T(8,128)S(1)} %get-tuple-element.49.kept_ref, f32[8,120,960]{2,1,0:T(8,128)} %bitcast.15), custom_call_target="tpu_custom_call" | custom-call | flops 1843200 | bytes 7249920 | tf_op jit(solution)/shard_map/final/pallas_call | solution.py:377
  (10 shorter events, 0.0 us)
Async XLA Ops:
  0.6 23.5 %copy-start.6 = (s32[128,1]{0,1:T(1,128)S(1)}, s32[128,1]{0,1:T(1,128)}, u32[]{:S(2)}) copy-start(s32[128,1]{0,1:T(1,128)} %param.23) | copy-start | bytes 1540
  0.6 23.5 %copy-start.5 = (f32[8,64]{1,0:T(8,128)S(1)}, f32[8,64]{1,0:T(8,128)}, u32[]{:S(2)}) copy-start(f32[8,64]{1,0:T(8,128)} %prob_ref.1) | copy-start | bytes 6148
  2.2 16.2 %all-to-all-start = ((bf16[16,8,1024]{2,1,0:T(8,128)(2,1)}), bf16[16,8,1024]{2,1,0:T(8,128)(2,1)S(1)}, u32[]{:S(2)}, u32[]{:S(2)}) async-start(bf16[16,8,1024]{2,1,0:T(8,128)(2,1)} %prep.1), calls=%async_computation | async-start | bytes 524288 | tf_op jit(solution)/shard_map/all_to_all | solution.py:32
  18.4 1.5 %collective-permute-start = (bf16[128,1024]{1,0:T(8,128)(2,1)S(1)}, bf16[128,1024]{1,0:T(8,128)(2,1)S(1)}, u32[]{:S(2)}, u32[]{:S(2)}) collective-permute-start(bf16[128,1024]{1,0:T(8,128)(2,1)S(1)} %bitcast.9), channel_id=1, source_target_pairs={{0,1},{1,0},{2,3},{3,2},{4,5},{5,4},{6,7},{7,6},{8,9},{9,8},{10,11... | collective-permute-start | bytes 786440 | tf_op jit(solution)/shard_map/ppermute | solution.py:464
  18.4 0.8 %copy-start.1 = (f32[8,960]{1,0:T(8,128)S(1)}, f32[8,960]{1,0:T(8,128)}, u32[]{:S(2)}) copy-start(f32[8,960]{1,0:T(8,128)} %get-tuple-element.30.feat_sum_ref) | copy-start | bytes 92164
  21.2 10.9 %all-to-all-start.1 = ((f32[32,8,128]{2,1,0:T(8,128)}), f32[32,8,128]{2,1,0:T(8,128)S(1)}, u32[]{:S(2)}, u32[]{:S(2)}) async-start(f32[32,8,128]{2,1,0:T(8,128)} %get-tuple-element.33), calls=%async_computation.1 | async-start | bytes 262144 | tf_op jit(solution)/shard_map/all_to_all | solution.py:32
  24.2 8.0 %copy-start.4 = (f32[8,128]{1,0:T(8,128)S(1)}, f32[8,128]{1,0:T(8,128)}, u32[]{:S(2)}) copy-start(f32[8,128]{1,0:T(8,128)} %base_ref.3) | copy-start | bytes 12292
  24.2 11.5 %copy-start.2 = (f32[8,960]{1,0:T(8,128)S(1)}, f32[8,960]{1,0:T(8,128)}, u32[]{:S(2)}) copy-start(f32[8,960]{1,0:T(8,128)} %get-tuple-element.30.feat_sum_ref) | copy-start | bytes 92164
  33.1 10.5 %all-to-all-start.2 = ((f32[32,8,128]{2,1,0:T(8,128)}), f32[32,8,128]{2,1,0:T(8,128)S(1)}, u32[]{:S(2)}, u32[]{:S(2)}) async-start(f32[32,8,128]{2,1,0:T(8,128)} %get-tuple-element.39), calls=%async_computation.2 | async-start | bytes 262144 | tf_op jit(solution)/shard_map/all_to_all | solution.py:32
  35.7 12.3 %copy-start = (f32[32,960]{1,0:T(8,128)S(1)}, f32[32,960]{1,0:T(8,128)}, u32[]{:S(2)}) copy-start(f32[32,960]{1,0:T(8,128)} %load_ref.1) | copy-start | bytes 368644
  35.7 12.3 %copy-start.3 = (f32[32,256]{1,0:T(8,128)S(1)}, f32[32,256]{1,0:T(8,128)}, u32[]{:S(2)}) copy-start(f32[32,256]{1,0:T(8,128)} %later_ref.1) | copy-start | bytes 98308
  44.8 11.4 %all-to-all-start.3 = ((f32[32,1,1280]{2,1,0:T(1,128)}), f32[32,1,1280]{2,1,0:T(1,128)S(1)}, u32[]{:S(2)}, u32[]{:S(2)}) async-start(f32[32,1,1280]{2,1,0:T(1,128)} %get-tuple-element.46), calls=%async_computation.3 | async-start | bytes 327680 | tf_op jit(solution)/shard_map/all_to_all | solution.py:32

commit v8 on v7

--- a/solution.py
+++ b/solution.py
@@ -181,9 +181,8 @@
     terms_ref[...] = stack(feat_sum_ref[...])
 
 
-def net_kernel(own_ref, other_ref, half_ref, terms_ref, flows_ref, net_ref, out_ref):
+def net_kernel(other_ref, half_ref, terms_ref, net_ref, out_ref):
     knot_count, sets = net_ref.shape
-    flows_ref[...] = jnp.concatenate([own_ref[...], other_ref[...]], axis=0)
     flows = other_ref[...]
     member = member_rows(flows, knot_count, sets).astype(BF16)
     net = (half_ref[...] + contract(flows[:, :knot_count], member, 0, 0)).astype(BF16)
@@ -193,7 +192,7 @@
 
 
 def value_kernel(
-    flows_ref, net_ref, cpty_ref, prob_ref, exact_hbm, values_ref, rows_ref, weight_ref, exact_buf, sems
+    own_ref, other_ref, net_ref, cpty_ref, prob_ref, exact_hbm, values_ref, rows_ref, weight_ref, flows_ref, exact_buf, sems
 ):
     dates = values_ref.shape[0]
     each(dates, lambda date: copy_of(exact_hbm, exact_buf, sems, date).start())
@@ -201,10 +200,9 @@
     chosen = (cpty_ref[...] == labels).astype(F32)
     weight_ref[...] = LOSS_RATE * contract(prob_ref[...], chosen, 1, 0, HIGHEST)
     sets, knot_count = rows_ref.shape
-    half = flows_ref.shape[0] // 2
+    flows_ref[...] = jnp.concatenate([own_ref[...], other_ref[...]], axis=0)
     rows = []
-    for first in (0, half):
-        flows = flows_ref[first : first + half, :]
+    for flows in (own_ref[...], other_ref[...]):
         member = member_rows(flows, knot_count, sets).astype(BF16)
         rows.append(contract(member, flows[:, :knot_count], 0, 0))
     rows_ref[...] = (rows[0] + rows[1]).astype(BF16)
@@ -469,20 +467,20 @@
         [own, feat_sums],
         flops=sets * all_trades * knot_count,
     )
-    flows, net_columns, copies = run(
+    net_columns, copies = run(
         "net",
         net_kernel,
-        [shaped((all_trades, width), BF16), shaped((knot_count, sets), BF16), set_copies],
-        [own, other, half, terms],
+        [shaped((knot_count, sets), BF16), set_copies],
+        [other, half, terms],
         flops=sets * all_trades * knot_count,
     )
     arrived = exchange(copies, [list(range(shards))[::-1]])
-    values, net_rows, weight = run(
+    values, net_rows, weight, flows = run(
         "values",
         value_kernel,
-        [shaped((dates, paths, sets)), shaped((sets, knot_count), BF16), set_rows],
-        [flows, net_columns, set_cpty.reshape(1, sets), default_prob, exact],
-        hbm=(4,),
+        [shaped((dates, paths, sets)), shaped((sets, knot_count), BF16), set_rows, shaped((all_trades, width), BF16)],
+        [own, other, net_columns, set_cpty.reshape(1, sets), default_prob, exact],
+        hbm=(5,),
         scratch=[shaped((dates, paths, knot_count))],
         copies=(dates,),
         flops=sets * work,

time: 58.9 us -> 58.9 us (level)
  no operation moved by 1% of the time
where the time goes in v8:
time: 58.9 us; the launch traced here: 58.4 us
  Pallas kernels  29 us (49%)
  starting transfers between devices  17.5 us (30%)
  waiting for transfers between devices  10.3 us (17%)
  between operations  0.8 us (1%)
  local copies, waits for them, and re-layouts  0.79 us (1%)
    pallas_call x10, Pallas kernels, run(): pl.pallas_call(kernel, out_shape=tuple(out_shape), in_specs=specs[:len(op...  29 us
    all_to_all x4, starting transfers between devices, exchange(): return lax.all_to_all(copies, 'path', 0, 0, axis_index_groups=groups)  17.5 us
    all_to_all x4, waiting for transfers between devices, exchange(): return lax.all_to_all(copies, 'path', 0, 0, axis_index_groups=groups)  9.91 us
  transfers between devices with their start and end apart: 5, of which 5 were waited for; matrix products, arithmetic and copies ran while one was open for 0% of the time, Pallas kernels for 38%

profile of v8, /device:TPU:0, one launch (start us, length us, event | category | flops | bytes accessed | tf_op | source)
XLA Modules:
  0.0 58.4 jit_solution(777174939264583644)
XLA Ops:
  0.7 1.6 %prep.1 = bf16[16,8,1024]{2,1,0:T(8,128)(2,1)} custom-call(s32[8]{0:T(128)} %end_ref.1, s32[8]{0:T(128)} %bitcast.17, bf16[8,960]{1,0:T(8,128)(2,1)} %cash_ref.1), custom_call_target="tpu_custom_call" | custom-call | bytes 286720 | tf_op jit(solution)/shard_map/prep/pallas_call | solution.py:375
  2.2 8.8 %all-to-all-start = ((bf16[16,8,1024]{2,1,0:T(8,128)(2,1)}), bf16[16,8,1024]{2,1,0:T(8,128)(2,1)S(1)}, u32[]{:S(2)}, u32[]{:S(2)}) async-start(bf16[16,8,1024]{2,1,0:T(8,128)(2,1)} %prep.1), calls=%async_computation | async-start | bytes 524288 | tf_op jit(solution)/shard_map/all_to_all | solution.py:32
  11.0 7.2 %features.1 = (f32[8,256,960]{2,1,0:T(8,128)}, f32[8,960]{1,0:T(8,128)}) custom-call(f32[8]{0:T(128)} %vol_hbm.1, f32[8,32,256]{2,1,0:T(8,128)} %normals_hbm.1, f32[32,256]{1,0:T(8,128)} %start_hbm.1, f32[32,960]{1,0:T(8,128)} %load_ref.1, f32[1,960]{1,0:T(1,128)} %bitcast.16, f32[8,120,960]{2,1,0:T(8,128)} %bitcast.13), custom_call_target="tpu_custom_call" | custom-call | flops 754974720 | bytes 12816384 | tf_op jit(solution)/shard_map/features/pallas_call | solution.py:375
  18.2 0.2 all-to-all-done
  18.4 0.8 %copy-done.1 = f32[8,960]{1,0:T(8,128)S(1)} copy-done((f32[8,960]{1,0:T(8,128)S(1)}, f32[8,960]{1,0:T(8,128)}, u32[]{:S(2)}) %copy-start.1) | copy-done | bytes 30744
  19.2 0.4 half.1
  19.6 0.4 collective-permute-done.other_ref
  20.0 1.3 %net.1 = (bf16[960,128]{1,0:T(8,128)(2,1)S(1)}, f32[32,8,128]{2,1,0:T(8,128)}) custom-call(bf16[128,1024]{1,0:T(8,128)(2,1)S(1)} %collective-permute-done.other_ref, f32[960,128]{1,0:T(8,128)S(1)} %get-tuple-element.31.half_ref, bf16[24,960]{1,0:T(8,128)(2,1)S(1)} %get-tuple-element.32.terms_ref), custom_call_target="tpu_custom_call" | custom-call | flops 31457280 | bytes 1179648 | tf_op jit(solution)/shard_map/net/pallas_call | solution.py:375
  21.2 2.9 %all-to-all-start.1 = ((f32[32,8,128]{2,1,0:T(8,128)}), f32[32,8,128]{2,1,0:T(8,128)S(1)}, u32[]{:S(2)}, u32[]{:S(2)}) async-start(f32[32,8,128]{2,1,0:T(8,128)} %get-tuple-element.33), calls=%async_computation.1 | async-start | bytes 262144 | tf_op jit(solution)/shard_map/all_to_all | solution.py:32
  24.2 0.0 copy-start.4
  24.2 0.0 copy-start.2
  24.2 3.8 %values.1 = (f32[8,256,128]{2,1,0:T(8,128)S(1)}, bf16[128,960]{1,0:T(8,128)(2,1)S(1)}, f32[8,128]{1,0:T(8,128)S(1)}, bf16[256,1024]{1,0:T(8,128)(2,1)S(1)}) custom-call(bf16[128,1024]{1,0:T(8,128)(2,1)S(1)} %bitcast.11, bf16[128,1024]{1,0:T(8,128)(2,1)S(1)} %collective-permute-done.other_ref, bf16[960,128]{1,0:T(8,128)(2,1)S(1)} %get-tuple-element.34.net_ref, ...), custom_call_target="tpu_custom_call" | custom-call | flops 503316480 | bytes 11005952 | tf_op jit(solution)/shard_map/values/pallas_call | solution.py:375
  28.0 4.1 %all-to-all-done.1.arrived_ref = f32[32,8,128]{2,1,0:T(8,128)S(1)} async-done(((f32[32,8,128]{2,1,0:T(8,128)}), f32[32,8,128]{2,1,0:T(8,128)S(1)}, u32[]{:S(2)}, u32[]{:S(2)}) %all-to-all-start.1) | async-done | bytes 131104 | tf_op jit(solution)/shard_map/all_to_all | solution.py:32
  32.1 1.0 %slopes.1 = (f32[8,128]{1,0:T(8,128)S(1)}, f32[8,128]{1,0:T(8,128)S(1)}, f32[32,8,128]{2,1,0:T(8,128)}) custom-call(f32[32,8,128]{2,1,0:T(8,128)S(1)} %all-to-all-done.1.arrived_ref, f32[8,256,128]{2,1,0:T(8,128)S(1)} %get-tuple-element.36.values_ref, f32[8,128]{1,0:T(8,128)S(1)} %get-tuple-element.37.weight_ref, f32[8,128]{1,0:T(8,128)S(1)} %copy-done.4), custom_call_target="tpu_custom_call" | custom-call | flops 4194304 | bytes 1327104 | tf_op jit(solution)/shard_map/slopes/pallas_call | solution.py:375
  33.1 2.6 %all-to-all-start.2 = ((f32[32,8,128]{2,1,0:T(8,128)}), f32[32,8,128]{2,1,0:T(8,128)S(1)}, u32[]{:S(2)}, u32[]{:S(2)}) async-start(f32[32,8,128]{2,1,0:T(8,128)} %get-tuple-element.38), calls=%async_computation.2 | async-start | bytes 262144 | tf_op jit(solution)/shard_map/all_to_all | solution.py:32
  35.7 0.0 copy-start
  35.7 0.0 copy-start.3
  35.7 5.3 %adjoint.1 = (f32[256,960]{1,0:T(8,128)S(1)}, f32[1,960]{1,0:T(1,128)S(1)}, f32[1,256]{1,0:T(1,128)S(1)}, f32[8,256]{1,0:T(8,128)S(1)}) custom-call(f32[8,128]{1,0:T(8,128)S(1)} %get-tuple-element.42.mean_ref, f32[8,128]{1,0:T(8,128)S(1)} %get-tuple-element.39.sums_ref, f32[8,128]{1,0:T(8,128)S(1)} %get-tuple-element.37.weight_ref, f32[8,128]{1,0:T(8,128)S(1)} %copy-done.4, ...), custom_call_target="tpu_custom_call" | custom-call | flops 1006632960 | bytes 11370496 | tf_op jit(solution)/shard_map/adjoint/pallas_call | solution.py:375
  41.0 2.7 %all-to-all-done.2.arrived_ref = f32[32,8,128]{2,1,0:T(8,128)S(1)} async-done(((f32[32,8,128]{2,1,0:T(8,128)}), f32[32,8,128]{2,1,0:T(8,128)S(1)}, u32[]{:S(2)}, u32[]{:S(2)}) %all-to-all-start.2) | async-done | bytes 131104 | tf_op jit(solution)/shard_map/all_to_all | solution.py:32
  43.7 1.2 %finish.1 = (f32[8,960]{1,0:T(8,128)S(1)}, f32[32,1,1280]{2,1,0:T(1,128)}) custom-call(s32[1]{0:T(128)} %bitcast.1.parity_ref, f32[32,8,128]{2,1,0:T(8,128)S(1)} %all-to-all-done.2.arrived_ref, f32[8,128]{1,0:T(8,128)S(1)} %get-tuple-element.39.sums_ref, f32[8,960]{1,0:T(8,128)S(1)} %copy-done.2, bf16[128,960]{1,0:T(8,128)(2,1)S(1)} %get-tuple-element.40.net_ref, ...), custom_call_target="tpu_custom_call" | custom-call | flops 5898240 | bytes 2351104 | tf_op jit(solution)/shard_map/finish/pallas_call | solution.py:375
  44.8 3.2 %all-to-all-start.3 = ((f32[32,1,1280]{2,1,0:T(1,128)}), f32[32,1,1280]{2,1,0:T(1,128)S(1)}, u32[]{:S(2)}, u32[]{:S(2)}) async-start(f32[32,1,1280]{2,1,0:T(1,128)} %get-tuple-element.46), calls=%async_computation.3 | async-start | bytes 327680 | tf_op jit(solution)/shard_map/all_to_all | solution.py:32
  48.0 5.3 %start.1 = (f32[32,256]{1,0:T(8,128)}, f32[4,120,960]{2,1,0:T(8,128)S(1)}) custom-call(f32[256,960]{1,0:T(8,128)S(1)} %get-tuple-element.47.blend_ref, f32[8,960]{1,0:T(8,128)S(1)} %get-tuple-element.48.shift_ref, f32[32,960]{1,0:T(8,128)S(1)} %copy-done, f32[32,256]{1,0:T(8,128)S(1)} %copy-done.3, f32[8,256,960]{2,1,0:T(8,128)} %get-tuple-element.35.exact_hbm, ...), custom_call_target="tpu_custom_call" | custom-call | flops 15728640 | bytes 15564800 | tf_op jit(solution)/shard_map/start/pallas_call | solution.py:375
  53.3 2.9 %all-to-all-done.3.arrived_ref = f32[32,1,1280]{2,1,0:T(1,128)S(1)} async-done(((f32[32,1,1280]{2,1,0:T(1,128)}), f32[32,1,1280]{2,1,0:T(1,128)S(1)}, u32[]{:S(2)}, u32[]{:S(2)}) %all-to-all-start.3) | async-done | bytes 163872 | tf_op jit(solution)/shard_map/all_to_all | solution.py:32
  56.2 2.2 %final.1 = (f32[1,960]{1,0:T(1,128)}, f32[1,8]{1,0:T(1,128)}) custom-call(s32[1]{0:T(128)} %bitcast.index_ref, f32[32,1,1280]{2,1,0:T(1,128)S(1)} %all-to-all-done.3.arrived_ref, f32[4,120,960]{2,1,0:T(8,128)S(1)} %get-tuple-element.49.kept_ref, f32[8,120,960]{2,1,0:T(8,128)} %bitcast.15), custom_call_target="tpu_custom_call" | custom-call | flops 1843200 | bytes 7249920 | tf_op jit(solution)/shard_map/final/pallas_call | solution.py:375
  (10 shorter events, 0.0 us)
Async XLA Ops:
  0.6 23.5 %copy-start.6 = (s32[128,1]{0,1:T(1,128)S(1)}, s32[128,1]{0,1:T(1,128)}, u32[]{:S(2)}) copy-start(s32[128,1]{0,1:T(1,128)} %param.23) | copy-start | bytes 1540
  0.6 23.5 %copy-start.5 = (f32[8,64]{1,0:T(8,128)S(1)}, f32[8,64]{1,0:T(8,128)}, u32[]{:S(2)}) copy-start(f32[8,64]{1,0:T(8,128)} %prob_ref.1) | copy-start | bytes 6148
  2.2 16.2 %all-to-all-start = ((bf16[16,8,1024]{2,1,0:T(8,128)(2,1)}), bf16[16,8,1024]{2,1,0:T(8,128)(2,1)S(1)}, u32[]{:S(2)}, u32[]{:S(2)}) async-start(bf16[16,8,1024]{2,1,0:T(8,128)(2,1)} %prep.1), calls=%async_computation | async-start | bytes 524288 | tf_op jit(solution)/shard_map/all_to_all | solution.py:32
  18.4 1.5 %collective-permute-start = (bf16[128,1024]{1,0:T(8,128)(2,1)S(1)}, bf16[128,1024]{1,0:T(8,128)(2,1)S(1)}, u32[]{:S(2)}, u32[]{:S(2)}) collective-permute-start(bf16[128,1024]{1,0:T(8,128)(2,1)S(1)} %bitcast.9), channel_id=1, source_target_pairs={{0,1},{1,0},{2,3},{3,2},{4,5},{5,4},{6,7},{7,6},{8,9},{9,8},{10,11... | collective-permute-start | bytes 786440 | tf_op jit(solution)/shard_map/ppermute | solution.py:462
  18.4 0.8 %copy-start.1 = (f32[8,960]{1,0:T(8,128)S(1)}, f32[8,960]{1,0:T(8,128)}, u32[]{:S(2)}) copy-start(f32[8,960]{1,0:T(8,128)} %get-tuple-element.30.feat_sum_ref) | copy-start | bytes 92164
  21.2 10.9 %all-to-all-start.1 = ((f32[32,8,128]{2,1,0:T(8,128)}), f32[32,8,128]{2,1,0:T(8,128)S(1)}, u32[]{:S(2)}, u32[]{:S(2)}) async-start(f32[32,8,128]{2,1,0:T(8,128)} %get-tuple-element.33), calls=%async_computation.1 | async-start | bytes 262144 | tf_op jit(solution)/shard_map/all_to_all | solution.py:32
  24.2 8.0 %copy-start.4 = (f32[8,128]{1,0:T(8,128)S(1)}, f32[8,128]{1,0:T(8,128)}, u32[]{:S(2)}) copy-start(f32[8,128]{1,0:T(8,128)} %base_ref.3) | copy-start | bytes 12292
  24.2 11.5 %copy-start.2 = (f32[8,960]{1,0:T(8,128)S(1)}, f32[8,960]{1,0:T(8,128)}, u32[]{:S(2)}) copy-start(f32[8,960]{1,0:T(8,128)} %get-tuple-element.30.feat_sum_ref) | copy-start | bytes 92164
  33.1 10.5 %all-to-all-start.2 = ((f32[32,8,128]{2,1,0:T(8,128)}), f32[32,8,128]{2,1,0:T(8,128)S(1)}, u32[]{:S(2)}, u32[]{:S(2)}) async-start(f32[32,8,128]{2,1,0:T(8,128)} %get-tuple-element.38), calls=%async_computation.2 | async-start | bytes 262144 | tf_op jit(solution)/shard_map/all_to_all | solution.py:32
  35.7 12.3 %copy-start = (f32[32,960]{1,0:T(8,128)S(1)}, f32[32,960]{1,0:T(8,128)}, u32[]{:S(2)}) copy-start(f32[32,960]{1,0:T(8,128)} %load_ref.1) | copy-start | bytes 368644
  35.7 12.3 %copy-start.3 = (f32[32,256]{1,0:T(8,128)S(1)}, f32[32,256]{1,0:T(8,128)}, u32[]{:S(2)}) copy-start(f32[32,256]{1,0:T(8,128)} %later_ref.1) | copy-start | bytes 98308
  44.8 11.4 %all-to-all-start.3 = ((f32[32,1,1280]{2,1,0:T(1,128)}), f32[32,1,1280]{2,1,0:T(1,128)S(1)}, u32[]{:S(2)}, u32[]{:S(2)}) async-start(f32[32,1,1280]{2,1,0:T(1,128)} %get-tuple-element.46), calls=%async_computation.3 | async-start | bytes 327680 | tf_op jit(solution)/shard_map/all_to_all | solution.py:32

commit v9 on v7

--- a/solution.py
+++ b/solution.py
@@ -146,11 +146,18 @@
 
     def zero_rates(block):
         copy_of(jac_hbm, jac_buf, jac_sems, block).wait()
-        sums = jnp.sum(jac_buf[block] * knots_ref[...], axis=1, keepdims=True)
-        column[pl.ds(pl.multiple_of(block * rows, rows), rows), :] = jnp.broadcast_to(sums, (rows, LANES))
+        sums = jnp.zeros((rows, LANES), F32)
+        for first in range(0, knot_count, LANES):
+            size = min(LANES, knot_count - first)
+            cut = slice(first, first + size)
+            part = jac_buf[block, :, cut] * knots_ref[:, cut]
+            if size < LANES:
+                part = jnp.concatenate([part, jnp.zeros((rows, LANES - size), F32)], axis=1)
+            sums = sums + part
+        column[pl.ds(pl.multiple_of(block * rows, rows), rows), :] = sums
 
     each(blocks, zero_rates)
-    rate_ref[...] = column[...].T[0:1]
+    rate_ref[...] = jnp.sum(column[...].T, axis=0, keepdims=True)
 
     def one(date):
         now = DECAY * state[...] + vol_ref[date] * normals_ref[date]
@@ -165,8 +172,7 @@
         for part in range(parts):
             sent(date, part).start()
         row = pl.ds(date, 1)
-        ones = jnp.ones((8, exact.shape[0]), BF16)
-        feat_sum_ref[row, :] = contract(ones, exact.astype(BF16), 1, 0)[0:1]
+        feat_sum_ref[row, :] = jnp.sum(exact.astype(BF16).astype(F32), axis=0, keepdims=True)
 
     each(dates, one, dates)
     for part in range(parts):

time: 58.9 us -> 58.9 us (level)
  transfers between devices with their start and end apart: 5 -> 5, of which waited for: 5 -> 4; matrix products, arithmetic and copies ran while one was open for 0% -> 0% of each run, Pallas kernels for 38% -> 38%
where the time goes in v9:
time: 58.9 us; the launch traced here: 58.4 us
  Pallas kernels  29.4 us (50%)
  starting transfers between devices  17.4 us (30%)
  waiting for transfers between devices  10 us (17%)
  between operations  0.82 us (1%)
  local copies, waits for them, and re-layouts  0.79 us (1%)
    pallas_call x10, Pallas kernels, run(): pl.pallas_call(kernel, out_shape=tuple(out_shape), in_specs=specs[:len(op...  29.4 us
    all_to_all x4, starting transfers between devices, exchange(): return lax.all_to_all(copies, 'path', 0, 0, axis_index_groups=groups)  17.3 us
    all_to_all x4, waiting for transfers between devices, exchange(): return lax.all_to_all(copies, 'path', 0, 0, axis_index_groups=groups)  9.68 us
  transfers between devices with their start and end apart: 5, of which 4 were waited for; matrix products, arithmetic and copies ran while one was open for 0% of the time, Pallas kernels for 38%

profile of v9, /device:TPU:0, one launch (start us, length us, event | category | flops | bytes accessed | tf_op | source)
XLA Modules:
  0.0 58.4 jit_solution(15415761358953596926)
XLA Ops:
  0.7 1.6 %prep.1 = bf16[16,8,1024]{2,1,0:T(8,128)(2,1)} custom-call(s32[8]{0:T(128)} %end_ref.1, s32[8]{0:T(128)} %bitcast.17, bf16[8,960]{1,0:T(8,128)(2,1)} %cash_ref.1), custom_call_target="tpu_custom_call" | custom-call | bytes 286720 | tf_op jit(solution)/shard_map/prep/pallas_call | solution.py:383
  2.2 8.8 %all-to-all-start = ((bf16[16,8,1024]{2,1,0:T(8,128)(2,1)}), bf16[16,8,1024]{2,1,0:T(8,128)(2,1)S(1)}, u32[]{:S(2)}, u32[]{:S(2)}) async-start(bf16[16,8,1024]{2,1,0:T(8,128)(2,1)} %prep.1), calls=%async_computation | async-start | bytes 524288 | tf_op jit(solution)/shard_map/all_to_all | solution.py:32
  11.0 7.5 %features.1 = (f32[8,256,960]{2,1,0:T(8,128)}, f32[8,960]{1,0:T(8,128)}) custom-call(f32[8]{0:T(128)} %vol_hbm.1, f32[8,32,256]{2,1,0:T(8,128)} %normals_hbm.1, f32[32,256]{1,0:T(8,128)} %start_hbm.1, f32[32,960]{1,0:T(8,128)} %load_ref.1, f32[1,960]{1,0:T(1,128)} %bitcast.16, f32[8,120,960]{2,1,0:T(8,128)} %bitcast.13), custom_call_target="tpu_custom_call" | custom-call | flops 754974720 | bytes 12816384 | tf_op jit(solution)/shard_map/features/pallas_call | solution.py:383
  18.5 0.1 collective-permute-start
  18.6 0.0 copy-start.1
  18.6 0.7 %copy-done.1 = f32[8,960]{1,0:T(8,128)S(1)} copy-done((f32[8,960]{1,0:T(8,128)S(1)}, f32[8,960]{1,0:T(8,128)}, u32[]{:S(2)}) %copy-start.1) | copy-done | bytes 30744
  19.4 0.4 half.1
  19.8 0.3 collective-permute-done.other_ref
  20.1 1.3 %net.1 = (bf16[256,1024]{1,0:T(8,128)(2,1)S(1)}, bf16[960,128]{1,0:T(8,128)(2,1)S(1)}, f32[32,8,128]{2,1,0:T(8,128)}) custom-call(bf16[128,1024]{1,0:T(8,128)(2,1)S(1)} %bitcast.11, bf16[128,1024]{1,0:T(8,128)(2,1)S(1)} %collective-permute-done.other_ref, f32[960,128]{1,0:T(8,128)S(1)} %get-tuple-element.31.half_ref, ...), custom_call_target="tpu_custom_call" | custom-call | flops 31457280 | bytes 1966080 | tf_op jit(solution)/shard_map/net/pallas_call | solution.py:383
  21.4 2.7 %all-to-all-start.1 = ((f32[32,8,128]{2,1,0:T(8,128)}), f32[32,8,128]{2,1,0:T(8,128)S(1)}, u32[]{:S(2)}, u32[]{:S(2)}) async-start(f32[32,8,128]{2,1,0:T(8,128)} %get-tuple-element.33), calls=%async_computation.1 | async-start | bytes 262144 | tf_op jit(solution)/shard_map/all_to_all | solution.py:32
  24.2 0.0 copy-start.2
  24.2 3.8 %values.1 = (f32[8,256,128]{2,1,0:T(8,128)S(1)}, bf16[128,960]{1,0:T(8,128)(2,1)S(1)}, f32[8,128]{1,0:T(8,128)S(1)}) custom-call(bf16[256,1024]{1,0:T(8,128)(2,1)S(1)} %get-tuple-element.34.flows_ref, bf16[960,128]{1,0:T(8,128)(2,1)S(1)} %get-tuple-element.35.net_ref, s32[1,128]{1,0:T(1,128)S(1)} %bitcast.12, f32[8,64]{1,0:T(8,128)S(1)} %copy-done.5, ...), custom_call_target="tpu_custom_call" | custom-call | flops 503316480 | bytes 10481664 | tf_op jit(solution)/shard_map/values/pallas_call | solution.py:383
  28.0 4.1 %all-to-all-done.1.arrived_ref = f32[32,8,128]{2,1,0:T(8,128)S(1)} async-done(((f32[32,8,128]{2,1,0:T(8,128)}), f32[32,8,128]{2,1,0:T(8,128)S(1)}, u32[]{:S(2)}, u32[]{:S(2)}) %all-to-all-start.1) | async-done | bytes 131104 | tf_op jit(solution)/shard_map/all_to_all | solution.py:32
  32.1 1.0 %slopes.1 = (f32[8,128]{1,0:T(8,128)S(1)}, f32[8,128]{1,0:T(8,128)S(1)}, f32[32,8,128]{2,1,0:T(8,128)}) custom-call(f32[32,8,128]{2,1,0:T(8,128)S(1)} %all-to-all-done.1.arrived_ref, f32[8,256,128]{2,1,0:T(8,128)S(1)} %get-tuple-element.37.values_ref, f32[8,128]{1,0:T(8,128)S(1)} %get-tuple-element.38.weight_ref, f32[8,128]{1,0:T(8,128)S(1)} %copy-done.4), custom_call_target="tpu_custom_call" | custom-call | flops 4194304 | bytes 1327104 | tf_op jit(solution)/shard_map/slopes/pallas_call | solution.py:383
  33.1 2.6 %all-to-all-start.2 = ((f32[32,8,128]{2,1,0:T(8,128)}), f32[32,8,128]{2,1,0:T(8,128)S(1)}, u32[]{:S(2)}, u32[]{:S(2)}) async-start(f32[32,8,128]{2,1,0:T(8,128)} %get-tuple-element.39), calls=%async_computation.2 | async-start | bytes 262144 | tf_op jit(solution)/shard_map/all_to_all | solution.py:32
  35.7 0.0 copy-start
  35.7 0.0 copy-start.3
  35.7 5.3 %adjoint.1 = (f32[256,960]{1,0:T(8,128)S(1)}, f32[1,960]{1,0:T(1,128)S(1)}, f32[1,256]{1,0:T(1,128)S(1)}, f32[8,256]{1,0:T(8,128)S(1)}) custom-call(f32[8,128]{1,0:T(8,128)S(1)} %get-tuple-element.42.mean_ref, f32[8,128]{1,0:T(8,128)S(1)} %get-tuple-element.40.sums_ref, f32[8,128]{1,0:T(8,128)S(1)} %get-tuple-element.38.weight_ref, f32[8,128]{1,0:T(8,128)S(1)} %copy-done.4, ...), custom_call_target="tpu_custom_call" | custom-call | flops 1006632960 | bytes 11370496 | tf_op jit(solution)/shard_map/adjoint/pallas_call | solution.py:383
  41.0 2.7 %all-to-all-done.2.arrived_ref = f32[32,8,128]{2,1,0:T(8,128)S(1)} async-done(((f32[32,8,128]{2,1,0:T(8,128)}), f32[32,8,128]{2,1,0:T(8,128)S(1)}, u32[]{:S(2)}, u32[]{:S(2)}) %all-to-all-start.2) | async-done | bytes 131104 | tf_op jit(solution)/shard_map/all_to_all | solution.py:32
  43.7 1.2 %finish.1 = (f32[8,960]{1,0:T(8,128)S(1)}, f32[32,1,1280]{2,1,0:T(1,128)}) custom-call(s32[1]{0:T(128)} %bitcast.1.parity_ref, f32[32,8,128]{2,1,0:T(8,128)S(1)} %all-to-all-done.2.arrived_ref, f32[8,128]{1,0:T(8,128)S(1)} %get-tuple-element.40.sums_ref, f32[8,960]{1,0:T(8,128)S(1)} %copy-done.2, bf16[128,960]{1,0:T(8,128)(2,1)S(1)} %get-tuple-element.41.net_ref, ...), custom_call_target="tpu_custom_call" | custom-call | flops 5898240 | bytes 2351104 | tf_op jit(solution)/shard_map/finish/pallas_call | solution.py:383
  44.8 3.2 %all-to-all-start.3 = ((f32[32,1,1280]{2,1,0:T(1,128)}), f32[32,1,1280]{2,1,0:T(1,128)S(1)}, u32[]{:S(2)}, u32[]{:S(2)}) async-start(f32[32,1,1280]{2,1,0:T(1,128)} %get-tuple-element.46), calls=%async_computation.3 | async-start | bytes 327680 | tf_op jit(solution)/shard_map/all_to_all | solution.py:32
  48.0 5.3 %start.1 = (f32[32,256]{1,0:T(8,128)}, f32[4,120,960]{2,1,0:T(8,128)S(1)}) custom-call(f32[256,960]{1,0:T(8,128)S(1)} %get-tuple-element.47.blend_ref, f32[8,960]{1,0:T(8,128)S(1)} %get-tuple-element.48.shift_ref, f32[32,960]{1,0:T(8,128)S(1)} %copy-done, f32[32,256]{1,0:T(8,128)S(1)} %copy-done.3, f32[8,256,960]{2,1,0:T(8,128)} %get-tuple-element.36.exact_hbm, ...), custom_call_target="tpu_custom_call" | custom-call | flops 15728640 | bytes 15564800 | tf_op jit(solution)/shard_map/start/pallas_call | solution.py:383
  53.3 2.9 %all-to-all-done.3.arrived_ref = f32[32,1,1280]{2,1,0:T(1,128)S(1)} async-done(((f32[32,1,1280]{2,1,0:T(1,128)}), f32[32,1,1280]{2,1,0:T(1,128)S(1)}, u32[]{:S(2)}, u32[]{:S(2)}) %all-to-all-start.3) | async-done | bytes 163872 | tf_op jit(solution)/shard_map/all_to_all | solution.py:32
  56.2 2.2 %final.1 = (f32[1,960]{1,0:T(1,128)}, f32[1,8]{1,0:T(1,128)}) custom-call(s32[1]{0:T(128)} %bitcast.index_ref, f32[32,1,1280]{2,1,0:T(1,128)S(1)} %all-to-all-done.3.arrived_ref, f32[4,120,960]{2,1,0:T(8,128)S(1)} %get-tuple-element.49.kept_ref, f32[8,120,960]{2,1,0:T(8,128)} %bitcast.15), custom_call_target="tpu_custom_call" | custom-call | flops 1843200 | bytes 7249920 | tf_op jit(solution)/shard_map/final/pallas_call | solution.py:383
  (10 shorter events, 0.0 us)
Async XLA Ops:
  0.6 23.5 %copy-start.6 = (s32[128,1]{0,1:T(1,128)S(1)}, s32[128,1]{0,1:T(1,128)}, u32[]{:S(2)}) copy-start(s32[128,1]{0,1:T(1,128)} %param.23) | copy-start | bytes 1540
  0.6 23.5 %copy-start.5 = (f32[8,64]{1,0:T(8,128)S(1)}, f32[8,64]{1,0:T(8,128)}, u32[]{:S(2)}) copy-start(f32[8,64]{1,0:T(8,128)} %prob_ref.1) | copy-start | bytes 6148
  2.2 16.3 %all-to-all-start = ((bf16[16,8,1024]{2,1,0:T(8,128)(2,1)}), bf16[16,8,1024]{2,1,0:T(8,128)(2,1)S(1)}, u32[]{:S(2)}, u32[]{:S(2)}) async-start(bf16[16,8,1024]{2,1,0:T(8,128)(2,1)} %prep.1), calls=%async_computation | async-start | bytes 524288 | tf_op jit(solution)/shard_map/all_to_all | solution.py:32
  18.5 1.6 %collective-permute-start = (bf16[128,1024]{1,0:T(8,128)(2,1)S(1)}, bf16[128,1024]{1,0:T(8,128)(2,1)S(1)}, u32[]{:S(2)}, u32[]{:S(2)}) collective-permute-start(bf16[128,1024]{1,0:T(8,128)(2,1)S(1)} %bitcast.9), channel_id=1, source_target_pairs={{0,1},{1,0},{2,3},{3,2},{4,5},{5,4},{6,7},{7,6},{8,9},{9,8},{10,11... | collective-permute-start | bytes 786440 | tf_op jit(solution)/shard_map/ppermute | solution.py:470
  18.6 0.8 %copy-start.1 = (f32[8,960]{1,0:T(8,128)S(1)}, f32[8,960]{1,0:T(8,128)}, u32[]{:S(2)}) copy-start(f32[8,960]{1,0:T(8,128)} %get-tuple-element.30.feat_sum_ref) | copy-start | bytes 92164
  21.4 10.7 %all-to-all-start.1 = ((f32[32,8,128]{2,1,0:T(8,128)}), f32[32,8,128]{2,1,0:T(8,128)S(1)}, u32[]{:S(2)}, u32[]{:S(2)}) async-start(f32[32,8,128]{2,1,0:T(8,128)} %get-tuple-element.33), calls=%async_computation.1 | async-start | bytes 262144 | tf_op jit(solution)/shard_map/all_to_all | solution.py:32
  24.2 8.0 %copy-start.4 = (f32[8,128]{1,0:T(8,128)S(1)}, f32[8,128]{1,0:T(8,128)}, u32[]{:S(2)}) copy-start(f32[8,128]{1,0:T(8,128)} %base_ref.3) | copy-start | bytes 12292
  24.2 11.5 %copy-start.2 = (f32[8,960]{1,0:T(8,128)S(1)}, f32[8,960]{1,0:T(8,128)}, u32[]{:S(2)}) copy-start(f32[8,960]{1,0:T(8,128)} %get-tuple-element.30.feat_sum_ref) | copy-start | bytes 92164
  33.1 10.5 %all-to-all-start.2 = ((f32[32,8,128]{2,1,0:T(8,128)}), f32[32,8,128]{2,1,0:T(8,128)S(1)}, u32[]{:S(2)}, u32[]{:S(2)}) async-start(f32[32,8,128]{2,1,0:T(8,128)} %get-tuple-element.39), calls=%async_computation.2 | async-start | bytes 262144 | tf_op jit(solution)/shard_map/all_to_all | solution.py:32
  35.7 12.3 %copy-start = (f32[32,960]{1,0:T(8,128)S(1)}, f32[32,960]{1,0:T(8,128)}, u32[]{:S(2)}) copy-start(f32[32,960]{1,0:T(8,128)} %load_ref.1) | copy-start | bytes 368644
  35.7 12.3 %copy-start.3 = (f32[32,256]{1,0:T(8,128)S(1)}, f32[32,256]{1,0:T(8,128)}, u32[]{:S(2)}) copy-start(f32[32,256]{1,0:T(8,128)} %later_ref.1) | copy-start | bytes 98308
  44.8 11.4 %all-to-all-start.3 = ((f32[32,1,1280]{2,1,0:T(1,128)}), f32[32,1,1280]{2,1,0:T(1,128)S(1)}, u32[]{:S(2)}, u32[]{:S(2)}) async-start(f32[32,1,1280]{2,1,0:T(1,128)} %get-tuple-element.46), calls=%async_computation.3 | async-start | bytes 327680 | tf_op jit(solution)/shard_map/all_to_all | solution.py:32
